TPU v7x, 32 devices: a whole 2x2x4 slice. The times are simulated.
32 devices in a mesh: mesh: 8 (over z, x), sub: 4 (over y, core).
Axes of the slice: x: 2, y: 2, z: 4, core: 2. Of those that a mesh axis runs over, the one named last changes fastest.
Arguments:
- coords: float32 [3, 65536], P(None, ('mesh', 'sub')), may hold values from -6 to 6
- veloc: float32 [3, 65536], P(None, ('mesh', 'sub')), may hold values from -6 to 6
- node_mass: float32 [65536], P(('mesh', 'sub')), may hold values from 0.5 to 2
- stress: float32 [3, 131072], P(None, ('mesh', 'sub')), may hold values from -4 to 4
- connect: int32 [4, 131072], P(None, ('mesh', 'sub')), may hold values from 0 to 3071
- send_mesh: int32 [16384], P(('mesh', 'sub')), may hold values from 0 to 2047
- send_sub: int32 [16384], P(('mesh', 'sub')), may hold values from 0 to 2047
- send_pick: int32 [4, 512], P(None, ('mesh', 'sub')), may hold values from 0 to 31
- bucket_list: int32 [4, 4, 512], P(None, None, ('mesh', 'sub')), may hold values from 0 to 15
- pair_mask: int32 [4, 4, 65536], P(None, None, ('mesh', 'sub')), may hold values 0 or 1
Outputs:
- veloc_out: float32 [3, 65536], P(None, ('mesh', 'sub'))
- stress_out: float32 [3, 131072], P(None, ('mesh', 'sub'))
Inputs may be any that keep to these rules, and one draw needn't show every extreme that they name: `connect`: columns below 2048 are own nodes, then 512 mesh ghosts, then 512 sub ghosts. `send_pick`: a block may be sent to several receivers and several places.
All inputs are finite; a program needn't handle non-finite values. No bound on the sum of `pair_mask` on one device may be relied on, other than what follows from the above.
Results may differ from a plain program's by a relative error of at most 0.0003.
Values sent between devices are 32-bit elements; how exact they have to be, the bound alone decides.
No kernel may reach another device: no remote copies, remote signals or barrier semaphores. Data moves between devices by JAX's collectives and lax.ppermute only.
A program may use at most 64 MiB of HBM per device.

v0:
```python
import functools
import math

import jax
import jax.numpy as jnp
from jax import lax
from jax.experimental import pallas as pl
from jax.experimental.pallas import tpu as pltpu
from jax.sharding import PartitionSpec as P


SEG = 128
STEPS = 4
LOW = 256
ROWS = 8
UNROLL = 16

TIME_STEP = 0.2
YOUNG = 1.0
POISSON = 0.3
HOURGLASS = 0.01
PENALTY = 0.2
REACH = 4.0
HOUR_SIGNS = (1.0, -1.0, 1.0, -1.0)

F32 = jnp.float32
BF16 = jnp.bfloat16


def shifted(value, axis, steps):
    count = lax.axis_size(axis)
    pairs = [(source, (source + steps) % count) for source in range(count)]
    return lax.ppermute(value, axis, pairs)


def split_two(value):
    high = value.astype(BF16).astype(F32)
    return high, value - high


def split_three(value):
    high = value.astype(BF16).astype(F32)
    rest = value - high
    mid = rest.astype(BF16).astype(F32)
    return high, mid, rest - mid


def one_hot_low(low_ids):
    width = low_ids.shape[1]
    rows = lax.broadcasted_iota(jnp.int32, (LOW, width), 0)
    return jnp.where(rows == low_ids, 1.0, 0.0).astype(BF16)


def stack_columns(rows_eight):
    count = rows_eight.shape[1] // LOW
    return jnp.concatenate(
        [rows_eight[:, part * LOW : (part + 1) * LOW] for part in range(count)], axis=0
    )


def pick_high(product, high_ids, count):
    width = product.shape[1]
    total = jnp.zeros((ROWS, width), F32)
    for part in range(count):
        total = jnp.where(high_ids == part, product[part * ROWS : (part + 1) * ROWS], total)
    return total


def split_rows(three):
    high, low = split_two(three)
    pad = jnp.zeros((ROWS - 6, three.shape[1]), F32)
    return jnp.concatenate([high, low, pad], axis=0)


def gather_tiles(table, conn_ref, out_ref):
    count = table.shape[0] // ROWS

    def tile(index, carry):
        ids = conn_ref[pl.ds(index, 1), :]
        product = jnp.dot(table, one_hot_low(ids & (LOW - 1)), preferred_element_type=F32)
        total = pick_high(product, ids >> 8, count)
        for half in range(LOW // SEG):
            start = pl.multiple_of((index * (LOW // SEG) + half) * ROWS, ROWS)
            out_ref[pl.ds(start, ROWS), :] = total[:, half * SEG : (half + 1) * SEG]
        return carry

    lax.fori_loop(0, conn_ref.shape[0], tile, 0, unroll=UNROLL)


def cross(left, right):
    return (
        left[1] * right[2] - left[2] * right[1],
        left[2] * right[0] - left[0] * right[2],
        left[0] * right[1] - left[1] * right[0],
    )


def sub3(left, right):
    return tuple(a - b for a, b in zip(left, right))


def dot3(left, right):
    return left[0] * right[0] + left[1] * right[1] + left[2] * right[2]


def geometry(corner):
    raw = cross(sub3(corner[2], corner[0]), sub3(corner[3], corner[1]))
    twice_area = jnp.maximum(jnp.sqrt(dot3(raw, raw)), 1.0)
    inverse = 1.0 / twice_area
    normal = tuple(part * inverse for part in raw)
    centre = tuple(
        0.25 * (corner[0][c] + corner[1][c] + corner[2][c] + corner[3][c]) for c in range(3)
    )
    return centre, normal, twice_area, inverse


def corner_rows(ref, group, component):
    return [
        ref[pl.ds((group * 32 + corner) * ROWS + component, 8, stride=4 * ROWS), :]
        for corner in range(4)
    ]


def tree_pick(values, bits):
    level = 0
    while len(values) > 1:
        values = [
            jnp.where(bits[level], values[i + 1], values[i]) if i + 1 < len(values) else values[i]
            for i in range(0, len(values), 2)
        ]
        level += 1
    return values[0]


def fill_chunks(three, chunk_ref, first):
    four = jnp.concatenate([three, jnp.zeros((1, three.shape[1]), F32)], axis=0)
    twice = jnp.concatenate([four, four], axis=0)
    for part in range(three.shape[1] // SEG):
        chunk_ref[first + part] = twice[:, part * SEG : (part + 1) * SEG]


def lane_ids(conn_ref, index):
    ids = conn_ref[pl.ds(index, 1), :]
    halves = [jnp.broadcast_to(ids[:, h * SEG : (h + 1) * SEG], (4, SEG)) for h in range(2)]
    return jnp.concatenate(halves, axis=0)


def lane_pick(chunk_ref, ids, high_ids):
    count = chunk_ref.shape[0]
    low_ids = ids & (SEG - 1)
    bits = [((high_ids >> bit) & 1) == 1 for bit in range((count - 1).bit_length())]
    values = [
        jnp.take_along_axis(chunk_ref[part], low_ids, axis=1, mode="promise_in_bounds")
        for part in range(count)
    ]
    return tree_pick(values, bits)


def own_rows_kernel(own_ref, conn_ref, rows_ref, chunk_ref):
    fill_chunks(own_ref[0:3, :], chunk_ref, 0)

    def tile(index, carry):
        ids = lane_ids(conn_ref, index)
        start = pl.multiple_of(index * ROWS, ROWS)
        rows_ref[pl.ds(start, ROWS), :] = lane_pick(chunk_ref, ids, ids >> 7)
        return carry

    lax.fori_loop(0, conn_ref.shape[0], tile, 0, unroll=8)


def geometry_kernel(
    step, nodes, picks_any, mesh_ref, sub_ref, conn_ref, own_rows_ref, corner_ref, geo_ref,
    out_ref, kept_ref, rows_ref, chunk_ref, picks_ref, sem,
):
    fetch = pltpu.make_async_copy(picks_any, picks_ref, sem)
    fetch.start()
    blocks = geo_ref.shape[0] // ROWS
    first = mesh_ref.shape[1] // SEG
    fill_chunks(mesh_ref[0:3, :], chunk_ref, 0)
    fill_chunks(sub_ref[0:3, :], chunk_ref, first)

    def tile(index, carry):
        ids = lane_ids(conn_ref, index)
        start = pl.multiple_of(index * ROWS, ROWS)
        far = lane_pick(chunk_ref, ids, (ids >> 7) - nodes // SEG)
        near = own_rows_ref[pl.ds(start, ROWS), :]
        rows_ref[pl.ds(start, ROWS), :] = jnp.where(ids >= nodes, far, near)
        return carry

    lax.fori_loop(0, conn_ref.shape[0], tile, 0, unroll=16)
    for group in range(blocks // 8):
        corner = [
            tuple(rows_ref[pl.ds(group * 128 + i * 4 + c, 8, stride=16), :] for c in range(3))
            for i in range(4)
        ]
        for i in range(4):
            for c in range(3):
                corner_ref[i * 3 + c, group * 8 : (group + 1) * 8, :] = corner[i][c]
        centre, normal, _, _ = geometry(corner)
        for c in range(3):
            geo_ref[pl.ds(group * 8 * ROWS + c, 8, stride=ROWS), :] = centre[c]
            geo_ref[pl.ds(group * 8 * ROWS + 3 + c, 8, stride=ROWS), :] = normal[c]
        for c in range(6, ROWS):
            geo_ref[pl.ds(group * 8 * ROWS + c, 8, stride=ROWS), :] = jnp.zeros((8, SEG), F32)

    def copy(slot, carry):
        start = pl.multiple_of(picks_ref[step, slot] * ROWS, ROWS)
        here = pl.ds(pl.multiple_of(slot * ROWS, ROWS), ROWS)
        block = geo_ref[pl.ds(start, ROWS), :]
        out_ref[here, :] = block
        kept_ref[here, :] = block
        return carry

    fetch.wait()
    lax.fori_loop(0, out_ref.shape[0] // ROWS, copy, 0, unroll=16)


def force_kernel(
    own_ref, mesh_ref, sub_ref, conn_ref, corner_ref, stress_ref, push_ref, new_ref, rows_ref
):
    blocks = corner_ref.shape[1]
    full = jnp.concatenate([own_ref[3:6, :], mesh_ref[3:6, :], sub_ref[3:6, :]], axis=1)
    gather_tiles(stack_columns(split_rows(full)).astype(BF16), conn_ref, rows_ref)
    stiff = YOUNG / (1.0 - POISSON * POISSON)
    for group in range(blocks // 8):
        here = slice(group * 8, (group + 1) * 8)
        speed_parts = []
        for component in range(3):
            high = corner_rows(rows_ref, group, component)
            low = corner_rows(rows_ref, group, component + 3)
            speed_parts.append([a + b for a, b in zip(high, low)])
        speed = [tuple(speed_parts[c][i] for c in range(3)) for i in range(4)]
        corner = [tuple(corner_ref[i * 3 + c, here, :] for c in range(3)) for i in range(4)]
        centre, normal, twice_area, inverse = geometry(corner)
        side = sub3(corner[1], corner[0])
        side_inverse = 1.0 / jnp.maximum(jnp.sqrt(dot3(side, side)), 1.0)
        axis_one = tuple(part * side_inverse for part in side)
        axis_two = cross(normal, axis_one)
        relative = [sub3(corner[i], centre) for i in range(4)]
        x = [dot3(relative[i], axis_one) for i in range(4)]
        y = [dot3(relative[i], axis_two) for i in range(4)]
        u = [dot3(speed[i], axis_one) for i in range(4)]
        v = [dot3(speed[i], axis_two) for i in range(4)]
        y13, y20 = (y[1] - y[3]) * inverse, (y[2] - y[0]) * inverse
        x31, x02 = (x[3] - x[1]) * inverse, (x[0] - x[2]) * inverse
        bx = [y13, y20, -y13, -y20]
        by = [x31, x02, -x31, -x02]
        u02, u13, v02, v13 = u[0] - u[2], u[1] - u[3], v[0] - v[2], v[1] - v[3]
        rate_xx = y13 * u02 + y20 * u13
        rate_yy = x31 * v02 + x02 * v13
        rate_xy = x31 * u02 + x02 * u13 + y13 * v02 + y20 * v13
        s0 = stress_ref[0, here, :] + TIME_STEP * (stiff * (rate_xx + POISSON * rate_yy))
        s1 = stress_ref[1, here, :] + TIME_STEP * (stiff * (POISSON * rate_xx + rate_yy))
        s2 = stress_ref[2, here, :] + TIME_STEP * (YOUNG / (2.0 * (1.0 + POISSON)) * rate_xy)
        new_ref[0, here, :] = s0
        new_ref[1, here, :] = s1
        new_ref[2, here, :] = s2
        half_area = 0.5 * twice_area
        hour_x = x[0] - x[1] + x[2] - x[3]
        hour_y = y[0] - y[1] + y[2] - y[3]
        shape = [HOUR_SIGNS[i] - hour_x * bx[i] - hour_y * by[i] for i in range(4)]
        rate = tuple(
            HOURGLASS * sum(shape[i] * speed[i][c] for i in range(4)) for c in range(3)
        )
        for i in range(4):
            force_x = half_area * (bx[i] * s0 + by[i] * s2)
            force_y = half_area * (by[i] * s1 + bx[i] * s2)
            start = (group * 32 + i) * ROWS
            for c in range(3):
                internal = force_x * axis_one[c] + force_y * axis_two[c] + shape[i] * rate[c]
                high, low = split_two(-internal)
                push_ref[pl.ds(start + c, 8, stride=4 * ROWS), :] = high
                push_ref[pl.ds(start + 3 + c, 8, stride=4 * ROWS), :] = low
            for c in range(6, ROWS):
                push_ref[pl.ds(start + c, 8, stride=4 * ROWS), :] = jnp.zeros((8, SEG), F32)


def product_tiles(value, turn):
    parts = split_three(value)
    order = (0, 0, 1, 0, 1, 2) if turn else (0, 1, 0, 2, 1, 0)
    return [parts[index] for index in order]


def row_mix(three, extras):
    width = three.shape[1]
    rows = [three] + extras
    pad = ROWS - sum(part.shape[0] for part in rows)
    if pad:
        rows.append(jnp.zeros((pad, width), F32))
    return jnp.concatenate(rows, axis=0)


def node_features(place):
    ones = jnp.ones((3, place.shape[1]), F32)
    square = jnp.concatenate(
        split_three(place[0:1] ** 2 + place[1:2] ** 2 + place[2:3] ** 2), axis=0
    )
    tiles = product_tiles(place, True)
    gap = [row_mix(tiles[0], [ones])] + [row_mix(tile, []) for tile in tiles[1:]]
    far = [row_mix(tiles[0], [ones]), row_mix(tiles[1], [square])]
    far += [row_mix(tile, []) for tile in tiles[2:]]
    return gap, far


def segment_features(centre, normal):
    ones = jnp.ones((3, centre.shape[1]), F32)
    lean = centre[0:1] * normal[0:1] + centre[1:2] * normal[1:2] + centre[2:3] * normal[2:3]
    lean = jnp.concatenate(split_three(-lean), axis=0)
    square = centre[0:1] ** 2 + centre[1:2] ** 2 + centre[2:3] ** 2
    square = jnp.concatenate(split_three(square), axis=0)
    tiles = product_tiles(normal, False)
    gap = [row_mix(tiles[0], [lean])] + [row_mix(tile, []) for tile in tiles[1:]]
    tiles = product_tiles(-2.0 * centre, False)
    far = [row_mix(tiles[0], [square]), row_mix(tiles[1], [ones])]
    far += [row_mix(tile, []) for tile in tiles[2:]]
    return gap, far


FEATURES = 12 * ROWS
SCALE = math.sqrt(math.log2(math.e) / REACH)


def feature_kernel(step, own_ref, mask_ref, node_ref):
    cands = mask_ref.shape[1]

    def features(index, carry):
        start = pl.multiple_of(index * SEG, SEG)
        gap, far = node_features(own_ref[0:3, pl.ds(start, SEG)] * SCALE)
        mask = mask_ref[step, :, pl.ds(start, SEG)].astype(F32)
        for k in range(cands):
            live = mask[k : k + 1]
            rows = jnp.concatenate([tile * live for tile in gap] + far, axis=0)
            rows = jnp.concatenate([rows, jnp.zeros((SEG - FEATURES, SEG), F32)], axis=0)
            node_ref[k, pl.ds(start, SEG), :] = rows.T.astype(BF16)
        return carry

    lax.fori_loop(0, own_ref.shape[1] // SEG, features, 0, unroll=2)


def contact_kernel(
    step, list_any, node_ref, slots_ref, force_ref, react_ref, seg_ref, push_ref, list_ref, sem
):
    fetch = pltpu.make_async_copy(list_any, list_ref, sem)
    fetch.start()
    buckets = node_ref.shape[1] // SEG
    cands = node_ref.shape[0]
    slots = react_ref.shape[0]
    react_ref[...] = jnp.zeros_like(react_ref)

    def segments(index, carry):
        tile = slots_ref[pl.ds(pl.multiple_of(index * ROWS, ROWS), ROWS), :]
        gap, far = segment_features(tile[0:3] * SCALE, tile[3:6])
        blank = jnp.zeros((6 * ROWS, SEG), F32)
        left = jnp.concatenate(gap + [blank], axis=0)
        right = jnp.concatenate([blank] + far, axis=0)
        rows = jnp.concatenate([left, right], axis=1)
        seg_ref[index] = rows.astype(BF16)
        push = split_rows(tile[3:6])
        push = jnp.concatenate([push, push], axis=1)
        push_ref[index] = jnp.concatenate([push, jnp.zeros_like(push)], axis=0).astype(BF16)
        return carry

    lax.fori_loop(0, slots, segments, 0, unroll=4)
    fetch.wait()

    def bucket(index, carry):
        start = pl.multiple_of(index * SEG, SEG)
        total = jnp.zeros((2 * ROWS, SEG), F32)
        for k in range(cands):
            slot = list_ref[step, k, index]
            pair = jnp.dot(
                node_ref[k, pl.ds(start, SEG), :][:, :FEATURES],
                seg_ref[slot],
                preferred_element_type=F32,
            )
            gap, far = pair[:, :SEG], pair[:, SEG:]
            weight = jnp.minimum(gap, 0.0) * jnp.exp2(gap * gap - far)
            react_ref[pl.ds(slot, 1), :] += jnp.sum(weight, axis=0, keepdims=True)
            high = weight.astype(BF16)
            low = (weight - high.astype(F32)).astype(BF16)
            total = total + lax.dot_general(
                push_ref[slot],
                jnp.concatenate([high, low], axis=1),
                (((1,), (1,)), ((), ())),
                preferred_element_type=F32,
            )
        force = (total[0:3] + total[3:6]) * (-PENALTY / SCALE)
        force_ref[:, pl.ds(start, SEG)] = row_mix(force, [])
        return carry

    lax.fori_loop(0, buckets, bucket, 0, unroll=4)
    react_ref[...] = react_ref[...] * (-PENALTY / SCALE)


def internal_kernel(rows_ref, conn_ref, acc_ref):
    scatter_tiles(rows_ref, conn_ref, acc_ref)


def pick_kernel(picks_ref, conn_ref, tiles_ref):
    for step in range(tiles_ref.shape[0]):

        def copy(slot, carry):
            for half in range(2):
                row = conn_ref[pl.ds(picks_ref[step, slot] * 2 + half, 1), :]
                tiles_ref[step, pl.ds(slot * 2 + half, 1), :] = row
            return carry

        lax.fori_loop(0, tiles_ref.shape[1] // 2, copy, 0, unroll=8)


def collect_kernel(step, picks_ref, back_ref, seg_ref):
    seg_ref[...] = jnp.zeros_like(seg_ref)

    def collect(slot, carry):
        seg_ref[pl.ds(picks_ref[step, slot], 1), :] += back_ref[pl.ds(slot, 1), :]
        return carry

    lax.fori_loop(0, back_ref.shape[0], collect, 0)


def react_tiles(step, first, last, blocks_ref, back_ref, tiles_ref):
    def tile(index, total):
        react = back_ref[pl.ds(index, 1), :]
        normal = blocks_ref[pl.ds(pl.multiple_of(index * ROWS, ROWS), ROWS), :][3:6]
        rows = split_rows(-0.25 * react * normal)
        values = jnp.concatenate([rows, rows], axis=1)
        for half in range(2):
            ids = tiles_ref[step, pl.ds(index * 2 + half, 1), :]
            high_ids = ids >> 8
            spread = jnp.concatenate(
                [jnp.where(high_ids == part, values, 0.0) for part in range(first, last)], axis=0
            ).astype(BF16)
            total = total + lax.dot_general(
                spread,
                one_hot_low(ids & (LOW - 1)),
                (((1,), (1,)), ((), ())),
                preferred_element_type=F32,
            )
        return total

    start = jnp.zeros(((last - first) * ROWS, LOW), F32)
    return lax.fori_loop(0, back_ref.shape[0], tile, start, unroll=8)


def unstack(total):
    count = total.shape[0] // ROWS
    full = jnp.concatenate(
        [total[part * ROWS : (part + 1) * ROWS] for part in range(count)], axis=1
    )
    return row_mix(full[0:3] + full[3:6], [])


def react_ghost_kernel(step, blocks_ref, back_ref, tiles_ref, acc_ref, mesh_ref, sub_ref):
    last = acc_ref.shape[0] // ROWS
    first = last - (mesh_ref.shape[1] + sub_ref.shape[1]) // LOW
    total = react_tiles(step, first, last, blocks_ref, back_ref, tiles_ref)
    full = unstack(total + acc_ref[first * ROWS :, :])
    mesh_ref[...] = full[:, : mesh_ref.shape[1]]
    sub_ref[...] = full[:, mesh_ref.shape[1] :]


def react_own_kernel(step, blocks_ref, back_ref, tiles_ref, acc_ref, own_ref):
    last = own_ref.shape[1] // LOW
    total = react_tiles(step, 0, last, blocks_ref, back_ref, tiles_ref)
    own_ref[...] = unstack(total + acc_ref[: last * ROWS, :])


def scatter_tiles(rows_ref, conn_ref, acc_ref):
    count = acc_ref.shape[0] // ROWS
    acc_ref[...] = jnp.zeros_like(acc_ref)

    def tile(index, carry):
        ids = conn_ref[pl.ds(index, 1), :]
        start = pl.multiple_of(index * (LOW // SEG) * ROWS, ROWS * (LOW // SEG))
        parts = [rows_ref[pl.ds(start + half * ROWS, ROWS), :] for half in range(LOW // SEG)]
        values = jnp.concatenate(parts, axis=1)
        high_ids = ids >> 8
        spread = jnp.concatenate(
            [jnp.where(high_ids == part, values, 0.0) for part in range(count)], axis=0
        ).astype(BF16)
        acc_ref[...] += lax.dot_general(
            spread,
            one_hot_low(ids & (LOW - 1)),
            (((1,), (1,)), ((), ())),
            preferred_element_type=F32,
        )
        return carry

    lax.fori_loop(0, conn_ref.shape[0], tile, 0, unroll=UNROLL)


def add_back(back, ids_ref, count):
    total = jnp.zeros((count * ROWS, LOW), F32)
    high, low = split_two(back[0:3])
    pad = jnp.zeros((ROWS - 6, back.shape[1]), F32)
    rows = jnp.concatenate([high, low, pad], axis=0)
    for index in range(ids_ref.shape[0]):
        ids = ids_ref[index : index + 1, :]
        values = rows[:, index * LOW : (index + 1) * LOW]
        spread = jnp.concatenate(
            [jnp.where((ids >> 8) == part, values, 0.0) for part in range(count)], axis=0
        ).astype(BF16)
        total = total + lax.dot_general(
            spread,
            one_hot_low(ids & (LOW - 1)),
            (((1,), (1,)), ((), ())),
            preferred_element_type=F32,
        )
    return total


def pack_ghosts(own, ids_ref, out_ref):
    count = own.shape[1] // LOW
    tables = [stack_columns(part).astype(BF16) for part in split_three(own)]
    for index in range(ids_ref.shape[0]):
        ids = ids_ref[index : index + 1, :]
        hot = one_hot_low(ids & (LOW - 1))
        product = sum(jnp.dot(table, hot, preferred_element_type=F32) for table in tables)
        out_ref[:, index * LOW : (index + 1) * LOW] = pick_high(product, ids >> 8, count)


def pack_kernel(own_ref, mesh_ids_ref, sub_ids_ref, to_mesh_ref, to_sub_ref):
    own = own_ref[...]
    pack_ghosts(own, mesh_ids_ref, to_mesh_ref)
    pack_ghosts(own, sub_ids_ref, to_sub_ref)


def update_kernel(
    own_ref, force_ref, slave_ref, back_mesh_ref, back_sub_ref, mass_ref, mesh_ids_ref,
    sub_ids_ref, new_ref, to_mesh_ref, to_sub_ref,
):
    count = own_ref.shape[1] // LOW
    extra = add_back(back_mesh_ref[...], mesh_ids_ref, count) + add_back(
        back_sub_ref[...], sub_ids_ref, count
    )
    full = jnp.concatenate(
        [extra[part * ROWS : (part + 1) * ROWS] for part in range(count)], axis=1
    )
    force = force_ref[0:3, :] + slave_ref[0:3, :] + (full[0:3] + full[3:6])
    speed = own_ref[3:6, :] + TIME_STEP * force / mass_ref[...]
    place = own_ref[0:3, :] + TIME_STEP * speed
    own = jnp.concatenate([place, speed, jnp.zeros((ROWS - 6, place.shape[1]), F32)], axis=0)
    new_ref[...] = own
    if to_mesh_ref is not None:
        pack_ghosts(own, mesh_ids_ref, to_mesh_ref)
        pack_ghosts(own, sub_ids_ref, to_sub_ref)


def last_kernel(*refs):
    update_kernel(*refs, None, None)


VM = pl.BlockSpec(memory_space=pltpu.VMEM)
SM = pl.BlockSpec(memory_space=pltpu.SMEM)
ANY = pl.BlockSpec(memory_space=pl.ANY)


def call(kernel, outs, ins, scratch=(), flops=0):
    shapes = tuple(
        jax.ShapeDtypeStruct(shape, F32) if isinstance(shape, tuple) else shape for shape in outs
    )
    return pl.pallas_call(
        kernel,
        out_shape=shapes,
        in_specs=list(ins),
        out_specs=tuple(VM for _ in outs),
        scratch_shapes=[
            pltpu.VMEM(shape, F32) if isinstance(shape, tuple) else shape for shape in scratch
        ],
        compiler_params=pltpu.CompilerParams(vmem_limit_bytes=20 << 20),
        cost_estimate=pl.CostEstimate(flops=flops, bytes_accessed=1 << 20, transcendentals=0),
    )


def per_device(
    coords,
    veloc,
    node_mass,
    stress,
    connect,
    send_mesh,
    send_sub,
    send_pick,
    bucket_list,
    pair_mask,
):
    nodes = coords.shape[1]
    elems = stress.shape[1]
    ghost_mesh = send_mesh.shape[0]
    ghost_sub = send_sub.shape[0]
    width = nodes + ghost_mesh + ghost_sub
    peers = lax.axis_size("mesh")
    slots = send_pick.shape[1]
    per_peer = slots // peers
    blocks = elems // SEG
    conn = connect.reshape(4, blocks, SEG).transpose(1, 0, 2).reshape(4 * elems // LOW, LOW)
    mesh_ids = send_mesh.reshape(ghost_mesh // LOW, LOW)
    sub_ids = send_sub.reshape(ghost_sub // LOW, LOW)
    mass = node_mass.reshape(1, nodes)
    stress_now = stress.reshape(3, blocks, SEG)
    own = jnp.concatenate([coords, veloc, jnp.zeros((ROWS - 6, nodes), F32)], axis=0)

    chunks = nodes // SEG
    ghost_chunks = (ghost_mesh + ghost_sub) // SEG
    cands = bucket_list.shape[1]

    pack = call(pack_kernel, [(ROWS, ghost_mesh), (ROWS, ghost_sub)], [VM] * 3)
    own_rows_of = call(
        own_rows_kernel, [(2 * blocks * ROWS, SEG)], [VM] * 2, [(chunks, ROWS, SEG)], flops=1 << 31
    )
    geom = lambda step: call(
        functools.partial(geometry_kernel, step, nodes),
        [(12, blocks, SEG), (blocks * ROWS, SEG)] + [(slots * ROWS, SEG)] * 2,
        [ANY] + [VM] * 4,
        [
            (2 * blocks * ROWS, SEG),
            (ghost_chunks, ROWS, SEG),
            pltpu.SMEM(send_pick.shape, jnp.int32),
            pltpu.SemaphoreType.DMA,
        ],
        flops=1 << 30,
    )
    forces = call(
        force_kernel,
        [(4 * blocks * ROWS, SEG), (3, blocks, SEG)],
        [VM] * 6,
        [(4 * blocks * ROWS, SEG)],
        flops=1 << 31,
    )
    features = lambda step: call(
        functools.partial(feature_kernel, step),
        [jax.ShapeDtypeStruct((cands, nodes, SEG), BF16)],
        [VM] * 2,
        flops=1 << 30,
    )
    contact = lambda step: call(
        functools.partial(contact_kernel, step),
        [(ROWS, nodes), (slots, SEG)],
        [ANY] + [VM] * 2,
        [
            pltpu.VMEM((slots, FEATURES, 2 * SEG), BF16),
            pltpu.VMEM((slots, 2 * ROWS, 2 * SEG), BF16),
            pltpu.SMEM(bucket_list.shape, jnp.int32),
            pltpu.SemaphoreType.DMA,
        ],
        flops=1 << 31,
    )
    internal_of = call(internal_kernel, [(width // LOW * ROWS, LOW)], [VM] * 2, flops=1 << 31)
    react_ghost = lambda step: call(
        functools.partial(react_ghost_kernel, step),
        [(ROWS, ghost_mesh), (ROWS, ghost_sub)],
        [VM] * 4,
        flops=1 << 29,
    )
    react_own = lambda step: call(
        functools.partial(react_own_kernel, step), [(ROWS, nodes)], [VM] * 4, flops=1 << 30
    )
    update = call(update_kernel, [(ROWS, nodes), (ROWS, ghost_mesh), (ROWS, ghost_sub)], [VM] * 8)
    finish = call(last_kernel, [(ROWS, nodes)], [VM] * 8)

    by_slot = slots <= blocks
    pick_tiles = call(
        pick_kernel,
        [jax.ShapeDtypeStruct((STEPS, slots * 2, LOW), jnp.int32)],
        [SM, VM],
        flops=1 << 20,
    )
    collect = lambda step: call(functools.partial(collect_kernel, step), [(blocks, SEG)], [SM, VM])

    to_mesh, to_sub = pack(own, mesh_ids, sub_ids)
    tiles = pick_tiles(send_pick, conn)[0] if by_slot else conn[None]
    for step in range(STEPS):
        from_mesh = shifted(to_mesh, "mesh", 1)
        from_sub = shifted(to_sub, "sub", 1)
        (own_rows,) = own_rows_of(own, conn)
        (node,) = features(step)(own, pair_mask)
        corner, geo, outgoing, kept = geom(step)(
            send_pick, from_mesh, from_sub, conn, own_rows
        )
        incoming = lax.all_to_all(
            outgoing.reshape(peers, per_peer * ROWS, SEG),
            "mesh", split_axis=0, concat_axis=0, tiled=True,
        ).reshape(slots * ROWS, SEG)
        pushes, stress_now = forces(own, from_mesh, from_sub, conn, corner, stress_now)
        slave, react = contact(step)(bucket_list, node, incoming)
        returned = lax.all_to_all(
            react.reshape(peers, per_peer, SEG),
            "mesh", split_axis=0, concat_axis=0, tiled=True,
        ).reshape(slots, SEG)
        (acc,) = internal_of(pushes, conn)
        if by_slot:
            rows = (kept, returned, tiles, acc)
        else:
            rows = (geo, collect(step)(send_pick, returned)[0], tiles, acc)
        at = step if by_slot else 0
        back_mesh, back_sub = react_ghost(at)(*rows)
        (force,) = react_own(at)(*rows)
        back_mesh = shifted(back_mesh, "mesh", -1)
        back_sub = shifted(back_sub, "sub", -1)
        args = (own, force, slave, back_mesh, back_sub, mass, mesh_ids, sub_ids)
        if step < STEPS - 1:
            own, to_mesh, to_sub = update(*args)
        else:
            (own,) = finish(*args)
    return own[3:6], stress_now.reshape(3, elems)


def solution(mesh):
    return jax.shard_map(
        per_device,
        mesh=mesh,
        in_specs=(
            P(None, ("mesh", "sub")),
            P(None, ("mesh", "sub")),
            P(("mesh", "sub")),
            P(None, ("mesh", "sub")),
            P(None, ("mesh", "sub")),
            P(("mesh", "sub")),
            P(("mesh", "sub")),
            P(None, ("mesh", "sub")),
            P(None, None, ("mesh", "sub")),
            P(None, None, ("mesh", "sub")),
        ),
        out_specs=(P(None, ("mesh", "sub")), P(None, ("mesh", "sub"))),
        check_vma=False,
    )
```

profile of v0, /device:TPU:0, one launch (start us, length us, event | category | flops | bytes accessed | tf_op | source)
XLA Modules:
  0.0 162.7 jit_solution(15439211071301817038)
XLA Ops:
  3.4 3.0 %collective-permute-start = (f32[8,512]{1,0:T(8,128)S(1)}, f32[8,512]{1,0:T(8,128)S(1)}, u32[]{:S(2)}, u32[]{:S(2)}) collective-permute-start(f32[8,512]{1,0:T(8,128)S(1)} %get-tuple-element.49), channel_id=1, source_target_pairs={{0,4},{4,8},{8,12},{12,16},{16,20},{20,24},{24,28},{28,0},{1,5},{5... | collective-permute-start | bytes 49160 | tf_op jit(solution)/shard_map/ppermute | solution.py:33
  6.4 0.9 reshape.76.conn_ref
  7.3 1.9 %shard_map.114.own_rows_ref = f32[512,128]{1,0:T(8,128)S(1)} custom-call(f32[8,2048]{1,0:T(8,128)S(1)} %maximum_maximum_fusion.own_ref, s32[64,256]{1,0:T(8,128)S(1)} %reshape.76.conn_ref), custom_call_target="tpu_custom_call" | custom-call | flops 2147483648 | bytes 1048576 | tf_op jit(solution)/shard_map/pallas_call | solution.py:675
  9.2 1.1 shard_map.116.node_ref
  10.4 1.2 shard_map.118.tiles_ref
  11.6 1.8 %shard_map.115 = (f32[12,32,128]{2,1,0:T(8,128)S(1)}, f32[256,128]{1,0:T(8,128)}, f32[128,128]{1,0:T(8,128)}, f32[128,128]{1,0:T(8,128)S(1)}) custom-call(s32[4,16]{1,0:T(4,128)S(1)} %copy-done.1, f32[8,512]{1,0:T(8,128)S(1)} %collective-permute-done.mesh_ref, f32[8,512]{1,0:T(8,128)S(1)} %collective-permute-done.1.sub_ref, s32[64,256]{1,0:T(8,128)S(1)} %reshape.76.conn_ref, ...), custom_call_target="tpu_custom_call" | custom-call | flops 1073741824 | bytes 1048576 | tf_op jit(solution)/shard_map/pallas_call | solution.py:677
  13.4 4.9 %all-to-all-start = ((f32[8,16,128]{2,1,0:T(8,128)}), f32[8,16,128]{2,1,0:T(8,128)S(1)}, u32[]{:S(2)}, u32[]{:S(2)}) async-start(f32[8,16,128]{2,1,0:T(8,128)} %bitcast.2), calls=%async_computation | async-start | bytes 131072 | tf_op jit(solution)/shard_map/all_to_all | solution.py:680
  18.3 3.8 %shard_map.119 = (f32[1024,128]{1,0:T(8,128)S(1)}, f32[3,32,128]{2,1,0:T(8,128)S(1)}) custom-call(f32[8,2048]{1,0:T(8,128)S(1)} %maximum_maximum_fusion.own_ref, f32[8,512]{1,0:T(8,128)S(1)} %collective-permute-done.mesh_ref, f32[8,512]{1,0:T(8,128)S(1)} %collective-permute-done.1.sub_ref, s32[64,256]{1,0:T(8,128)S(1)} %reshape.76.conn_ref, ...), custom_call_target="tpu_custom_call" | custom-call | flops 2147483648 | bytes 1048576 | tf_op jit(solution)/shard_map/pallas_call | solution.py:684
  22.2 3.1 %all-to-all-done = f32[8,16,128]{2,1,0:T(8,128)S(1)} async-done(((f32[8,16,128]{2,1,0:T(8,128)}), f32[8,16,128]{2,1,0:T(8,128)S(1)}, u32[]{:S(2)}, u32[]{:S(2)}) %all-to-all-start) | async-done | bytes 65568 | tf_op jit(solution)/shard_map/all_to_all | solution.py:680
  25.3 4.4 %shard_map.117 = (f32[8,2048]{1,0:T(8,128)S(1)}, f32[16,128]{1,0:T(8,128)}) custom-call(s32[4,4,16]{2,1,0:T(4,128)S(1)} %copy-done.3, bf16[4,2048,128]{2,1,0:T(8,128)(2,1)S(1)} %shard_map.116.node_ref, f32[128,128]{1,0:T(8,128)S(1)} %bitcast.35), custom_call_target="tpu_custom_call" | custom-call | flops 2147483648 | bytes 1048576 | tf_op jit(solution)/shard_map/pallas_call | solution.py:685
  29.6 3.3 %all-to-all-start.1 = ((f32[8,2,128]{2,1,0:T(2,128)}), f32[8,2,128]{2,1,0:T(2,128)S(1)}, u32[]{:S(2)}, u32[]{:S(2)}) async-start(f32[8,2,128]{2,1,0:T(2,128)} %bitcast.4), calls=%async_computation.1 | async-start | bytes 16384 | tf_op jit(solution)/shard_map/all_to_all | solution.py:686
  33.0 3.3 %shard_map.120.acc_ref = f32[96,256]{1,0:T(8,128)S(1)} custom-call(f32[1024,128]{1,0:T(8,128)S(1)} %get-tuple-element.55.rows_ref, s32[64,256]{1,0:T(8,128)S(1)} %reshape.76.conn_ref), custom_call_target="tpu_custom_call" | custom-call | flops 2147483648 | bytes 1048576 | tf_op jit(solution)/shard_map/pallas_call | solution.py:690
  36.3 3.1 %all-to-all-done.1 = f32[8,2,128]{2,1,0:T(2,128)S(1)} async-done(((f32[8,2,128]{2,1,0:T(2,128)}), f32[8,2,128]{2,1,0:T(2,128)S(1)}, u32[]{:S(2)}, u32[]{:S(2)}) %all-to-all-start.1) | async-done | bytes 8224 | tf_op jit(solution)/shard_map/all_to_all | solution.py:686
  39.4 1.5 shard_map.122
  40.9 1.6 collective-permute-start.2
  42.5 1.6 shard_map.121.force_ref
  44.7 0.9 shard_map.123
  45.6 1.5 collective-permute-start.4
  47.1 1.9 %shard_map.124.own_rows_ref = f32[512,128]{1,0:T(8,128)S(1)} custom-call(f32[8,2048]{1,0:T(8,128)S(1)} %get-tuple-element.59.own_ref, s32[64,256]{1,0:T(8,128)S(1)} %reshape.76.conn_ref), custom_call_target="tpu_custom_call" | custom-call | flops 2147483648 | bytes 1048576 | tf_op jit(solution)/shard_map/pallas_call | solution.py:675
  49.0 1.1 shard_map.126.node_ref
  50.2 2.0 %collective-permute-done.4.mesh_ref = f32[8,512]{1,0:T(8,128)S(1)} collective-permute-done((f32[8,512]{1,0:T(8,128)S(1)}, f32[8,512]{1,0:T(8,128)S(1)}, u32[]{:S(2)}, u32[]{:S(2)}) %collective-permute-start.4) | collective-permute-done | bytes 16416 | tf_op jit(solution)/shard_map/ppermute | solution.py:33
  52.1 1.8 %shard_map.125 = (f32[12,32,128]{2,1,0:T(8,128)S(1)}, f32[256,128]{1,0:T(8,128)}, f32[128,128]{1,0:T(8,128)}, f32[128,128]{1,0:T(8,128)S(1)}) custom-call(s32[4,16]{1,0:T(4,128)S(1)} %copy-done.1, f32[8,512]{1,0:T(8,128)S(1)} %collective-permute-done.4.mesh_ref, f32[8,512]{1,0:T(8,128)S(1)} %collective-permute-done.5.sub_ref, ...), custom_call_target="tpu_custom_call" | custom-call | flops 1073741824 | bytes 1048576 | tf_op jit(solution)/shard_map/pallas_call | solution.py:677
  54.0 3.4 %all-to-all-start.2 = ((f32[8,16,128]{2,1,0:T(8,128)}), f32[8,16,128]{2,1,0:T(8,128)S(1)}, u32[]{:S(2)}, u32[]{:S(2)}) async-start(f32[8,16,128]{2,1,0:T(8,128)} %bitcast.7), calls=%async_computation.2 | async-start | bytes 131072 | tf_op jit(solution)/shard_map/all_to_all | solution.py:680
  57.4 3.8 %shard_map.128 = (f32[1024,128]{1,0:T(8,128)S(1)}, f32[3,32,128]{2,1,0:T(8,128)S(1)}) custom-call(f32[8,2048]{1,0:T(8,128)S(1)} %get-tuple-element.59.own_ref, f32[8,512]{1,0:T(8,128)S(1)} %collective-permute-done.4.mesh_ref, f32[8,512]{1,0:T(8,128)S(1)} %collective-permute-done.5.sub_ref, s32[64,256]{1,0:T(8,128)S(1)} %reshape.76.conn_ref, ...), custom_call_target="tpu_custom_call" | custom-call | flops 2147483648 | bytes 1048576 | tf_op jit(solution)/shard_map/pallas_call | solution.py:684
  61.2 3.2 %all-to-all-done.2 = f32[8,16,128]{2,1,0:T(8,128)S(1)} async-done(((f32[8,16,128]{2,1,0:T(8,128)}), f32[8,16,128]{2,1,0:T(8,128)S(1)}, u32[]{:S(2)}, u32[]{:S(2)}) %all-to-all-start.2) | async-done | bytes 65568 | tf_op jit(solution)/shard_map/all_to_all | solution.py:680
  64.4 4.4 %shard_map.127 = (f32[8,2048]{1,0:T(8,128)S(1)}, f32[16,128]{1,0:T(8,128)}) custom-call(s32[4,4,16]{2,1,0:T(4,128)S(1)} %copy-done.3, bf16[4,2048,128]{2,1,0:T(8,128)(2,1)S(1)} %shard_map.126.node_ref, f32[128,128]{1,0:T(8,128)S(1)} %bitcast.32), custom_call_target="tpu_custom_call" | custom-call | flops 2147483648 | bytes 1048576 | tf_op jit(solution)/shard_map/pallas_call | solution.py:685
  68.8 3.3 %all-to-all-start.3 = ((f32[8,2,128]{2,1,0:T(2,128)}), f32[8,2,128]{2,1,0:T(2,128)S(1)}, u32[]{:S(2)}, u32[]{:S(2)}) async-start(f32[8,2,128]{2,1,0:T(2,128)} %bitcast.9), calls=%async_computation.3 | async-start | bytes 16384 | tf_op jit(solution)/shard_map/all_to_all | solution.py:686
  72.1 3.3 %shard_map.129.acc_ref = f32[96,256]{1,0:T(8,128)S(1)} custom-call(f32[1024,128]{1,0:T(8,128)S(1)} %get-tuple-element.67.rows_ref, s32[64,256]{1,0:T(8,128)S(1)} %reshape.76.conn_ref), custom_call_target="tpu_custom_call" | custom-call | flops 2147483648 | bytes 1048576 | tf_op jit(solution)/shard_map/pallas_call | solution.py:690
  75.5 3.1 %all-to-all-done.3 = f32[8,2,128]{2,1,0:T(2,128)S(1)} async-done(((f32[8,2,128]{2,1,0:T(2,128)}), f32[8,2,128]{2,1,0:T(2,128)S(1)}, u32[]{:S(2)}, u32[]{:S(2)}) %all-to-all-start.3) | async-done | bytes 8224 | tf_op jit(solution)/shard_map/all_to_all | solution.py:686
  78.6 1.5 shard_map.131
  80.1 1.6 collective-permute-start.6
  81.7 1.6 shard_map.130.force_ref
  83.9 0.9 shard_map.132
  84.8 1.5 collective-permute-start.8
  86.3 1.9 %shard_map.133.own_rows_ref = f32[512,128]{1,0:T(8,128)S(1)} custom-call(f32[8,2048]{1,0:T(8,128)S(1)} %get-tuple-element.71.own_ref, s32[64,256]{1,0:T(8,128)S(1)} %reshape.76.conn_ref), custom_call_target="tpu_custom_call" | custom-call | flops 2147483648 | bytes 1048576 | tf_op jit(solution)/shard_map/pallas_call | solution.py:675
  88.1 1.1 shard_map.135.node_ref
  89.3 2.0 %collective-permute-done.8.mesh_ref = f32[8,512]{1,0:T(8,128)S(1)} collective-permute-done((f32[8,512]{1,0:T(8,128)S(1)}, f32[8,512]{1,0:T(8,128)S(1)}, u32[]{:S(2)}, u32[]{:S(2)}) %collective-permute-start.8) | collective-permute-done | bytes 16416 | tf_op jit(solution)/shard_map/ppermute | solution.py:33
  91.3 1.8 %shard_map.134 = (f32[12,32,128]{2,1,0:T(8,128)S(1)}, f32[256,128]{1,0:T(8,128)}, f32[128,128]{1,0:T(8,128)}, f32[128,128]{1,0:T(8,128)S(1)}) custom-call(s32[4,16]{1,0:T(4,128)S(1)} %copy-done.1, f32[8,512]{1,0:T(8,128)S(1)} %collective-permute-done.8.mesh_ref, f32[8,512]{1,0:T(8,128)S(1)} %collective-permute-done.9.sub_ref, ...), custom_call_target="tpu_custom_call" | custom-call | flops 1073741824 | bytes 1048576 | tf_op jit(solution)/shard_map/pallas_call | solution.py:677
  93.1 3.4 %all-to-all-start.4 = ((f32[8,16,128]{2,1,0:T(8,128)}), f32[8,16,128]{2,1,0:T(8,128)S(1)}, u32[]{:S(2)}, u32[]{:S(2)}) async-start(f32[8,16,128]{2,1,0:T(8,128)} %bitcast.11), calls=%async_computation.4 | async-start | bytes 131072 | tf_op jit(solution)/shard_map/all_to_all | solution.py:680
  96.5 3.8 %shard_map.137 = (f32[1024,128]{1,0:T(8,128)S(1)}, f32[3,32,128]{2,1,0:T(8,128)S(1)}) custom-call(f32[8,2048]{1,0:T(8,128)S(1)} %get-tuple-element.71.own_ref, f32[8,512]{1,0:T(8,128)S(1)} %collective-permute-done.8.mesh_ref, f32[8,512]{1,0:T(8,128)S(1)} %collective-permute-done.9.sub_ref, s32[64,256]{1,0:T(8,128)S(1)} %reshape.76.conn_ref, ...), custom_call_target="tpu_custom_call" | custom-call | flops 2147483648 | bytes 1048576 | tf_op jit(solution)/shard_map/pallas_call | solution.py:684
  100.3 3.0 %all-to-all-done.4 = f32[8,16,128]{2,1,0:T(8,128)S(1)} async-done(((f32[8,16,128]{2,1,0:T(8,128)}), f32[8,16,128]{2,1,0:T(8,128)S(1)}, u32[]{:S(2)}, u32[]{:S(2)}) %all-to-all-start.4) | async-done | bytes 65568 | tf_op jit(solution)/shard_map/all_to_all | solution.py:680
  103.3 4.4 %shard_map.136 = (f32[8,2048]{1,0:T(8,128)S(1)}, f32[16,128]{1,0:T(8,128)}) custom-call(s32[4,4,16]{2,1,0:T(4,128)S(1)} %copy-done.3, bf16[4,2048,128]{2,1,0:T(8,128)(2,1)S(1)} %shard_map.135.node_ref, f32[128,128]{1,0:T(8,128)S(1)} %bitcast.33), custom_call_target="tpu_custom_call" | custom-call | flops 2147483648 | bytes 1048576 | tf_op jit(solution)/shard_map/pallas_call | solution.py:685
  107.7 3.3 %all-to-all-start.5 = ((f32[8,2,128]{2,1,0:T(2,128)}), f32[8,2,128]{2,1,0:T(2,128)S(1)}, u32[]{:S(2)}, u32[]{:S(2)}) async-start(f32[8,2,128]{2,1,0:T(2,128)} %bitcast.13), calls=%async_computation.5 | async-start | bytes 16384 | tf_op jit(solution)/shard_map/all_to_all | solution.py:686
  111.0 3.3 %shard_map.138.acc_ref = f32[96,256]{1,0:T(8,128)S(1)} custom-call(f32[1024,128]{1,0:T(8,128)S(1)} %get-tuple-element.79.rows_ref, s32[64,256]{1,0:T(8,128)S(1)} %reshape.76.conn_ref), custom_call_target="tpu_custom_call" | custom-call | flops 2147483648 | bytes 1048576 | tf_op jit(solution)/shard_map/pallas_call | solution.py:690
  114.4 3.1 %all-to-all-done.5 = f32[8,2,128]{2,1,0:T(2,128)S(1)} async-done(((f32[8,2,128]{2,1,0:T(2,128)}), f32[8,2,128]{2,1,0:T(2,128)S(1)}, u32[]{:S(2)}, u32[]{:S(2)}) %all-to-all-start.5) | async-done | bytes 8224 | tf_op jit(solution)/shard_map/all_to_all | solution.py:686
  117.5 1.5 shard_map.140
  119.0 1.6 collective-permute-start.10
  120.6 1.6 shard_map.139.force_ref
  122.8 0.9 shard_map.141
  123.7 1.5 collective-permute-start.12
  125.2 1.9 %shard_map.142.own_rows_ref = f32[512,128]{1,0:T(8,128)S(1)} custom-call(f32[8,2048]{1,0:T(8,128)S(1)} %get-tuple-element.83.own_ref.refs_0_, s32[64,256]{1,0:T(8,128)S(1)} %reshape.76.conn_ref), custom_call_target="tpu_custom_call" | custom-call | flops 2147483648 | bytes 1048576 | tf_op jit(solution)/shard_map/pallas_call | solution.py:675
  127.0 1.1 shard_map.144.node_ref
  128.2 2.0 %collective-permute-done.12.mesh_ref = f32[8,512]{1,0:T(8,128)S(1)} collective-permute-done((f32[8,512]{1,0:T(8,128)S(1)}, f32[8,512]{1,0:T(8,128)S(1)}, u32[]{:S(2)}, u32[]{:S(2)}) %collective-permute-start.12) | collective-permute-done | bytes 16416 | tf_op jit(solution)/shard_map/ppermute | solution.py:33
  130.2 1.8 %shard_map.143 = (f32[12,32,128]{2,1,0:T(8,128)S(1)}, f32[256,128]{1,0:T(8,128)}, f32[128,128]{1,0:T(8,128)}, f32[128,128]{1,0:T(8,128)S(1)}) custom-call(s32[4,16]{1,0:T(4,128)S(1)} %copy-done.1, f32[8,512]{1,0:T(8,128)S(1)} %collective-permute-done.12.mesh_ref, f32[8,512]{1,0:T(8,128)S(1)} %collective-permute-done.13.sub_ref, ...), custom_call_target="tpu_custom_call" | custom-call | flops 1073741824 | bytes 1048576 | tf_op jit(solution)/shard_map/pallas_call | solution.py:677
  132.0 3.4 %all-to-all-start.6 = ((f32[8,16,128]{2,1,0:T(8,128)}), f32[8,16,128]{2,1,0:T(8,128)S(1)}, u32[]{:S(2)}, u32[]{:S(2)}) async-start(f32[8,16,128]{2,1,0:T(8,128)} %bitcast.15), calls=%async_computation.6 | async-start | bytes 131072 | tf_op jit(solution)/shard_map/all_to_all | solution.py:680
  135.4 3.8 %shard_map.146 = (f32[1024,128]{1,0:T(8,128)S(1)}, f32[3,32,128]{2,1,0:T(8,128)S(1)}) custom-call(f32[8,2048]{1,0:T(8,128)S(1)} %get-tuple-element.83.own_ref.refs_0_, f32[8,512]{1,0:T(8,128)S(1)} %collective-permute-done.12.mesh_ref, f32[8,512]{1,0:T(8,128)S(1)} %collective-permute-done.13.sub_ref, s32[64,256]{1,0:T(8,128)S(1)} %reshape.76.conn_ref, ...), custom_call_target="tpu_custom_call" | custom-call | flops 2147483648 | bytes 1048576 | tf_op jit(solution)/shard_map/pallas_call | solution.py:684
  139.2 3.0 %all-to-all-done.6 = f32[8,16,128]{2,1,0:T(8,128)S(1)} async-done(((f32[8,16,128]{2,1,0:T(8,128)}), f32[8,16,128]{2,1,0:T(8,128)S(1)}, u32[]{:S(2)}, u32[]{:S(2)}) %all-to-all-start.6) | async-done | bytes 65568 | tf_op jit(solution)/shard_map/all_to_all | solution.py:680
  142.2 4.4 %shard_map.145 = (f32[8,2048]{1,0:T(8,128)S(1)}, f32[16,128]{1,0:T(8,128)}) custom-call(s32[4,4,16]{2,1,0:T(4,128)S(1)} %copy-done.3, bf16[4,2048,128]{2,1,0:T(8,128)(2,1)S(1)} %shard_map.144.node_ref, f32[128,128]{1,0:T(8,128)S(1)} %bitcast.34), custom_call_target="tpu_custom_call" | custom-call | flops 2147483648 | bytes 1048576 | tf_op jit(solution)/shard_map/pallas_call | solution.py:685
  146.6 3.3 %all-to-all-start.7 = ((f32[8,2,128]{2,1,0:T(2,128)}), f32[8,2,128]{2,1,0:T(2,128)S(1)}, u32[]{:S(2)}, u32[]{:S(2)}) async-start(f32[8,2,128]{2,1,0:T(2,128)} %bitcast.17), calls=%async_computation.7 | async-start | bytes 16384 | tf_op jit(solution)/shard_map/all_to_all | solution.py:686
  149.9 3.3 %shard_map.147.acc_ref = f32[96,256]{1,0:T(8,128)S(1)} custom-call(f32[1024,128]{1,0:T(8,128)S(1)} %get-tuple-element.91.rows_ref, s32[64,256]{1,0:T(8,128)S(1)} %reshape.76.conn_ref), custom_call_target="tpu_custom_call" | custom-call | flops 2147483648 | bytes 1048576 | tf_op jit(solution)/shard_map/pallas_call | solution.py:690
  153.9 2.5 %all-to-all-done.7 = f32[8,2,128]{2,1,0:T(2,128)S(1)} async-done(((f32[8,2,128]{2,1,0:T(2,128)}), f32[8,2,128]{2,1,0:T(2,128)S(1)}, u32[]{:S(2)}, u32[]{:S(2)}) %all-to-all-start.7) | async-done | bytes 8224 | tf_op jit(solution)/shard_map/all_to_all | solution.py:686
  156.4 1.5 shard_map.149
  157.9 2.2 %collective-permute-start.14 = (f32[8,512]{1,0:T(8,128)S(1)}, f32[8,512]{1,0:T(8,128)S(1)}, u32[]{:S(2)}, u32[]{:S(2)}) collective-permute-start(f32[8,512]{1,0:T(8,128)S(1)} %get-tuple-element.93), channel_id=1, source_target_pairs={{0,28},{4,0},{8,4},{12,8},{16,12},{20,16},{24,20},{28,24},{1,29},{... | collective-permute-start | bytes 49160 | tf_op jit(solution)/shard_map/ppermute | solution.py:33
  160.1 1.6 shard_map.148.refs_1_
  (45 shorter events, 6.3 us)
Async XLA Ops:
  3.4 8.2 %collective-permute-start = (f32[8,512]{1,0:T(8,128)S(1)}, f32[8,512]{1,0:T(8,128)S(1)}, u32[]{:S(2)}, u32[]{:S(2)}) collective-permute-start(f32[8,512]{1,0:T(8,128)S(1)} %get-tuple-element.49), channel_id=1, source_target_pairs={{0,4},{4,8},{8,12},{12,16},{16,20},{20,24},{24,28},{28,0},{1,5},{5... | collective-permute-start | bytes 49160 | tf_op jit(solution)/shard_map/ppermute | solution.py:33
  6.4 5.2 %collective-permute-start.1 = (f32[8,512]{1,0:T(8,128)S(1)}, f32[8,512]{1,0:T(8,128)S(1)}, u32[]{:S(2)}, u32[]{:S(2)}) collective-permute-start(f32[8,512]{1,0:T(8,128)S(1)} %get-tuple-element.50), channel_id=1, source_target_pairs={{0,1},{1,2},{2,3},{3,0},{4,5},{5,6},{6,7},{7,4},{8,9},{9,10},{10,1... | collective-permute-start | bytes 49160 | tf_op jit(solution)/shard_map/ppermute | solution.py:33
  7.3 1.9 %copy-start.2 = (s32[4,4,2048]{2,1,0:T(4,128)S(1)}, s32[4,4,2048]{2,1,0:T(4,128)}, u32[]{:S(2)}) copy-start(s32[4,4,2048]{2,1,0:T(4,128)} %mask_ref.7) | copy-start | bytes 393220
  9.1 1.2 copy-start.6
  9.2 1.2 copy-start.1
  13.4 11.9 %all-to-all-start = ((f32[8,16,128]{2,1,0:T(8,128)}), f32[8,16,128]{2,1,0:T(8,128)S(1)}, u32[]{:S(2)}, u32[]{:S(2)}) async-start(f32[8,16,128]{2,1,0:T(8,128)} %bitcast.2), calls=%async_computation | async-start | bytes 131072 | tf_op jit(solution)/shard_map/all_to_all | solution.py:680
  18.3 7.0 %copy-start.3 = (s32[4,4,16]{2,1,0:T(4,128)S(1)}, s32[4,4,16]{2,1,0:T(4,128)}, u32[]{:S(2)}) copy-start(s32[4,4,16]{2,1,0:T(4,128)} %list_any.7) | copy-start | bytes 3076
  29.6 9.8 %all-to-all-start.1 = ((f32[8,2,128]{2,1,0:T(2,128)}), f32[8,2,128]{2,1,0:T(2,128)S(1)}, u32[]{:S(2)}, u32[]{:S(2)}) async-start(f32[8,2,128]{2,1,0:T(2,128)} %bitcast.4), calls=%async_computation.1 | async-start | bytes 16384 | tf_op jit(solution)/shard_map/all_to_all | solution.py:686
  40.9 3.8 %copy-start = (f32[2048]{0:T(1024)S(1)}, f32[2048]{0:T(1024)}, u32[]{:S(2)}) copy-start(f32[2048]{0:T(1024)} %param.12) | copy-start | bytes 24580
  40.9 3.8 %collective-permute-start.2 = (f32[8,512]{1,0:T(8,128)S(1)}, f32[8,512]{1,0:T(8,128)S(1)}, u32[]{:S(2)}, u32[]{:S(2)}) collective-permute-start(f32[8,512]{1,0:T(8,128)S(1)} %get-tuple-element.57), channel_id=1, source_target_pairs={{0,28},{4,0},{8,4},{12,8},{16,12},{20,16},{24,20},{28,24},{1,29},{... | collective-permute-start | bytes 49160 | tf_op jit(solution)/shard_map/ppermute | solution.py:33
  42.5 2.2 %collective-permute-start.3 = (f32[8,512]{1,0:T(8,128)S(1)}, f32[8,512]{1,0:T(8,128)S(1)}, u32[]{:S(2)}, u32[]{:S(2)}) collective-permute-start(f32[8,512]{1,0:T(8,128)S(1)} %get-tuple-element.58), channel_id=1, source_target_pairs={{0,3},{1,0},{2,1},{3,2},{4,7},{5,4},{6,5},{7,6},{8,11},{9,8},{10,9... | collective-permute-start | bytes 49160 | tf_op jit(solution)/shard_map/ppermute | solution.py:33
  45.6 6.5 %collective-permute-start.4 = (f32[8,512]{1,0:T(8,128)S(1)}, f32[8,512]{1,0:T(8,128)S(1)}, u32[]{:S(2)}, u32[]{:S(2)}) collective-permute-start(f32[8,512]{1,0:T(8,128)S(1)} %get-tuple-element.60), channel_id=1, source_target_pairs={{0,4},{4,8},{8,12},{12,16},{16,20},{20,24},{24,28},{28,0},{1,5},{5... | collective-permute-start | bytes 49160 | tf_op jit(solution)/shard_map/ppermute | solution.py:33
  47.1 5.0 %collective-permute-start.5 = (f32[8,512]{1,0:T(8,128)S(1)}, f32[8,512]{1,0:T(8,128)S(1)}, u32[]{:S(2)}, u32[]{:S(2)}) collective-permute-start(f32[8,512]{1,0:T(8,128)S(1)} %get-tuple-element.61), channel_id=1, source_target_pairs={{0,1},{1,2},{2,3},{3,0},{4,5},{5,6},{6,7},{7,4},{8,9},{9,10},{10,1... | collective-permute-start | bytes 49160 | tf_op jit(solution)/shard_map/ppermute | solution.py:33
  54.0 10.4 %all-to-all-start.2 = ((f32[8,16,128]{2,1,0:T(8,128)}), f32[8,16,128]{2,1,0:T(8,128)S(1)}, u32[]{:S(2)}, u32[]{:S(2)}) async-start(f32[8,16,128]{2,1,0:T(8,128)} %bitcast.7), calls=%async_computation.2 | async-start | bytes 131072 | tf_op jit(solution)/shard_map/all_to_all | solution.py:680
  68.8 9.8 %all-to-all-start.3 = ((f32[8,2,128]{2,1,0:T(2,128)}), f32[8,2,128]{2,1,0:T(2,128)S(1)}, u32[]{:S(2)}, u32[]{:S(2)}) async-start(f32[8,2,128]{2,1,0:T(2,128)} %bitcast.9), calls=%async_computation.3 | async-start | bytes 16384 | tf_op jit(solution)/shard_map/all_to_all | solution.py:686
  80.1 3.8 %collective-permute-start.6 = (f32[8,512]{1,0:T(8,128)S(1)}, f32[8,512]{1,0:T(8,128)S(1)}, u32[]{:S(2)}, u32[]{:S(2)}) collective-permute-start(f32[8,512]{1,0:T(8,128)S(1)} %get-tuple-element.69), channel_id=1, source_target_pairs={{0,28},{4,0},{8,4},{12,8},{16,12},{20,16},{24,20},{28,24},{1,29},{... | collective-permute-start | bytes 49160 | tf_op jit(solution)/shard_map/ppermute | solution.py:33
  81.6 2.2 %collective-permute-start.7 = (f32[8,512]{1,0:T(8,128)S(1)}, f32[8,512]{1,0:T(8,128)S(1)}, u32[]{:S(2)}, u32[]{:S(2)}) collective-permute-start(f32[8,512]{1,0:T(8,128)S(1)} %get-tuple-element.70), channel_id=1, source_target_pairs={{0,3},{1,0},{2,1},{3,2},{4,7},{5,4},{6,5},{7,6},{8,11},{9,8},{10,9... | collective-permute-start | bytes 49160 | tf_op jit(solution)/shard_map/ppermute | solution.py:33
  84.8 6.5 %collective-permute-start.8 = (f32[8,512]{1,0:T(8,128)S(1)}, f32[8,512]{1,0:T(8,128)S(1)}, u32[]{:S(2)}, u32[]{:S(2)}) collective-permute-start(f32[8,512]{1,0:T(8,128)S(1)} %get-tuple-element.72), channel_id=1, source_target_pairs={{0,4},{4,8},{8,12},{12,16},{16,20},{20,24},{24,28},{28,0},{1,5},{5... | collective-permute-start | bytes 49160 | tf_op jit(solution)/shard_map/ppermute | solution.py:33
  86.3 5.0 %collective-permute-start.9 = (f32[8,512]{1,0:T(8,128)S(1)}, f32[8,512]{1,0:T(8,128)S(1)}, u32[]{:S(2)}, u32[]{:S(2)}) collective-permute-start(f32[8,512]{1,0:T(8,128)S(1)} %get-tuple-element.73), channel_id=1, source_target_pairs={{0,1},{1,2},{2,3},{3,0},{4,5},{5,6},{6,7},{7,4},{8,9},{9,10},{10,1... | collective-permute-start | bytes 49160 | tf_op jit(solution)/shard_map/ppermute | solution.py:33
  93.1 10.2 %all-to-all-start.4 = ((f32[8,16,128]{2,1,0:T(8,128)}), f32[8,16,128]{2,1,0:T(8,128)S(1)}, u32[]{:S(2)}, u32[]{:S(2)}) async-start(f32[8,16,128]{2,1,0:T(8,128)} %bitcast.11), calls=%async_computation.4 | async-start | bytes 131072 | tf_op jit(solution)/shard_map/all_to_all | solution.py:680
  100.3 7.4 %copy-start.4 = (f32[3,32,128]{2,1,0:T(8,128)}, f32[3,32,128]{2,1,0:T(8,128)S(1)}, u32[]{:S(2)}) copy-start(f32[3,32,128]{2,1,0:T(8,128)S(1)} %get-tuple-element.90.stress_ref) | copy-start | bytes 147460
  107.7 9.8 %all-to-all-start.5 = ((f32[8,2,128]{2,1,0:T(2,128)}), f32[8,2,128]{2,1,0:T(2,128)S(1)}, u32[]{:S(2)}, u32[]{:S(2)}) async-start(f32[8,2,128]{2,1,0:T(2,128)} %bitcast.13), calls=%async_computation.5 | async-start | bytes 16384 | tf_op jit(solution)/shard_map/all_to_all | solution.py:686
  119.0 3.8 %collective-permute-start.10 = (f32[8,512]{1,0:T(8,128)S(1)}, f32[8,512]{1,0:T(8,128)S(1)}, u32[]{:S(2)}, u32[]{:S(2)}) collective-permute-start(f32[8,512]{1,0:T(8,128)S(1)} %get-tuple-element.81), channel_id=1, source_target_pairs={{0,28},{4,0},{8,4},{12,8},{16,12},{20,16},{24,20},{28,24},{1,29},{... | collective-permute-start | bytes 49160 | tf_op jit(solution)/shard_map/ppermute | solution.py:33
  120.6 2.2 %collective-permute-start.11 = (f32[8,512]{1,0:T(8,128)S(1)}, f32[8,512]{1,0:T(8,128)S(1)}, u32[]{:S(2)}, u32[]{:S(2)}) collective-permute-start(f32[8,512]{1,0:T(8,128)S(1)} %get-tuple-element.82), channel_id=1, source_target_pairs={{0,3},{1,0},{2,1},{3,2},{4,7},{5,4},{6,5},{7,6},{8,11},{9,8},{10,9... | collective-permute-start | bytes 49160 | tf_op jit(solution)/shard_map/ppermute | solution.py:33
  123.7 6.5 %collective-permute-start.12 = (f32[8,512]{1,0:T(8,128)S(1)}, f32[8,512]{1,0:T(8,128)S(1)}, u32[]{:S(2)}, u32[]{:S(2)}) collective-permute-start(f32[8,512]{1,0:T(8,128)S(1)} %get-tuple-element.84), channel_id=1, source_target_pairs={{0,4},{4,8},{8,12},{12,16},{16,20},{20,24},{24,28},{28,0},{1,5},{5... | collective-permute-start | bytes 49160 | tf_op jit(solution)/shard_map/ppermute | solution.py:33
  125.2 5.0 %collective-permute-start.13 = (f32[8,512]{1,0:T(8,128)S(1)}, f32[8,512]{1,0:T(8,128)S(1)}, u32[]{:S(2)}, u32[]{:S(2)}) collective-permute-start(f32[8,512]{1,0:T(8,128)S(1)} %get-tuple-element.85), channel_id=1, source_target_pairs={{0,1},{1,2},{2,3},{3,0},{4,5},{5,6},{6,7},{7,4},{8,9},{9,10},{10,1... | collective-permute-start | bytes 49160 | tf_op jit(solution)/shard_map/ppermute | solution.py:33
  128.2 7.2 %copy-start.5 = (f32[3,32,128]{2,1,0:T(8,128)S(1)}, f32[3,32,128]{2,1,0:T(8,128)}, u32[]{:S(2)}) copy-start(f32[3,32,128]{2,1,0:T(8,128)} %copy-done.4) | copy-start | bytes 147460
  132.0 10.2 %all-to-all-start.6 = ((f32[8,16,128]{2,1,0:T(8,128)}), f32[8,16,128]{2,1,0:T(8,128)S(1)}, u32[]{:S(2)}, u32[]{:S(2)}) async-start(f32[8,16,128]{2,1,0:T(8,128)} %bitcast.15), calls=%async_computation.6 | async-start | bytes 131072 | tf_op jit(solution)/shard_map/all_to_all | solution.py:680
  146.6 9.8 %all-to-all-start.7 = ((f32[8,2,128]{2,1,0:T(2,128)}), f32[8,2,128]{2,1,0:T(2,128)S(1)}, u32[]{:S(2)}, u32[]{:S(2)}) async-start(f32[8,2,128]{2,1,0:T(2,128)} %bitcast.17), calls=%async_computation.7 | async-start | bytes 16384 | tf_op jit(solution)/shard_map/all_to_all | solution.py:686
  157.9 3.8 %collective-permute-start.14 = (f32[8,512]{1,0:T(8,128)S(1)}, f32[8,512]{1,0:T(8,128)S(1)}, u32[]{:S(2)}, u32[]{:S(2)}) collective-permute-start(f32[8,512]{1,0:T(8,128)S(1)} %get-tuple-element.93), channel_id=1, source_target_pairs={{0,28},{4,0},{8,4},{12,8},{16,12},{20,16},{24,20},{28,24},{1,29},{... | collective-permute-start | bytes 49160 | tf_op jit(solution)/shard_map/ppermute | solution.py:33
  160.1 1.6 collective-permute-start.15
where the time goes:
time: 164 us; the launch traced here: 163 us
  Pallas kernels  82.2 us (50%)
  starting transfers between devices  42.9 us (26%)
  waiting for transfers between devices  32 us (20%)
  local copies, waits for them, and re-layouts  3.67 us (2%)
    pallas_call x4, Pallas kernels, per_device(): slave, react = contact(step)(bucket_list, node, incoming)  17.4 us
    pallas_call x4, Pallas kernels, per_device(): forces(own, from_mesh, from_sub, conn, corner, stress_now)  15.3 us
    all_to_all x4, starting transfers between devices, per_device(): lax.all_to_all(outgoing.reshape(peers, per_peer * ROWS, SEG), 'mesh', spl...  15 us
    ppermute x16, starting transfers between devices, shifted(): return lax.ppermute(value, axis, pairs)  14.5 us
    all_to_all x4, starting transfers between devices, per_device(): lax.all_to_all(react.reshape(peers, per_peer, SEG), 'mesh', split_axis=0,...  13.4 us
    pallas_call x4, Pallas kernels, per_device(): acc, = internal_of(pushes, conn)  13.2 us
    all_to_all x4, waiting for transfers between devices, per_device(): lax.all_to_all(outgoing.reshape(peers, per_peer * ROWS, SEG), 'mesh', spl...  12.3 us
    all_to_all x4, waiting for transfers between devices, per_device(): lax.all_to_all(react.reshape(peers, per_peer, SEG), 'mesh', split_axis=0,...  11.9 us
  transfers between devices with their start and end apart: 24, of which 14 were waited for; matrix products, arithmetic and copies ran while one was open for 1% of the time, Pallas kernels for 30%

commit v1 on v0

--- a/solution.py
+++ b/solution.py
@@ -13,7 +13,8 @@
 STEPS = 4
 LOW = 256
 ROWS = 8
-UNROLL = 16
+SENT = 6
+UNROLL = 8
 
 TIME_STEP = 0.2
 YOUNG = 1.0
@@ -45,9 +46,9 @@
     return high, mid, rest - mid
 
 
-def one_hot_low(low_ids):
+def one_hot_low(low_ids, low=LOW):
     width = low_ids.shape[1]
-    rows = lax.broadcasted_iota(jnp.int32, (LOW, width), 0)
+    rows = lax.broadcasted_iota(jnp.int32, (low, width), 0)
     return jnp.where(rows == low_ids, 1.0, 0.0).astype(BF16)
 
 
@@ -72,19 +73,34 @@
     return jnp.concatenate([high, low, pad], axis=0)
 
 
+def corner_ids(conn_ref, block):
+    return conn_ref[:, pl.ds(pl.multiple_of(block * SEG, SEG), SEG)]
+
+
+def pair_row(ids, half):
+    return jnp.concatenate([ids[2 * half : 2 * half + 1], ids[2 * half + 1 : 2 * half + 2]], axis=1)
+
+
+def pair_lanes(ids, half):
+    rows = [jnp.broadcast_to(ids[2 * half + i : 2 * half + i + 1], (4, SEG)) for i in range(2)]
+    return jnp.concatenate(rows, axis=0)
+
+
 def gather_tiles(table, conn_ref, out_ref):
     count = table.shape[0] // ROWS
 
-    def tile(index, carry):
-        ids = conn_ref[pl.ds(index, 1), :]
-        product = jnp.dot(table, one_hot_low(ids & (LOW - 1)), preferred_element_type=F32)
-        total = pick_high(product, ids >> 8, count)
-        for half in range(LOW // SEG):
-            start = pl.multiple_of((index * (LOW // SEG) + half) * ROWS, ROWS)
-            out_ref[pl.ds(start, ROWS), :] = total[:, half * SEG : (half + 1) * SEG]
+    def tile(block, carry):
+        corners = corner_ids(conn_ref, block)
+        for half in range(2):
+            ids = pair_row(corners, half)
+            product = jnp.dot(table, one_hot_low(ids & (LOW - 1)), preferred_element_type=F32)
+            total = pick_high(product, ids >> 8, count)
+            for i in range(2):
+                start = pl.multiple_of((block * 4 + half * 2 + i) * ROWS, ROWS)
+                out_ref[pl.ds(start, ROWS), :] = total[:, i * SEG : (i + 1) * SEG]
         return carry
 
-    lax.fori_loop(0, conn_ref.shape[0], tile, 0, unroll=UNROLL)
+    lax.fori_loop(0, conn_ref.shape[1] // SEG, tile, 0, unroll=UNROLL // 2)
 
 
 def cross(left, right):
@@ -139,12 +155,6 @@
         chunk_ref[first + part] = twice[:, part * SEG : (part + 1) * SEG]
 
 
-def lane_ids(conn_ref, index):
-    ids = conn_ref[pl.ds(index, 1), :]
-    halves = [jnp.broadcast_to(ids[:, h * SEG : (h + 1) * SEG], (4, SEG)) for h in range(2)]
-    return jnp.concatenate(halves, axis=0)
-
-
 def lane_pick(chunk_ref, ids, high_ids):
     count = chunk_ref.shape[0]
     low_ids = ids & (SEG - 1)
@@ -159,13 +169,15 @@
 def own_rows_kernel(own_ref, conn_ref, rows_ref, chunk_ref):
     fill_chunks(own_ref[0:3, :], chunk_ref, 0)
 
-    def tile(index, carry):
-        ids = lane_ids(conn_ref, index)
-        start = pl.multiple_of(index * ROWS, ROWS)
-        rows_ref[pl.ds(start, ROWS), :] = lane_pick(chunk_ref, ids, ids >> 7)
+    def tile(block, carry):
+        corners = corner_ids(conn_ref, block)
+        for half in range(2):
+            ids = pair_lanes(corners, half)
+            start = pl.multiple_of((block * 2 + half) * ROWS, ROWS)
+            rows_ref[pl.ds(start, ROWS), :] = lane_pick(chunk_ref, ids, ids >> 7)
         return carry
 
-    lax.fori_loop(0, conn_ref.shape[0], tile, 0, unroll=8)
+    lax.fori_loop(0, conn_ref.shape[1] // SEG, tile, 0, unroll=4)
 
 
 def geometry_kernel(
@@ -179,15 +191,17 @@
     fill_chunks(mesh_ref[0:3, :], chunk_ref, 0)
     fill_chunks(sub_ref[0:3, :], chunk_ref, first)
 
-    def tile(index, carry):
-        ids = lane_ids(conn_ref, index)
-        start = pl.multiple_of(index * ROWS, ROWS)
-        far = lane_pick(chunk_ref, ids, (ids >> 7) - nodes // SEG)
-        near = own_rows_ref[pl.ds(start, ROWS), :]
-        rows_ref[pl.ds(start, ROWS), :] = jnp.where(ids >= nodes, far, near)
+    def tile(block, carry):
+        corners = corner_ids(conn_ref, block)
+        for half in range(2):
+            ids = pair_lanes(corners, half)
+            start = pl.multiple_of((block * 2 + half) * ROWS, ROWS)
+            far = lane_pick(chunk_ref, ids, (ids >> 7) - nodes // SEG)
+            near = own_rows_ref[pl.ds(start, ROWS), :]
+            rows_ref[pl.ds(start, ROWS), :] = jnp.where(ids >= nodes, far, near)
         return carry
 
-    lax.fori_loop(0, conn_ref.shape[0], tile, 0, unroll=16)
+    lax.fori_loop(0, conn_ref.shape[1] // SEG, tile, 0, unroll=16)
     for group in range(blocks // 8):
         corner = [
             tuple(rows_ref[pl.ds(group * 128 + i * 4 + c, 8, stride=16), :] for c in range(3))
@@ -203,16 +217,30 @@
         for c in range(6, ROWS):
             geo_ref[pl.ds(group * 8 * ROWS + c, 8, stride=ROWS), :] = jnp.zeros((8, SEG), F32)
 
-    def copy(slot, carry):
-        start = pl.multiple_of(picks_ref[step, slot] * ROWS, ROWS)
-        here = pl.ds(pl.multiple_of(slot * ROWS, ROWS), ROWS)
-        block = geo_ref[pl.ds(start, ROWS), :]
-        out_ref[here, :] = block
-        kept_ref[here, :] = block
-        return carry
-
     fetch.wait()
-    lax.fori_loop(0, out_ref.shape[0] // ROWS, copy, 0, unroll=16)
+    peers, groups = out_ref.shape[:2]
+    per_peer = picks_ref.shape[1] // peers
+    for peer in range(peers):
+        rows = []
+        for slot in range(peer * per_peer, (peer + 1) * per_peer):
+            start = pl.multiple_of(picks_ref[step, slot] * ROWS, ROWS)
+            block = geo_ref[pl.ds(start, ROWS), :]
+            rows.append(block[:SENT])
+            if kept_ref is not None:
+                kept_ref[slot * ROWS : (slot + 1) * ROWS, :] = block
+        rows.append(jnp.zeros((groups * 4 - per_peer * SENT, SEG), F32))
+        rows = jnp.concatenate([part for part in rows if part.shape[0]], axis=0)
+        for group in range(groups):
+            out_ref[peer, group] = rows[group * 4 : (group + 1) * 4]
+
+
+def geometry_slots_kernel(step, nodes, *refs):
+    ins, (corner_ref, kept_ref, out_ref), (geo_ref, *scratch) = refs[:5], refs[5:8], refs[8:]
+    geometry_kernel(step, nodes, *ins, corner_ref, geo_ref, out_ref, kept_ref, *scratch)
+
+
+def geometry_blocks_kernel(step, nodes, *refs):
+    geometry_kernel(step, nodes, *refs[:8], None, *refs[8:])
 
 
 def force_kernel(
@@ -284,7 +312,7 @@
 def row_mix(three, extras):
     width = three.shape[1]
     rows = [three] + extras
-    pad = ROWS - sum(part.shape[0] for part in rows)
+    pad = -sum(part.shape[0] for part in rows) % ROWS
     if pad:
         rows.append(jnp.zeros((pad, width), F32))
     return jnp.concatenate(rows, axis=0)
@@ -296,10 +324,7 @@
         split_three(place[0:1] ** 2 + place[1:2] ** 2 + place[2:3] ** 2), axis=0
     )
     tiles = product_tiles(place, True)
-    gap = [row_mix(tiles[0], [ones])] + [row_mix(tile, []) for tile in tiles[1:]]
-    far = [row_mix(tiles[0], [ones]), row_mix(tiles[1], [square])]
-    far += [row_mix(tile, []) for tile in tiles[2:]]
-    return gap, far
+    return row_mix(tiles[0], tiles[1:] + [ones]), row_mix(tiles[0], tiles[1:] + [ones, square])
 
 
 def segment_features(centre, normal):
@@ -309,14 +334,12 @@
     square = centre[0:1] ** 2 + centre[1:2] ** 2 + centre[2:3] ** 2
     square = jnp.concatenate(split_three(square), axis=0)
     tiles = product_tiles(normal, False)
-    gap = [row_mix(tiles[0], [lean])] + [row_mix(tile, []) for tile in tiles[1:]]
+    gap = row_mix(tiles[0], tiles[1:] + [lean])
     tiles = product_tiles(-2.0 * centre, False)
-    far = [row_mix(tiles[0], [square]), row_mix(tiles[1], [ones])]
-    far += [row_mix(tile, []) for tile in tiles[2:]]
-    return gap, far
-
-
-FEATURES = 12 * ROWS
+    return gap, row_mix(tiles[0], tiles[1:] + [square, ones])
+
+
+FEATURES = 6 * ROWS
 SCALE = math.sqrt(math.log2(math.e) / REACH)
 
 
@@ -329,7 +352,7 @@
         mask = mask_ref[step, :, pl.ds(start, SEG)].astype(F32)
         for k in range(cands):
             live = mask[k : k + 1]
-            rows = jnp.concatenate([tile * live for tile in gap] + far, axis=0)
+            rows = jnp.concatenate([gap * live, far], axis=0)
             rows = jnp.concatenate([rows, jnp.zeros((SEG - FEATURES, SEG), F32)], axis=0)
             node_ref[k, pl.ds(start, SEG), :] = rows.T.astype(BF16)
         return carry
@@ -347,48 +370,51 @@
     slots = react_ref.shape[0]
     react_ref[...] = jnp.zeros_like(react_ref)
 
-    def segments(index, carry):
-        tile = slots_ref[pl.ds(pl.multiple_of(index * ROWS, ROWS), ROWS), :]
+    peers, groups = slots_ref.shape[:2]
+    per_peer = slots // peers
+    for index in range(slots):
+        if index % per_peer == 0:
+            rows = [slots_ref[index // per_peer, group] for group in range(groups)]
+            rows = jnp.concatenate(rows, axis=0)
+        tile = rows[index % per_peer * SENT : (index % per_peer + 1) * SENT]
         gap, far = segment_features(tile[0:3] * SCALE, tile[3:6])
-        blank = jnp.zeros((6 * ROWS, SEG), F32)
-        left = jnp.concatenate(gap + [blank], axis=0)
-        right = jnp.concatenate([blank] + far, axis=0)
-        rows = jnp.concatenate([left, right], axis=1)
-        seg_ref[index] = rows.astype(BF16)
+        blank = jnp.zeros((FEATURES // 2, SEG), F32)
+        left = jnp.concatenate([gap, blank], axis=0)
+        right = jnp.concatenate([blank, far], axis=0)
+        seg_ref[index] = jnp.concatenate([left, right], axis=1).astype(BF16)
         push = split_rows(tile[3:6])
         push = jnp.concatenate([push, push], axis=1)
         push_ref[index] = jnp.concatenate([push, jnp.zeros_like(push)], axis=0).astype(BF16)
-        return carry
-
-    lax.fori_loop(0, slots, segments, 0, unroll=4)
     fetch.wait()
 
     def bucket(index, carry):
         start = pl.multiple_of(index * SEG, SEG)
-        total = jnp.zeros((2 * ROWS, SEG), F32)
-        for k in range(cands):
-            slot = list_ref[step, k, index]
-            pair = jnp.dot(
+        chosen = [list_ref[step, k, index] for k in range(cands)]
+        pairs = [
+            jnp.dot(
                 node_ref[k, pl.ds(start, SEG), :][:, :FEATURES],
-                seg_ref[slot],
+                seg_ref[chosen[k]],
                 preferred_element_type=F32,
             )
-            gap, far = pair[:, :SEG], pair[:, SEG:]
+            for k in range(cands)
+        ]
+        parts = []
+        for k in range(cands):
+            gap, far = pairs[k][:, :SEG], pairs[k][:, SEG:]
             weight = jnp.minimum(gap, 0.0) * jnp.exp2(gap * gap - far)
-            react_ref[pl.ds(slot, 1), :] += jnp.sum(weight, axis=0, keepdims=True)
+            react_ref[pl.ds(chosen[k], 1), :] += jnp.sum(weight, axis=0, keepdims=True)
             high = weight.astype(BF16)
             low = (weight - high.astype(F32)).astype(BF16)
-            total = total + lax.dot_general(
-                push_ref[slot],
-                jnp.concatenate([high, low], axis=1),
-                (((1,), (1,)), ((), ())),
-                preferred_element_type=F32,
-            )
+            parts.append(jnp.concatenate([high, low], axis=1))
+        total = dot_rows(
+            jnp.concatenate([push_ref[slot] for slot in chosen], axis=1),
+            jnp.concatenate(parts, axis=1),
+        )
         force = (total[0:3] + total[3:6]) * (-PENALTY / SCALE)
         force_ref[:, pl.ds(start, SEG)] = row_mix(force, [])
         return carry
 
-    lax.fori_loop(0, buckets, bucket, 0, unroll=4)
+    lax.fori_loop(0, buckets, bucket, 0, unroll=16)
     react_ref[...] = react_ref[...] * (-PENALTY / SCALE)
 
 
@@ -400,12 +426,10 @@
     for step in range(tiles_ref.shape[0]):
 
         def copy(slot, carry):
-            for half in range(2):
-                row = conn_ref[pl.ds(picks_ref[step, slot] * 2 + half, 1), :]
-                tiles_ref[step, pl.ds(slot * 2 + half, 1), :] = row
+            tiles_ref[step, slot] = corner_ids(conn_ref, picks_ref[step, slot])
             return carry
 
-        lax.fori_loop(0, tiles_ref.shape[1] // 2, copy, 0, unroll=8)
+        lax.fori_loop(0, tiles_ref.shape[1], copy, 0, unroll=8)
 
 
 def collect_kernel(step, picks_ref, back_ref, seg_ref):
@@ -418,28 +442,21 @@
     lax.fori_loop(0, back_ref.shape[0], collect, 0)
 
 
-def react_tiles(step, first, last, blocks_ref, back_ref, tiles_ref):
+def react_tiles(step, first, last, low, unroll, blocks_ref, back_ref, tiles_ref):
     def tile(index, total):
         react = back_ref[pl.ds(index, 1), :]
         normal = blocks_ref[pl.ds(pl.multiple_of(index * ROWS, ROWS), ROWS), :][3:6]
         rows = split_rows(-0.25 * react * normal)
         values = jnp.concatenate([rows, rows], axis=1)
+        corners = tiles_ref[step, index]
         for half in range(2):
-            ids = tiles_ref[step, pl.ds(index * 2 + half, 1), :]
-            high_ids = ids >> 8
-            spread = jnp.concatenate(
-                [jnp.where(high_ids == part, values, 0.0) for part in range(first, last)], axis=0
-            ).astype(BF16)
-            total = total + lax.dot_general(
-                spread,
-                one_hot_low(ids & (LOW - 1)),
-                (((1,), (1,)), ((), ())),
-                preferred_element_type=F32,
-            )
+            ids = pair_row(corners, half)
+            spread = spread_rows(values, ids, first, last, low)
+            total = total + dot_rows(spread, one_hot_low(ids & (low - 1), low))
         return total
 
-    start = jnp.zeros(((last - first) * ROWS, LOW), F32)
-    return lax.fori_loop(0, back_ref.shape[0], tile, start, unroll=8)
+    start = jnp.zeros(((last - first) * ROWS, low), F32)
+    return lax.fori_loop(0, back_ref.shape[0], tile, start, unroll=unroll)
 
 
 def unstack(total):
@@ -451,108 +468,128 @@
 
 
 def react_ghost_kernel(step, blocks_ref, back_ref, tiles_ref, acc_ref, mesh_ref, sub_ref):
-    last = acc_ref.shape[0] // ROWS
-    first = last - (mesh_ref.shape[1] + sub_ref.shape[1]) // LOW
-    total = react_tiles(step, first, last, blocks_ref, back_ref, tiles_ref)
-    full = unstack(total + acc_ref[first * ROWS :, :])
+    count = acc_ref.shape[0] // ROWS
+    ghosts = mesh_ref.shape[1] + sub_ref.shape[1]
+    first, last = count * LOW // SEG - ghosts // SEG, count * LOW // SEG
+    total = react_tiles(step, first, last, SEG, 16, blocks_ref, back_ref, tiles_ref)
+    full = unstack(total) + unstack(acc_ref[(count - ghosts // LOW) * ROWS :, :])
     mesh_ref[...] = full[:, : mesh_ref.shape[1]]
     sub_ref[...] = full[:, mesh_ref.shape[1] :]
 
 
 def react_own_kernel(step, blocks_ref, back_ref, tiles_ref, acc_ref, own_ref):
     last = own_ref.shape[1] // LOW
-    total = react_tiles(step, 0, last, blocks_ref, back_ref, tiles_ref)
+    total = react_tiles(step, 0, last, LOW, 8, blocks_ref, back_ref, tiles_ref)
     own_ref[...] = unstack(total + acc_ref[: last * ROWS, :])
+
+
+def spread_rows(values, ids, first, last, low=LOW):
+    high_ids = ids >> (low.bit_length() - 1)
+    parts = [jnp.where(high_ids == part, values, 0.0) for part in range(first, last)]
+    return jnp.concatenate(parts, axis=0).astype(BF16)
+
+
+def dot_rows(left, right):
+    return lax.dot_general(left, right, (((1,), (1,)), ((), ())), preferred_element_type=F32)
 
 
 def scatter_tiles(rows_ref, conn_ref, acc_ref):
     count = acc_ref.shape[0] // ROWS
     acc_ref[...] = jnp.zeros_like(acc_ref)
 
-    def tile(index, carry):
-        ids = conn_ref[pl.ds(index, 1), :]
-        start = pl.multiple_of(index * (LOW // SEG) * ROWS, ROWS * (LOW // SEG))
-        parts = [rows_ref[pl.ds(start + half * ROWS, ROWS), :] for half in range(LOW // SEG)]
-        values = jnp.concatenate(parts, axis=1)
-        high_ids = ids >> 8
-        spread = jnp.concatenate(
-            [jnp.where(high_ids == part, values, 0.0) for part in range(count)], axis=0
-        ).astype(BF16)
-        acc_ref[...] += lax.dot_general(
-            spread,
-            one_hot_low(ids & (LOW - 1)),
-            (((1,), (1,)), ((), ())),
-            preferred_element_type=F32,
-        )
+    def tile(block, carry):
+        corners = corner_ids(conn_ref, block)
+        for half in range(2):
+            ids = pair_row(corners, half)
+            start = pl.multiple_of((block * 2 + half) * 2 * ROWS, 2 * ROWS)
+            parts = [rows_ref[pl.ds(start + i * ROWS, ROWS), :] for i in range(2)]
+            spread = spread_rows(jnp.concatenate(parts, axis=1), ids, 0, count)
+            acc_ref[...] += dot_rows(spread, one_hot_low(ids & (LOW - 1)))
         return carry
 
-    lax.fori_loop(0, conn_ref.shape[0], tile, 0, unroll=UNROLL)
+    lax.fori_loop(0, conn_ref.shape[1] // SEG, tile, 0, unroll=UNROLL // 2)
 
 
 def add_back(back, ids_ref, count):
+    rows = split_rows(back[0:3])
     total = jnp.zeros((count * ROWS, LOW), F32)
-    high, low = split_two(back[0:3])
-    pad = jnp.zeros((ROWS - 6, back.shape[1]), F32)
-    rows = jnp.concatenate([high, low, pad], axis=0)
-    for index in range(ids_ref.shape[0]):
-        ids = ids_ref[index : index + 1, :]
-        values = rows[:, index * LOW : (index + 1) * LOW]
-        spread = jnp.concatenate(
-            [jnp.where((ids >> 8) == part, values, 0.0) for part in range(count)], axis=0
-        ).astype(BF16)
-        total = total + lax.dot_general(
-            spread,
-            one_hot_low(ids & (LOW - 1)),
-            (((1,), (1,)), ((), ())),
-            preferred_element_type=F32,
-        )
+    for index in range(back.shape[1] // LOW):
+        here = slice(index * LOW, (index + 1) * LOW)
+        ids = ids_ref[:, here]
+        spread = spread_rows(rows[:, here], ids, 0, count)
+        total = total + dot_rows(spread, one_hot_low(ids & (LOW - 1)))
     return total
 
 
-def pack_ghosts(own, ids_ref, out_ref):
-    count = own.shape[1] // LOW
-    tables = [stack_columns(part).astype(BF16) for part in split_three(own)]
-    for index in range(ids_ref.shape[0]):
-        ids = ids_ref[index : index + 1, :]
-        hot = one_hot_low(ids & (LOW - 1))
-        product = sum(jnp.dot(table, hot, preferred_element_type=F32) for table in tables)
-        out_ref[:, index * LOW : (index + 1) * LOW] = pick_high(product, ids >> 8, count)
-
-
-def pack_kernel(own_ref, mesh_ids_ref, sub_ids_ref, to_mesh_ref, to_sub_ref):
-    own = own_ref[...]
-    pack_ghosts(own, mesh_ids_ref, to_mesh_ref)
-    pack_ghosts(own, sub_ids_ref, to_sub_ref)
-
-
-def update_kernel(
+def pack_ghosts(table, ids_ref, out_ref):
+    count = table.shape[0] // (3 * ROWS)
+    size = count * ROWS
+    for index in range(out_ref.shape[1] // LOW):
+        here = slice(index * LOW, (index + 1) * LOW)
+        ids = ids_ref[:, here]
+        product = jnp.dot(table, one_hot_low(ids & (LOW - 1)), preferred_element_type=F32)
+        product = product[:size] + product[size : 2 * size] + product[2 * size :]
+        out_ref[:, here] = pick_high(product, ids >> 8, count)
+
+
+def pack_both(own, mesh_ids_ref, sub_ids_ref, to_mesh_ref, to_sub_ref):
+    parts = [stack_columns(part) for part in split_three(own)]
+    table = jnp.concatenate(parts, axis=0).astype(BF16)
+    pack_ghosts(table, mesh_ids_ref, to_mesh_ref)
+    pack_ghosts(table, sub_ids_ref, to_sub_ref)
+
+
+def pack_kernel(
+    coords_any, veloc_any, mesh_any, sub_any, own_ref, to_mesh_ref, to_sub_ref, coords_ref,
+    veloc_ref, mesh_ids_ref, sub_ids_ref, sems,
+):
+    sources = (coords_any, veloc_any, mesh_any, sub_any)
+    targets = (coords_ref, veloc_ref, mesh_ids_ref, sub_ids_ref)
+    copies = [
+        pltpu.make_async_copy(source, target, sems.at[index])
+        for index, (source, target) in enumerate(zip(sources, targets))
+    ]
+    for copy in copies:
+        copy.start()
+    for copy in copies:
+        copy.wait()
+    pad = jnp.zeros((ROWS - 6, coords_ref.shape[1]), F32)
+    own = jnp.concatenate([coords_ref[...], veloc_ref[...], pad], axis=0)
+    own_ref[...] = own
+    pack_both(own, mesh_ids_ref, sub_ids_ref, to_mesh_ref, to_sub_ref)
+
+
+def new_state(
     own_ref, force_ref, slave_ref, back_mesh_ref, back_sub_ref, mass_ref, mesh_ids_ref,
-    sub_ids_ref, new_ref, to_mesh_ref, to_sub_ref,
+    sub_ids_ref,
 ):
     count = own_ref.shape[1] // LOW
     extra = add_back(back_mesh_ref[...], mesh_ids_ref, count) + add_back(
         back_sub_ref[...], sub_ids_ref, count
     )
-    full = jnp.concatenate(
-        [extra[part * ROWS : (part + 1) * ROWS] for part in range(count)], axis=1
-    )
-    force = force_ref[0:3, :] + slave_ref[0:3, :] + (full[0:3] + full[3:6])
-    speed = own_ref[3:6, :] + TIME_STEP * force / mass_ref[...]
+    full = unstack(extra)
+    force = force_ref[0:3, :] + slave_ref[0:3, :] + full[0:3]
+    return own_ref[3:6, :] + TIME_STEP * force / mass_ref[...]
+
+
+def update_kernel(*refs):
+    own_ref, mesh_ids_ref, sub_ids_ref = refs[0], refs[6], refs[7]
+    new_ref, to_mesh_ref, to_sub_ref = refs[8:]
+    speed = new_state(*refs[:8])
     place = own_ref[0:3, :] + TIME_STEP * speed
     own = jnp.concatenate([place, speed, jnp.zeros((ROWS - 6, place.shape[1]), F32)], axis=0)
     new_ref[...] = own
-    if to_mesh_ref is not None:
-        pack_ghosts(own, mesh_ids_ref, to_mesh_ref)
-        pack_ghosts(own, sub_ids_ref, to_sub_ref)
+    pack_both(own, mesh_ids_ref, sub_ids_ref, to_mesh_ref, to_sub_ref)
 
 
 def last_kernel(*refs):
-    update_kernel(*refs, None, None)
+    refs[8][...] = new_state(*refs[:8])
 
 
 VM = pl.BlockSpec(memory_space=pltpu.VMEM)
 SM = pl.BlockSpec(memory_space=pltpu.SMEM)
 ANY = pl.BlockSpec(memory_space=pl.ANY)
+HBM = pl.BlockSpec(memory_space=pltpu.HBM)
 
 
 def call(kernel, outs, ins, scratch=(), flops=0):
@@ -567,7 +604,7 @@
         scratch_shapes=[
             pltpu.VMEM(shape, F32) if isinstance(shape, tuple) else shape for shape in scratch
         ],
-        compiler_params=pltpu.CompilerParams(vmem_limit_bytes=20 << 20),
+        compiler_params=pltpu.CompilerParams(vmem_limit_bytes=8 << 20),
         cost_estimate=pl.CostEstimate(flops=flops, bytes_accessed=1 << 20, transcendentals=0),
     )
 
@@ -593,26 +630,48 @@
     slots = send_pick.shape[1]
     per_peer = slots // peers
     blocks = elems // SEG
-    conn = connect.reshape(4, blocks, SEG).transpose(1, 0, 2).reshape(4 * elems // LOW, LOW)
-    mesh_ids = send_mesh.reshape(ghost_mesh // LOW, LOW)
-    sub_ids = send_sub.reshape(ghost_sub // LOW, LOW)
+    mesh_ids = send_mesh.reshape(1, ghost_mesh)
+    sub_ids = send_sub.reshape(1, ghost_sub)
     mass = node_mass.reshape(1, nodes)
     stress_now = stress.reshape(3, blocks, SEG)
-    own = jnp.concatenate([coords, veloc, jnp.zeros((ROWS - 6, nodes), F32)], axis=0)
+    conn = connect
 
     chunks = nodes // SEG
     ghost_chunks = (ghost_mesh + ghost_sub) // SEG
     cands = bucket_list.shape[1]
 
-    pack = call(pack_kernel, [(ROWS, ghost_mesh), (ROWS, ghost_sub)], [VM] * 3)
+    pack = call(
+        pack_kernel,
+        [
+            (ROWS, nodes),
+            (ROWS, ghost_mesh),
+            (ROWS, ghost_sub),
+        ],
+        [HBM] * 4,
+        [
+            (3, nodes),
+            (3, nodes),
+            pltpu.VMEM((1, ghost_mesh), jnp.int32),
+            pltpu.VMEM((1, ghost_sub), jnp.int32),
+            pltpu.SemaphoreType.DMA((4,)),
+        ],
+    )
     own_rows_of = call(
         own_rows_kernel, [(2 * blocks * ROWS, SEG)], [VM] * 2, [(chunks, ROWS, SEG)], flops=1 << 31
     )
+    by_slot = slots <= blocks
     geom = lambda step: call(
-        functools.partial(geometry_kernel, step, nodes),
-        [(12, blocks, SEG), (blocks * ROWS, SEG)] + [(slots * ROWS, SEG)] * 2,
+        functools.partial(
+            geometry_slots_kernel if by_slot else geometry_blocks_kernel, step, nodes
+        ),
+        [
+            (12, blocks, SEG),
+            (slots * ROWS if by_slot else blocks * ROWS, SEG),
+            (peers, pl.cdiv(per_peer * SENT, 4), 4, SEG),
+        ],
         [ANY] + [VM] * 4,
-        [
+        ([(blocks * ROWS, SEG)] if by_slot else [])
+        + [
             (2 * blocks * ROWS, SEG),
             (ghost_chunks, ROWS, SEG),
             pltpu.SMEM(send_pick.shape, jnp.int32),
@@ -656,31 +715,34 @@
         functools.partial(react_own_kernel, step), [(ROWS, nodes)], [VM] * 4, flops=1 << 30
     )
     update = call(update_kernel, [(ROWS, nodes), (ROWS, ghost_mesh), (ROWS, ghost_sub)], [VM] * 8)
-    finish = call(last_kernel, [(ROWS, nodes)], [VM] * 8)
-
-    by_slot = slots <= blocks
+    finish = call(last_kernel, [(3, nodes)], [VM] * 8)
+
     pick_tiles = call(
         pick_kernel,
-        [jax.ShapeDtypeStruct((STEPS, slots * 2, LOW), jnp.int32)],
+        [jax.ShapeDtypeStruct((STEPS, slots, 4, SEG), jnp.int32)],
         [SM, VM],
         flops=1 << 20,
     )
     collect = lambda step: call(functools.partial(collect_kernel, step), [(blocks, SEG)], [SM, VM])
 
-    to_mesh, to_sub = pack(own, mesh_ids, sub_ids)
-    tiles = pick_tiles(send_pick, conn)[0] if by_slot else conn[None]
+    own, to_mesh, to_sub = pack(
+        *[pltpu.with_memory_space_constraint(x, pltpu.HBM) for x in (coords, veloc, mesh_ids, sub_ids)]
+    )
+    if by_slot:
+        (tiles,) = pick_tiles(send_pick, conn)
+    else:
+        tiles = conn.reshape(4, blocks, SEG).transpose(1, 0, 2)[None]
     for step in range(STEPS):
         from_mesh = shifted(to_mesh, "mesh", 1)
         from_sub = shifted(to_sub, "sub", 1)
         (own_rows,) = own_rows_of(own, conn)
         (node,) = features(step)(own, pair_mask)
-        corner, geo, outgoing, kept = geom(step)(
+        corner, kept, outgoing = geom(step)(
             send_pick, from_mesh, from_sub, conn, own_rows
         )
         incoming = lax.all_to_all(
-            outgoing.reshape(peers, per_peer * ROWS, SEG),
-            "mesh", split_axis=0, concat_axis=0, tiled=True,
-        ).reshape(slots * ROWS, SEG)
+            outgoing, "mesh", split_axis=0, concat_axis=0, tiled=True
+        )
         pushes, stress_now = forces(own, from_mesh, from_sub, conn, corner, stress_now)
         slave, react = contact(step)(bucket_list, node, incoming)
         returned = lax.all_to_all(
@@ -688,11 +750,11 @@
             "mesh", split_axis=0, concat_axis=0, tiled=True,
         ).reshape(slots, SEG)
         (acc,) = internal_of(pushes, conn)
+        at = step if by_slot else 0
         if by_slot:
             rows = (kept, returned, tiles, acc)
         else:
-            rows = (geo, collect(step)(send_pick, returned)[0], tiles, acc)
-        at = step if by_slot else 0
+            rows = (kept, collect(step)(send_pick, returned)[0], tiles, acc)
         back_mesh, back_sub = react_ghost(at)(*rows)
         (force,) = react_own(at)(*rows)
         back_mesh = shifted(back_mesh, "mesh", -1)
@@ -702,7 +764,7 @@
             own, to_mesh, to_sub = update(*args)
         else:
             (own,) = finish(*args)
-    return own[3:6], stress_now.reshape(3, elems)
+    return own, stress_now.reshape(3, elems)
 
 
 def solution(mesh):

time: 164 us -> 163 us (level)
  starting transfers between devices: 42.9 us -> 46.7 us
  Pallas kernels: 82.2 us -> 78.6 us
    ppermute x16, waiting for transfers between devices: 7.77 us -> 11.6 us  [shifted(): return lax.ppermute(value, axis, pairs)]
    all_to_all x4, waiting for transfers between devices: 11.9 us -> 8.14 us  [per_device(): lax.all_to_all(react.reshape(peers, per_peer, SEG), 'mesh', split_axis=0,...]
    pallas_call x4, Pallas kernels: 13.2 us -> 16.8 us  [per_device(): acc, = internal_of(pushes, conn)]
    ppermute x16, starting transfers between devices: 14.5 us -> 17.9 us  [shifted(): return lax.ppermute(value, axis, pairs)]
    pallas_call x4, Pallas kernels: 17.4 us -> 14.3 us  [per_device(): slave, react = contact(step)(bucket_list, node, incoming)]
    pallas_call x4, Pallas kernels: 15.3 us -> 12.9 us  [per_device(): forces(own, from_mesh, from_sub, conn, corner, stress_now)]
    reshape x3 -> x0, local copies, waits for them, and re-layouts: 2.26 us -> none  [the longest x1 0.87 us: per_device(): connect.reshape(4, blocks, SEG).transpose(1, 0, 2)]
    pallas_call x4, Pallas kernels: 5.86 us -> 4.12 us  [per_device(): back_mesh, back_sub = react_ghost(at)(*rows)]
  transfers between devices with their start and end apart: 24 -> 24, of which waited for: 14 -> 11; matrix products, arithmetic and copies ran while one was open for 1% -> 0% of each run, Pallas kernels for 30% -> 27%
where the time goes in v1:
time: 163 us; the launch traced here: 162 us
  Pallas kernels  78.6 us (48%)
  starting transfers between devices  46.7 us (29%)
  waiting for transfers between devices  33.1 us (20%)
  local copies, waits for them, and re-layouts  2.16 us (1%)
    ppermute x16, starting transfers between devices, shifted(): return lax.ppermute(value, axis, pairs)  17.9 us
    pallas_call x4, Pallas kernels, per_device(): acc, = internal_of(pushes, conn)  16.8 us
    all_to_all x4, starting transfers between devices, per_device(): lax.all_to_all(outgoing, 'mesh', split_axis=0, concat_axis=0, tiled=True)  15.2 us
    pallas_call x4, Pallas kernels, per_device(): slave, react = contact(step)(bucket_list, node, incoming)  14.3 us
    all_to_all x4, starting transfers between devices, per_device(): lax.all_to_all(react.reshape(peers, per_peer, SEG), 'mesh', split_axis=0,...  13.6 us
    all_to_all x4, waiting for transfers between devices, per_device(): lax.all_to_all(outgoing, 'mesh', split_axis=0, concat_axis=0, tiled=True)  13.3 us
    pallas_call x4, Pallas kernels, per_device(): forces(own, from_mesh, from_sub, conn, corner, stress_now)  12.9 us
    ppermute x16, waiting for transfers between devices, shifted(): return lax.ppermute(value, axis, pairs)  11.6 us
  transfers between devices with their start and end apart: 24, of which 11 were waited for; matrix products, arithmetic and copies ran while one was open for 0% of the time, Pallas kernels for 27%

profile of v1, /device:TPU:0, one launch (start us, length us, event | category | flops | bytes accessed | tf_op | source)
XLA Modules:
  0.0 161.6 jit_solution(11311225252511298348)
XLA Ops:
  0.6 1.1 shard_map.113
  1.7 3.0 %collective-permute-start = (f32[8,512]{1,0:T(8,128)S(1)}, f32[8,512]{1,0:T(8,128)S(1)}, u32[]{:S(2)}, u32[]{:S(2)}) collective-permute-start(f32[8,512]{1,0:T(8,128)S(1)} %get-tuple-element.51), channel_id=1, source_target_pairs={{0,4},{4,8},{8,12},{12,16},{16,20},{20,24},{24,28},{28,0},{1,5},{5... | collective-permute-start | bytes 49160 | tf_op jit(solution)/shard_map/ppermute | solution.py:34
  4.8 0.8 copy-done.1
  5.6 1.9 %shard_map.114.refs_4_ = f32[512,128]{1,0:T(8,128)S(1)} custom-call(f32[8,2048]{1,0:T(8,128)S(1)} %get-tuple-element.50.own_ref.refs_0_, s32[4,4096]{1,0:T(4,128)S(1)} %copy-done.1), custom_call_target="tpu_custom_call" | custom-call | flops 2147483648 | bytes 1048576 | tf_op jit(solution)/shard_map/pallas_call | solution.py:738
  7.5 1.2 shard_map.116.node_ref
  8.7 0.8 shard_map.118.tiles_ref
  9.5 1.6 %shard_map.115 = (f32[12,32,128]{2,1,0:T(8,128)S(1)}, f32[128,128]{1,0:T(8,128)S(1)}, f32[8,3,4,128]{3,2,1,0:T(4,128)}) custom-call(s32[4,16]{1,0:T(4,128)S(1)} %copy-done.5, f32[8,512]{1,0:T(8,128)S(1)} %collective-permute-done.refs_1_.mesh_ref, f32[8,512]{1,0:T(8,128)S(1)} %collective-permute-done.1.refs_2_.sub_ref, s32[4,4096]{1,0:T(4,128)S(1)} %copy-done.2, ...), custom_call_target="tpu_custom_call" | custom-call | flops 1073741824 | bytes 1048576 | tf_op jit(solution)/shard_map/pallas_call | solution.py:740
  11.2 4.9 %all-to-all-start = ((f32[8,3,4,128]{3,2,1,0:T(4,128)}), f32[8,3,4,128]{3,2,1,0:T(4,128)S(1)}, u32[]{:S(2)}, u32[]{:S(2)}) async-start(f32[8,3,4,128]{3,2,1,0:T(4,128)} %get-tuple-element.54), calls=%async_computation | async-start | bytes 98304 | tf_op jit(solution)/shard_map/all_to_all | solution.py:743
  16.1 3.2 %shard_map.119 = (f32[1024,128]{1,0:T(8,128)S(1)}, f32[3,32,128]{2,1,0:T(8,128)S(1)}) custom-call(f32[8,2048]{1,0:T(8,128)S(1)} %get-tuple-element.50.own_ref.refs_0_, f32[8,512]{1,0:T(8,128)S(1)} %collective-permute-done.refs_1_.mesh_ref, f32[8,512]{1,0:T(8,128)S(1)} %collective-permute-done.1.refs_2_.sub_ref, s32[4,4096]{1,0:T(4,128)S(1)} %copy-done.2, ...), custom_call_target="tpu_custom_call" | custom-call | flops 2147483648 | bytes 1048576 | tf_op jit(solution)/shard_map/pallas_call | solution.py:746
  19.3 3.6 %all-to-all-done.slots_ref = f32[8,3,4,128]{3,2,1,0:T(4,128)S(1)} async-done(((f32[8,3,4,128]{3,2,1,0:T(4,128)}), f32[8,3,4,128]{3,2,1,0:T(4,128)S(1)}, u32[]{:S(2)}, u32[]{:S(2)}) %all-to-all-start) | async-done | bytes 49184 | tf_op jit(solution)/shard_map/all_to_all | solution.py:743
  22.9 3.6 %shard_map.117 = (f32[8,2048]{1,0:T(8,128)S(1)}, f32[16,128]{1,0:T(8,128)}) custom-call(s32[4,4,16]{2,1,0:T(4,128)S(1)} %copy-done.7, bf16[4,2048,128]{2,1,0:T(8,128)(2,1)S(1)} %shard_map.116.node_ref, f32[8,3,4,128]{3,2,1,0:T(4,128)S(1)} %all-to-all-done.slots_ref), custom_call_target="tpu_custom_call" | custom-call | flops 2147483648 | bytes 1048576 | tf_op jit(solution)/shard_map/pallas_call | solution.py:747
  26.5 3.3 %all-to-all-start.1 = ((f32[8,2,128]{2,1,0:T(2,128)}), f32[8,2,128]{2,1,0:T(2,128)S(1)}, u32[]{:S(2)}, u32[]{:S(2)}) async-start(f32[8,2,128]{2,1,0:T(2,128)} %bitcast.2), calls=%async_computation.1 | async-start | bytes 16384 | tf_op jit(solution)/shard_map/all_to_all | solution.py:748
  29.8 4.2 %shard_map.120.acc_ref = f32[96,256]{1,0:T(8,128)S(1)} custom-call(f32[1024,128]{1,0:T(8,128)S(1)} %get-tuple-element.57.rows_ref, s32[4,4096]{1,0:T(4,128)S(1)} %copy-done.2), custom_call_target="tpu_custom_call" | custom-call | flops 2147483648 | bytes 1048576 | tf_op jit(solution)/shard_map/pallas_call | solution.py:752
  34.0 2.3 %all-to-all-done.1 = f32[8,2,128]{2,1,0:T(2,128)S(1)} async-done(((f32[8,2,128]{2,1,0:T(2,128)}), f32[8,2,128]{2,1,0:T(2,128)S(1)}, u32[]{:S(2)}, u32[]{:S(2)}) %all-to-all-start.1) | async-done | bytes 8224 | tf_op jit(solution)/shard_map/all_to_all | solution.py:748
  36.3 1.0 shard_map.122
  37.4 2.5 %collective-permute-start.2 = (f32[8,512]{1,0:T(8,128)S(1)}, f32[8,512]{1,0:T(8,128)S(1)}, u32[]{:S(2)}, u32[]{:S(2)}) collective-permute-start(f32[8,512]{1,0:T(8,128)S(1)} %get-tuple-element.59), channel_id=1, source_target_pairs={{0,28},{4,0},{8,4},{12,8},{16,12},{20,16},{24,20},{28,24},{1,29},{... | collective-permute-start | bytes 49160 | tf_op jit(solution)/shard_map/ppermute | solution.py:34
  39.8 1.7 %shard_map.121.refs_1_ = f32[8,2048]{1,0:T(8,128)S(1)} custom-call(f32[128,128]{1,0:T(8,128)S(1)} %get-tuple-element.53.blocks_ref, f32[16,128]{1,0:T(8,128)S(1)} %bitcast.38, s32[4,16,4,128]{3,2,1,0:T(4,128)S(1)} %shard_map.118.tiles_ref, f32[96,256]{1,0:T(8,128)S(1)} %shard_map.120.acc_ref), custom_call_target="tpu_custom_call" | custom-call | flops 1073741824 | bytes 1048576 | tf_op jit(solution)/shard_map/pallas_call | solution.py:759
  41.5 0.7 shard_map.123
  42.3 1.9 %shard_map.124.refs_4_ = f32[512,128]{1,0:T(8,128)S(1)} custom-call(f32[8,2048]{1,0:T(8,128)S(1)} %get-tuple-element.61.own_ref.refs_0_, s32[4,4096]{1,0:T(4,128)S(1)} %copy-done.2), custom_call_target="tpu_custom_call" | custom-call | flops 2147483648 | bytes 1048576 | tf_op jit(solution)/shard_map/pallas_call | solution.py:738
  44.2 1.1 collective-permute-start.4
  45.6 1.2 shard_map.126.node_ref
  46.8 3.9 %collective-permute-done.4.refs_1_.mesh_ref = f32[8,512]{1,0:T(8,128)S(1)} collective-permute-done((f32[8,512]{1,0:T(8,128)S(1)}, f32[8,512]{1,0:T(8,128)S(1)}, u32[]{:S(2)}, u32[]{:S(2)}) %collective-permute-start.4) | collective-permute-done | bytes 16416 | tf_op jit(solution)/shard_map/ppermute | solution.py:34
  50.7 1.6 %shard_map.125 = (f32[12,32,128]{2,1,0:T(8,128)S(1)}, f32[128,128]{1,0:T(8,128)S(1)}, f32[8,3,4,128]{3,2,1,0:T(4,128)}) custom-call(s32[4,16]{1,0:T(4,128)S(1)} %copy-done.5, f32[8,512]{1,0:T(8,128)S(1)} %collective-permute-done.4.refs_1_.mesh_ref, f32[8,512]{1,0:T(8,128)S(1)} %collective-permute-done.5.refs_2_.sub_ref, s32[4,4096]{1,0:T(4,128)S(1)} %copy-done.2, ...), custom_call_target="tpu_custom_call" | custom-call | flops 1073741824 | bytes 1048576 | tf_op jit(solution)/shard_map/pallas_call | solution.py:740
  52.3 3.5 %all-to-all-start.2 = ((f32[8,3,4,128]{3,2,1,0:T(4,128)}), f32[8,3,4,128]{3,2,1,0:T(4,128)S(1)}, u32[]{:S(2)}, u32[]{:S(2)}) async-start(f32[8,3,4,128]{3,2,1,0:T(4,128)} %get-tuple-element.65), calls=%async_computation.2 | async-start | bytes 98304 | tf_op jit(solution)/shard_map/all_to_all | solution.py:743
  55.9 3.2 %shard_map.128 = (f32[1024,128]{1,0:T(8,128)S(1)}, f32[3,32,128]{2,1,0:T(8,128)S(1)}) custom-call(f32[8,2048]{1,0:T(8,128)S(1)} %get-tuple-element.61.own_ref.refs_0_, f32[8,512]{1,0:T(8,128)S(1)} %collective-permute-done.4.refs_1_.mesh_ref, f32[8,512]{1,0:T(8,128)S(1)} %collective-permute-done.5.refs_2_.sub_ref, s32[4,4096]{1,0:T(4,128)S(1)} %copy-done.2, ...), custom_call_target="tpu_custom_call" | custom-call | flops 2147483648 | bytes 1048576 | tf_op jit(solution)/shard_map/pallas_call | solution.py:746
  59.7 2.7 %all-to-all-done.2.slots_ref = f32[8,3,4,128]{3,2,1,0:T(4,128)S(1)} async-done(((f32[8,3,4,128]{3,2,1,0:T(4,128)}), f32[8,3,4,128]{3,2,1,0:T(4,128)S(1)}, u32[]{:S(2)}, u32[]{:S(2)}) %all-to-all-start.2) | async-done | bytes 49184 | tf_op jit(solution)/shard_map/all_to_all | solution.py:743
  62.4 3.6 %shard_map.127 = (f32[8,2048]{1,0:T(8,128)S(1)}, f32[16,128]{1,0:T(8,128)}) custom-call(s32[4,4,16]{2,1,0:T(4,128)S(1)} %copy-done.7, bf16[4,2048,128]{2,1,0:T(8,128)(2,1)S(1)} %shard_map.126.node_ref, f32[8,3,4,128]{3,2,1,0:T(4,128)S(1)} %all-to-all-done.2.slots_ref), custom_call_target="tpu_custom_call" | custom-call | flops 2147483648 | bytes 1048576 | tf_op jit(solution)/shard_map/pallas_call | solution.py:747
  66.0 3.3 %all-to-all-start.3 = ((f32[8,2,128]{2,1,0:T(2,128)}), f32[8,2,128]{2,1,0:T(2,128)S(1)}, u32[]{:S(2)}, u32[]{:S(2)}) async-start(f32[8,2,128]{2,1,0:T(2,128)} %bitcast.5), calls=%async_computation.3 | async-start | bytes 16384 | tf_op jit(solution)/shard_map/all_to_all | solution.py:748
  69.4 4.2 %shard_map.129.acc_ref = f32[96,256]{1,0:T(8,128)S(1)} custom-call(f32[1024,128]{1,0:T(8,128)S(1)} %get-tuple-element.69.rows_ref, s32[4,4096]{1,0:T(4,128)S(1)} %copy-done.2), custom_call_target="tpu_custom_call" | custom-call | flops 2147483648 | bytes 1048576 | tf_op jit(solution)/shard_map/pallas_call | solution.py:752
  73.6 2.3 %all-to-all-done.3 = f32[8,2,128]{2,1,0:T(2,128)S(1)} async-done(((f32[8,2,128]{2,1,0:T(2,128)}), f32[8,2,128]{2,1,0:T(2,128)S(1)}, u32[]{:S(2)}, u32[]{:S(2)}) %all-to-all-start.3) | async-done | bytes 8224 | tf_op jit(solution)/shard_map/all_to_all | solution.py:748
  75.8 1.0 shard_map.131
  76.9 2.5 %collective-permute-start.6 = (f32[8,512]{1,0:T(8,128)S(1)}, f32[8,512]{1,0:T(8,128)S(1)}, u32[]{:S(2)}, u32[]{:S(2)}) collective-permute-start(f32[8,512]{1,0:T(8,128)S(1)} %get-tuple-element.71), channel_id=1, source_target_pairs={{0,28},{4,0},{8,4},{12,8},{16,12},{20,16},{24,20},{28,24},{1,29},{... | collective-permute-start | bytes 49160 | tf_op jit(solution)/shard_map/ppermute | solution.py:34
  79.3 1.7 %shard_map.130.refs_1_ = f32[8,2048]{1,0:T(8,128)S(1)} custom-call(f32[128,128]{1,0:T(8,128)S(1)} %get-tuple-element.64.blocks_ref, f32[16,128]{1,0:T(8,128)S(1)} %bitcast.40, s32[4,16,4,128]{3,2,1,0:T(4,128)S(1)} %shard_map.118.tiles_ref, f32[96,256]{1,0:T(8,128)S(1)} %shard_map.129.acc_ref), custom_call_target="tpu_custom_call" | custom-call | flops 1073741824 | bytes 1048576 | tf_op jit(solution)/shard_map/pallas_call | solution.py:759
  81.8 1.9 %shard_map.133.refs_4_ = f32[512,128]{1,0:T(8,128)S(1)} custom-call(f32[8,2048]{1,0:T(8,128)S(1)} %get-tuple-element.73.own_ref.refs_0_, s32[4,4096]{1,0:T(4,128)S(1)} %copy-done.2), custom_call_target="tpu_custom_call" | custom-call | flops 2147483648 | bytes 1048576 | tf_op jit(solution)/shard_map/pallas_call | solution.py:738
  83.6 1.1 collective-permute-start.8
  85.1 1.2 shard_map.135.node_ref
  86.3 3.9 %collective-permute-done.8.refs_1_.mesh_ref = f32[8,512]{1,0:T(8,128)S(1)} collective-permute-done((f32[8,512]{1,0:T(8,128)S(1)}, f32[8,512]{1,0:T(8,128)S(1)}, u32[]{:S(2)}, u32[]{:S(2)}) %collective-permute-start.8) | collective-permute-done | bytes 16416 | tf_op jit(solution)/shard_map/ppermute | solution.py:34
  90.2 1.6 %shard_map.134 = (f32[12,32,128]{2,1,0:T(8,128)S(1)}, f32[128,128]{1,0:T(8,128)S(1)}, f32[8,3,4,128]{3,2,1,0:T(4,128)}) custom-call(s32[4,16]{1,0:T(4,128)S(1)} %copy-done.5, f32[8,512]{1,0:T(8,128)S(1)} %collective-permute-done.8.refs_1_.mesh_ref, f32[8,512]{1,0:T(8,128)S(1)} %collective-permute-done.9.refs_2_.sub_ref, s32[4,4096]{1,0:T(4,128)S(1)} %copy-done.2, ...), custom_call_target="tpu_custom_call" | custom-call | flops 1073741824 | bytes 1048576 | tf_op jit(solution)/shard_map/pallas_call | solution.py:740
  91.8 3.4 %all-to-all-start.4 = ((f32[8,3,4,128]{3,2,1,0:T(4,128)}), f32[8,3,4,128]{3,2,1,0:T(4,128)S(1)}, u32[]{:S(2)}, u32[]{:S(2)}) async-start(f32[8,3,4,128]{3,2,1,0:T(4,128)} %get-tuple-element.77), calls=%async_computation.4 | async-start | bytes 98304 | tf_op jit(solution)/shard_map/all_to_all | solution.py:743
  95.2 3.2 %shard_map.137 = (f32[1024,128]{1,0:T(8,128)S(1)}, f32[3,32,128]{2,1,0:T(8,128)S(1)}) custom-call(f32[8,2048]{1,0:T(8,128)S(1)} %get-tuple-element.73.own_ref.refs_0_, f32[8,512]{1,0:T(8,128)S(1)} %collective-permute-done.8.refs_1_.mesh_ref, f32[8,512]{1,0:T(8,128)S(1)} %collective-permute-done.9.refs_2_.sub_ref, s32[4,4096]{1,0:T(4,128)S(1)} %copy-done.2, ...), custom_call_target="tpu_custom_call" | custom-call | flops 2147483648 | bytes 1048576 | tf_op jit(solution)/shard_map/pallas_call | solution.py:746
  98.4 3.5 %all-to-all-done.4.slots_ref = f32[8,3,4,128]{3,2,1,0:T(4,128)S(1)} async-done(((f32[8,3,4,128]{3,2,1,0:T(4,128)}), f32[8,3,4,128]{3,2,1,0:T(4,128)S(1)}, u32[]{:S(2)}, u32[]{:S(2)}) %all-to-all-start.4) | async-done | bytes 49184 | tf_op jit(solution)/shard_map/all_to_all | solution.py:743
  101.9 3.6 %shard_map.136 = (f32[8,2048]{1,0:T(8,128)S(1)}, f32[16,128]{1,0:T(8,128)}) custom-call(s32[4,4,16]{2,1,0:T(4,128)S(1)} %copy-done.7, bf16[4,2048,128]{2,1,0:T(8,128)(2,1)S(1)} %shard_map.135.node_ref, f32[8,3,4,128]{3,2,1,0:T(4,128)S(1)} %all-to-all-done.4.slots_ref), custom_call_target="tpu_custom_call" | custom-call | flops 2147483648 | bytes 1048576 | tf_op jit(solution)/shard_map/pallas_call | solution.py:747
  105.5 3.6 %all-to-all-start.5 = ((f32[8,2,128]{2,1,0:T(2,128)}), f32[8,2,128]{2,1,0:T(2,128)S(1)}, u32[]{:S(2)}, u32[]{:S(2)}) async-start(f32[8,2,128]{2,1,0:T(2,128)} %bitcast.7), calls=%async_computation.5 | async-start | bytes 16384 | tf_op jit(solution)/shard_map/all_to_all | solution.py:748
  109.1 4.2 %shard_map.138.acc_ref = f32[96,256]{1,0:T(8,128)S(1)} custom-call(f32[1024,128]{1,0:T(8,128)S(1)} %get-tuple-element.81.rows_ref, s32[4,4096]{1,0:T(4,128)S(1)} %copy-done.2), custom_call_target="tpu_custom_call" | custom-call | flops 2147483648 | bytes 1048576 | tf_op jit(solution)/shard_map/pallas_call | solution.py:752
  113.3 2.0 %all-to-all-done.5 = f32[8,2,128]{2,1,0:T(2,128)S(1)} async-done(((f32[8,2,128]{2,1,0:T(2,128)}), f32[8,2,128]{2,1,0:T(2,128)S(1)}, u32[]{:S(2)}, u32[]{:S(2)}) %all-to-all-start.5) | async-done | bytes 8224 | tf_op jit(solution)/shard_map/all_to_all | solution.py:748
  115.3 1.0 shard_map.140
  116.4 2.5 %collective-permute-start.10 = (f32[8,512]{1,0:T(8,128)S(1)}, f32[8,512]{1,0:T(8,128)S(1)}, u32[]{:S(2)}, u32[]{:S(2)}) collective-permute-start(f32[8,512]{1,0:T(8,128)S(1)} %get-tuple-element.83), channel_id=1, source_target_pairs={{0,28},{4,0},{8,4},{12,8},{16,12},{20,16},{24,20},{28,24},{1,29},{... | collective-permute-start | bytes 49160 | tf_op jit(solution)/shard_map/ppermute | solution.py:34
  118.8 1.7 %shard_map.139.refs_1_ = f32[8,2048]{1,0:T(8,128)S(1)} custom-call(f32[128,128]{1,0:T(8,128)S(1)} %get-tuple-element.76.blocks_ref, f32[16,128]{1,0:T(8,128)S(1)} %bitcast.42, s32[4,16,4,128]{3,2,1,0:T(4,128)S(1)} %shard_map.118.tiles_ref, f32[96,256]{1,0:T(8,128)S(1)} %shard_map.138.acc_ref), custom_call_target="tpu_custom_call" | custom-call | flops 1073741824 | bytes 1048576 | tf_op jit(solution)/shard_map/pallas_call | solution.py:759
  121.3 1.9 %shard_map.142.refs_4_ = f32[512,128]{1,0:T(8,128)S(1)} custom-call(f32[8,2048]{1,0:T(8,128)S(1)} %get-tuple-element.85.own_ref.refs_0_, s32[4,4096]{1,0:T(4,128)S(1)} %copy-done.2), custom_call_target="tpu_custom_call" | custom-call | flops 2147483648 | bytes 1048576 | tf_op jit(solution)/shard_map/pallas_call | solution.py:738
  123.1 1.1 collective-permute-start.12
  124.6 1.2 shard_map.144.node_ref
  125.8 3.9 %collective-permute-done.12.refs_1_.mesh_ref = f32[8,512]{1,0:T(8,128)S(1)} collective-permute-done((f32[8,512]{1,0:T(8,128)S(1)}, f32[8,512]{1,0:T(8,128)S(1)}, u32[]{:S(2)}, u32[]{:S(2)}) %collective-permute-start.12) | collective-permute-done | bytes 16416 | tf_op jit(solution)/shard_map/ppermute | solution.py:34
  129.6 1.6 %shard_map.143 = (f32[12,32,128]{2,1,0:T(8,128)S(1)}, f32[128,128]{1,0:T(8,128)S(1)}, f32[8,3,4,128]{3,2,1,0:T(4,128)}) custom-call(s32[4,16]{1,0:T(4,128)S(1)} %copy-done.5, f32[8,512]{1,0:T(8,128)S(1)} %collective-permute-done.12.refs_1_.mesh_ref, f32[8,512]{1,0:T(8,128)S(1)} %collective-permute-done.13.refs_2_.sub_ref, s32[4,4096]{1,0:T(4,128)S(1)} %copy-done.2, ...), custom_call_target="tpu_custom_call" | custom-call | flops 1073741824 | bytes 1048576 | tf_op jit(solution)/shard_map/pallas_call | solution.py:740
  131.3 3.4 %all-to-all-start.6 = ((f32[8,3,4,128]{3,2,1,0:T(4,128)}), f32[8,3,4,128]{3,2,1,0:T(4,128)S(1)}, u32[]{:S(2)}, u32[]{:S(2)}) async-start(f32[8,3,4,128]{3,2,1,0:T(4,128)} %get-tuple-element.89), calls=%async_computation.6 | async-start | bytes 98304 | tf_op jit(solution)/shard_map/all_to_all | solution.py:743
  134.7 3.2 %shard_map.146 = (f32[1024,128]{1,0:T(8,128)S(1)}, f32[3,32,128]{2,1,0:T(8,128)S(1)}) custom-call(f32[8,2048]{1,0:T(8,128)S(1)} %get-tuple-element.85.own_ref.refs_0_, f32[8,512]{1,0:T(8,128)S(1)} %collective-permute-done.12.refs_1_.mesh_ref, f32[8,512]{1,0:T(8,128)S(1)} %collective-permute-done.13.refs_2_.sub_ref, s32[4,4096]{1,0:T(4,128)S(1)} %copy-done.2, ...), custom_call_target="tpu_custom_call" | custom-call | flops 2147483648 | bytes 1048576 | tf_op jit(solution)/shard_map/pallas_call | solution.py:746
  137.9 3.5 %all-to-all-done.6.slots_ref = f32[8,3,4,128]{3,2,1,0:T(4,128)S(1)} async-done(((f32[8,3,4,128]{3,2,1,0:T(4,128)}), f32[8,3,4,128]{3,2,1,0:T(4,128)S(1)}, u32[]{:S(2)}, u32[]{:S(2)}) %all-to-all-start.6) | async-done | bytes 49184 | tf_op jit(solution)/shard_map/all_to_all | solution.py:743
  141.4 3.6 %shard_map.145 = (f32[8,2048]{1,0:T(8,128)S(1)}, f32[16,128]{1,0:T(8,128)}) custom-call(s32[4,4,16]{2,1,0:T(4,128)S(1)} %copy-done.7, bf16[4,2048,128]{2,1,0:T(8,128)(2,1)S(1)} %shard_map.144.node_ref, f32[8,3,4,128]{3,2,1,0:T(4,128)S(1)} %all-to-all-done.6.slots_ref), custom_call_target="tpu_custom_call" | custom-call | flops 2147483648 | bytes 1048576 | tf_op jit(solution)/shard_map/pallas_call | solution.py:747
  145.0 3.3 %all-to-all-start.7 = ((f32[8,2,128]{2,1,0:T(2,128)}), f32[8,2,128]{2,1,0:T(2,128)S(1)}, u32[]{:S(2)}, u32[]{:S(2)}) async-start(f32[8,2,128]{2,1,0:T(2,128)} %bitcast.9), calls=%async_computation.7 | async-start | bytes 16384 | tf_op jit(solution)/shard_map/all_to_all | solution.py:748
  148.3 4.2 %shard_map.147.acc_ref = f32[96,256]{1,0:T(8,128)S(1)} custom-call(f32[1024,128]{1,0:T(8,128)S(1)} %get-tuple-element.93.rows_ref, s32[4,4096]{1,0:T(4,128)S(1)} %copy-done.2), custom_call_target="tpu_custom_call" | custom-call | flops 2147483648 | bytes 1048576 | tf_op jit(solution)/shard_map/pallas_call | solution.py:752
  153.2 1.6 all-to-all-done.7
  154.8 1.0 shard_map.149
  155.8 3.1 %collective-permute-start.14 = (f32[8,512]{1,0:T(8,128)S(1)}, f32[8,512]{1,0:T(8,128)S(1)}, u32[]{:S(2)}, u32[]{:S(2)}) collective-permute-start(f32[8,512]{1,0:T(8,128)S(1)} %get-tuple-element.95), channel_id=1, source_target_pairs={{0,28},{4,0},{8,4},{12,8},{16,12},{20,16},{24,20},{28,24},{1,29},{... | collective-permute-start | bytes 49160 | tf_op jit(solution)/shard_map/ppermute | solution.py:34
  159.0 1.7 %shard_map.148.refs_1_ = f32[8,2048]{1,0:T(8,128)S(1)} custom-call(f32[128,128]{1,0:T(8,128)S(1)} %get-tuple-element.88.blocks_ref, f32[16,128]{1,0:T(8,128)S(1)} %bitcast.36, s32[4,16,4,128]{3,2,1,0:T(4,128)S(1)} %shard_map.118.tiles_ref, f32[96,256]{1,0:T(8,128)S(1)} %shard_map.147.acc_ref), custom_call_target="tpu_custom_call" | custom-call | flops 1073741824 | bytes 1048576 | tf_op jit(solution)/shard_map/pallas_call | solution.py:759
  160.7 1.0 shard_map.150
  (46 shorter events, 3.9 us)
Async XLA Ops:
  1.7 7.8 %collective-permute-start = (f32[8,512]{1,0:T(8,128)S(1)}, f32[8,512]{1,0:T(8,128)S(1)}, u32[]{:S(2)}, u32[]{:S(2)}) collective-permute-start(f32[8,512]{1,0:T(8,128)S(1)} %get-tuple-element.51), channel_id=1, source_target_pairs={{0,4},{4,8},{8,12},{12,16},{16,20},{20,24},{24,28},{28,0},{1,5},{5... | collective-permute-start | bytes 49160 | tf_op jit(solution)/shard_map/ppermute | solution.py:34
  4.8 4.8 %collective-permute-start.1 = (f32[8,512]{1,0:T(8,128)S(1)}, f32[8,512]{1,0:T(8,128)S(1)}, u32[]{:S(2)}, u32[]{:S(2)}) collective-permute-start(f32[8,512]{1,0:T(8,128)S(1)} %get-tuple-element.52), channel_id=1, source_target_pairs={{0,1},{1,2},{2,3},{3,0},{4,5},{5,6},{6,7},{7,4},{8,9},{9,10},{10,1... | collective-permute-start | bytes 49160 | tf_op jit(solution)/shard_map/ppermute | solution.py:34
  4.8 0.8 copy-start.1
  5.6 1.9 %copy-start.6 = (s32[4,4,2048]{2,1,0:T(4,128)S(1)}, s32[4,4,2048]{2,1,0:T(4,128)}, u32[]{:S(2)}) copy-start(s32[4,4,2048]{2,1,0:T(4,128)} %mask_ref.7) | copy-start | bytes 393220
  7.5 1.2 copy-start.10
  7.5 1.2 copy-start.2
  7.5 1.2 copy-start.5
  11.2 11.7 %all-to-all-start = ((f32[8,3,4,128]{3,2,1,0:T(4,128)}), f32[8,3,4,128]{3,2,1,0:T(4,128)S(1)}, u32[]{:S(2)}, u32[]{:S(2)}) async-start(f32[8,3,4,128]{3,2,1,0:T(4,128)} %get-tuple-element.54), calls=%async_computation | async-start | bytes 98304 | tf_op jit(solution)/shard_map/all_to_all | solution.py:743
  16.1 6.8 %copy-start.7 = (s32[4,4,16]{2,1,0:T(4,128)S(1)}, s32[4,4,16]{2,1,0:T(4,128)}, u32[]{:S(2)}) copy-start(s32[4,4,16]{2,1,0:T(4,128)} %list_any.7) | copy-start | bytes 3076
  26.5 9.8 %all-to-all-start.1 = ((f32[8,2,128]{2,1,0:T(2,128)}), f32[8,2,128]{2,1,0:T(2,128)S(1)}, u32[]{:S(2)}, u32[]{:S(2)}) async-start(f32[8,2,128]{2,1,0:T(2,128)} %bitcast.2), calls=%async_computation.1 | async-start | bytes 16384 | tf_op jit(solution)/shard_map/all_to_all | solution.py:748
  37.3 4.2 %copy-start = (f32[2048]{0:T(1024)S(1)}, f32[2048]{0:T(1024)}, u32[]{:S(2)}) copy-start(f32[2048]{0:T(1024)} %param.12) | copy-start | bytes 24580
  37.3 4.2 %copy-start.3 = (s32[512]{0:T(512)S(1)}, s32[512]{0:T(512)}, u32[]{:S(2)}) copy-start(s32[512]{0:T(512)} %param.15) | copy-start | bytes 6148
  37.3 4.2 %copy-start.4 = (s32[512]{0:T(512)S(1)}, s32[512]{0:T(512)}, u32[]{:S(2)}) copy-start(s32[512]{0:T(512)} %param.16) | copy-start | bytes 6148
  37.4 4.1 %collective-permute-start.2 = (f32[8,512]{1,0:T(8,128)S(1)}, f32[8,512]{1,0:T(8,128)S(1)}, u32[]{:S(2)}, u32[]{:S(2)}) collective-permute-start(f32[8,512]{1,0:T(8,128)S(1)} %get-tuple-element.59), channel_id=1, source_target_pairs={{0,28},{4,0},{8,4},{12,8},{16,12},{20,16},{24,20},{28,24},{1,29},{... | collective-permute-start | bytes 49160 | tf_op jit(solution)/shard_map/ppermute | solution.py:34
  39.8 1.7 %collective-permute-start.3 = (f32[8,512]{1,0:T(8,128)S(1)}, f32[8,512]{1,0:T(8,128)S(1)}, u32[]{:S(2)}, u32[]{:S(2)}) collective-permute-start(f32[8,512]{1,0:T(8,128)S(1)} %get-tuple-element.60), channel_id=1, source_target_pairs={{0,3},{1,0},{2,1},{3,2},{4,7},{5,4},{6,5},{7,6},{8,11},{9,8},{10,9... | collective-permute-start | bytes 49160 | tf_op jit(solution)/shard_map/ppermute | solution.py:34
  44.2 6.5 %collective-permute-start.4 = (f32[8,512]{1,0:T(8,128)S(1)}, f32[8,512]{1,0:T(8,128)S(1)}, u32[]{:S(2)}, u32[]{:S(2)}) collective-permute-start(f32[8,512]{1,0:T(8,128)S(1)} %get-tuple-element.62), channel_id=1, source_target_pairs={{0,4},{4,8},{8,12},{12,16},{16,20},{20,24},{24,28},{28,0},{1,5},{5... | collective-permute-start | bytes 49160 | tf_op jit(solution)/shard_map/ppermute | solution.py:34
  45.3 5.4 %collective-permute-start.5 = (f32[8,512]{1,0:T(8,128)S(1)}, f32[8,512]{1,0:T(8,128)S(1)}, u32[]{:S(2)}, u32[]{:S(2)}) collective-permute-start(f32[8,512]{1,0:T(8,128)S(1)} %get-tuple-element.63), channel_id=1, source_target_pairs={{0,1},{1,2},{2,3},{3,0},{4,5},{5,6},{6,7},{7,4},{8,9},{9,10},{10,1... | collective-permute-start | bytes 49160 | tf_op jit(solution)/shard_map/ppermute | solution.py:34
  52.3 10.1 %all-to-all-start.2 = ((f32[8,3,4,128]{3,2,1,0:T(4,128)}), f32[8,3,4,128]{3,2,1,0:T(4,128)S(1)}, u32[]{:S(2)}, u32[]{:S(2)}) async-start(f32[8,3,4,128]{3,2,1,0:T(4,128)} %get-tuple-element.65), calls=%async_computation.2 | async-start | bytes 98304 | tf_op jit(solution)/shard_map/all_to_all | solution.py:743
  59.1 0.6 copy-start.8
  66.0 9.8 %all-to-all-start.3 = ((f32[8,2,128]{2,1,0:T(2,128)}), f32[8,2,128]{2,1,0:T(2,128)S(1)}, u32[]{:S(2)}, u32[]{:S(2)}) async-start(f32[8,2,128]{2,1,0:T(2,128)} %bitcast.5), calls=%async_computation.3 | async-start | bytes 16384 | tf_op jit(solution)/shard_map/all_to_all | solution.py:748
  76.9 4.1 %collective-permute-start.6 = (f32[8,512]{1,0:T(8,128)S(1)}, f32[8,512]{1,0:T(8,128)S(1)}, u32[]{:S(2)}, u32[]{:S(2)}) collective-permute-start(f32[8,512]{1,0:T(8,128)S(1)} %get-tuple-element.71), channel_id=1, source_target_pairs={{0,28},{4,0},{8,4},{12,8},{16,12},{20,16},{24,20},{28,24},{1,29},{... | collective-permute-start | bytes 49160 | tf_op jit(solution)/shard_map/ppermute | solution.py:34
  79.3 1.7 %collective-permute-start.7 = (f32[8,512]{1,0:T(8,128)S(1)}, f32[8,512]{1,0:T(8,128)S(1)}, u32[]{:S(2)}, u32[]{:S(2)}) collective-permute-start(f32[8,512]{1,0:T(8,128)S(1)} %get-tuple-element.72), channel_id=1, source_target_pairs={{0,3},{1,0},{2,1},{3,2},{4,7},{5,4},{6,5},{7,6},{8,11},{9,8},{10,9... | collective-permute-start | bytes 49160 | tf_op jit(solution)/shard_map/ppermute | solution.py:34
  83.6 6.5 %collective-permute-start.8 = (f32[8,512]{1,0:T(8,128)S(1)}, f32[8,512]{1,0:T(8,128)S(1)}, u32[]{:S(2)}, u32[]{:S(2)}) collective-permute-start(f32[8,512]{1,0:T(8,128)S(1)} %get-tuple-element.74), channel_id=1, source_target_pairs={{0,4},{4,8},{8,12},{12,16},{16,20},{20,24},{24,28},{28,0},{1,5},{5... | collective-permute-start | bytes 49160 | tf_op jit(solution)/shard_map/ppermute | solution.py:34
  84.8 5.4 %collective-permute-start.9 = (f32[8,512]{1,0:T(8,128)S(1)}, f32[8,512]{1,0:T(8,128)S(1)}, u32[]{:S(2)}, u32[]{:S(2)}) collective-permute-start(f32[8,512]{1,0:T(8,128)S(1)} %get-tuple-element.75), channel_id=1, source_target_pairs={{0,1},{1,2},{2,3},{3,0},{4,5},{5,6},{6,7},{7,4},{8,9},{9,10},{10,1... | collective-permute-start | bytes 49160 | tf_op jit(solution)/shard_map/ppermute | solution.py:34
  86.3 8.9 %copy-start.9 = (f32[3,32,128]{2,1,0:T(8,128)S(1)}, f32[3,32,128]{2,1,0:T(8,128)}, u32[]{:S(2)}) copy-start(f32[3,32,128]{2,1,0:T(8,128)} %copy-done.8) | copy-start | bytes 147460
  91.8 10.1 %all-to-all-start.4 = ((f32[8,3,4,128]{3,2,1,0:T(4,128)}), f32[8,3,4,128]{3,2,1,0:T(4,128)S(1)}, u32[]{:S(2)}, u32[]{:S(2)}) async-start(f32[8,3,4,128]{3,2,1,0:T(4,128)} %get-tuple-element.77), calls=%async_computation.4 | async-start | bytes 98304 | tf_op jit(solution)/shard_map/all_to_all | solution.py:743
  105.5 9.8 %all-to-all-start.5 = ((f32[8,2,128]{2,1,0:T(2,128)}), f32[8,2,128]{2,1,0:T(2,128)S(1)}, u32[]{:S(2)}, u32[]{:S(2)}) async-start(f32[8,2,128]{2,1,0:T(2,128)} %bitcast.7), calls=%async_computation.5 | async-start | bytes 16384 | tf_op jit(solution)/shard_map/all_to_all | solution.py:748
  116.4 4.1 %collective-permute-start.10 = (f32[8,512]{1,0:T(8,128)S(1)}, f32[8,512]{1,0:T(8,128)S(1)}, u32[]{:S(2)}, u32[]{:S(2)}) collective-permute-start(f32[8,512]{1,0:T(8,128)S(1)} %get-tuple-element.83), channel_id=1, source_target_pairs={{0,28},{4,0},{8,4},{12,8},{16,12},{20,16},{24,20},{28,24},{1,29},{... | collective-permute-start | bytes 49160 | tf_op jit(solution)/shard_map/ppermute | solution.py:34
  118.8 1.7 %collective-permute-start.11 = (f32[8,512]{1,0:T(8,128)S(1)}, f32[8,512]{1,0:T(8,128)S(1)}, u32[]{:S(2)}, u32[]{:S(2)}) collective-permute-start(f32[8,512]{1,0:T(8,128)S(1)} %get-tuple-element.84), channel_id=1, source_target_pairs={{0,3},{1,0},{2,1},{3,2},{4,7},{5,4},{6,5},{7,6},{8,11},{9,8},{10,9... | collective-permute-start | bytes 49160 | tf_op jit(solution)/shard_map/ppermute | solution.py:34
  123.1 6.5 %collective-permute-start.12 = (f32[8,512]{1,0:T(8,128)S(1)}, f32[8,512]{1,0:T(8,128)S(1)}, u32[]{:S(2)}, u32[]{:S(2)}) collective-permute-start(f32[8,512]{1,0:T(8,128)S(1)} %get-tuple-element.86), channel_id=1, source_target_pairs={{0,4},{4,8},{8,12},{12,16},{16,20},{20,24},{24,28},{28,0},{1,5},{5... | collective-permute-start | bytes 49160 | tf_op jit(solution)/shard_map/ppermute | solution.py:34
  124.2 5.4 %collective-permute-start.13 = (f32[8,512]{1,0:T(8,128)S(1)}, f32[8,512]{1,0:T(8,128)S(1)}, u32[]{:S(2)}, u32[]{:S(2)}) collective-permute-start(f32[8,512]{1,0:T(8,128)S(1)} %get-tuple-element.87), channel_id=1, source_target_pairs={{0,1},{1,2},{2,3},{3,0},{4,5},{5,6},{6,7},{7,4},{8,9},{9,10},{10,1... | collective-permute-start | bytes 49160 | tf_op jit(solution)/shard_map/ppermute | solution.py:34
  131.3 10.1 %all-to-all-start.6 = ((f32[8,3,4,128]{3,2,1,0:T(4,128)}), f32[8,3,4,128]{3,2,1,0:T(4,128)S(1)}, u32[]{:S(2)}, u32[]{:S(2)}) async-start(f32[8,3,4,128]{3,2,1,0:T(4,128)} %get-tuple-element.89), calls=%async_computation.6 | async-start | bytes 98304 | tf_op jit(solution)/shard_map/all_to_all | solution.py:743
  145.0 9.8 %all-to-all-start.7 = ((f32[8,2,128]{2,1,0:T(2,128)}), f32[8,2,128]{2,1,0:T(2,128)S(1)}, u32[]{:S(2)}, u32[]{:S(2)}) async-start(f32[8,2,128]{2,1,0:T(2,128)} %bitcast.9), calls=%async_computation.7 | async-start | bytes 16384 | tf_op jit(solution)/shard_map/all_to_all | solution.py:748
  155.8 4.8 %collective-permute-start.14 = (f32[8,512]{1,0:T(8,128)S(1)}, f32[8,512]{1,0:T(8,128)S(1)}, u32[]{:S(2)}, u32[]{:S(2)}) collective-permute-start(f32[8,512]{1,0:T(8,128)S(1)} %get-tuple-element.95), channel_id=1, source_target_pairs={{0,28},{4,0},{8,4},{12,8},{16,12},{20,16},{24,20},{28,24},{1,29},{... | collective-permute-start | bytes 49160 | tf_op jit(solution)/shard_map/ppermute | solution.py:34
  159.0 1.7 %collective-permute-start.15 = (f32[8,512]{1,0:T(8,128)S(1)}, f32[8,512]{1,0:T(8,128)S(1)}, u32[]{:S(2)}, u32[]{:S(2)}) collective-permute-start(f32[8,512]{1,0:T(8,128)S(1)} %get-tuple-element.96), channel_id=1, source_target_pairs={{0,3},{1,0},{2,1},{3,2},{4,7},{5,4},{6,5},{7,6},{8,11},{9,8},{10,9... | collective-permute-start | bytes 49160 | tf_op jit(solution)/shard_map/ppermute | solution.py:34

commit v2 on v1

--- a/solution.py
+++ b/solution.py
@@ -201,7 +201,7 @@
             rows_ref[pl.ds(start, ROWS), :] = jnp.where(ids >= nodes, far, near)
         return carry
 
-    lax.fori_loop(0, conn_ref.shape[1] // SEG, tile, 0, unroll=16)
+    lax.fori_loop(0, conn_ref.shape[1] // SEG, tile, 0, unroll=32)
     for group in range(blocks // 8):
         corner = [
             tuple(rows_ref[pl.ds(group * 128 + i * 4 + c, 8, stride=16), :] for c in range(3))
@@ -478,15 +478,22 @@
 
 
 def react_own_kernel(step, blocks_ref, back_ref, tiles_ref, acc_ref, own_ref):
-    last = own_ref.shape[1] // LOW
-    total = react_tiles(step, 0, last, LOW, 8, blocks_ref, back_ref, tiles_ref)
-    own_ref[...] = unstack(total + acc_ref[: last * ROWS, :])
+    nodes = own_ref.shape[1]
+    total = react_tiles(step, 0, nodes // SEG, SEG, 16, blocks_ref, back_ref, tiles_ref)
+    own_ref[...] = unstack(total) + unstack(acc_ref[: nodes // LOW * ROWS, :])
 
 
 def spread_rows(values, ids, first, last, low=LOW):
-    high_ids = ids >> (low.bit_length() - 1)
-    parts = [jnp.where(high_ids == part, values, 0.0) for part in range(first, last)]
-    return jnp.concatenate(parts, axis=0).astype(BF16)
+    width = values.shape[1]
+    twice = jnp.concatenate([values, values], axis=0).astype(BF16)
+    high_ids = jnp.broadcast_to((ids >> (low.bit_length() - 1)).astype(F32), (2 * ROWS, width))
+    second = lax.broadcasted_iota(jnp.int32, (2 * ROWS, width), 0) >= ROWS
+    offset = (high_ids - jnp.where(second, 1.0, 0.0)).astype(BF16)
+    zero = jnp.zeros((), BF16)
+    parts = [
+        jnp.where(offset == jnp.asarray(part, BF16), twice, zero) for part in range(first, last, 2)
+    ]
+    return jnp.concatenate(parts, axis=0)
 
 
 def dot_rows(left, right):
@@ -512,12 +519,12 @@
 
 def add_back(back, ids_ref, count):
     rows = split_rows(back[0:3])
-    total = jnp.zeros((count * ROWS, LOW), F32)
+    total = jnp.zeros((count * ROWS, SEG), F32)
     for index in range(back.shape[1] // LOW):
         here = slice(index * LOW, (index + 1) * LOW)
         ids = ids_ref[:, here]
-        spread = spread_rows(rows[:, here], ids, 0, count)
-        total = total + dot_rows(spread, one_hot_low(ids & (LOW - 1)))
+        spread = spread_rows(rows[:, here], ids, 0, count, SEG)
+        total = total + dot_rows(spread, one_hot_low(ids & (SEG - 1), SEG))
     return total
 
 
@@ -563,7 +570,7 @@
     own_ref, force_ref, slave_ref, back_mesh_ref, back_sub_ref, mass_ref, mesh_ids_ref,
     sub_ids_ref,
 ):
-    count = own_ref.shape[1] // LOW
+    count = own_ref.shape[1] // SEG
     extra = add_back(back_mesh_ref[...], mesh_ids_ref, count) + add_back(
         back_sub_ref[...], sub_ids_ref, count
     )
@@ -726,7 +733,10 @@
     collect = lambda step: call(functools.partial(collect_kernel, step), [(blocks, SEG)], [SM, VM])
 
     own, to_mesh, to_sub = pack(
-        *[pltpu.with_memory_space_constraint(x, pltpu.HBM) for x in (coords, veloc, mesh_ids, sub_ids)]
+        *[
+            pltpu.with_memory_space_constraint(source, pltpu.HBM)
+            for source in (coords, veloc, mesh_ids, sub_ids)
+        ]
     )
     if by_slot:
         (tiles,) = pick_tiles(send_pick, conn)

time: 163 us -> 160 us (0.982)
  Pallas kernels: 78.6 us -> 71 us
  waiting for transfers between devices: 33.1 us -> 39.1 us
  starting transfers between devices: 46.7 us -> 44.6 us
    ppermute x16, waiting for transfers between devices: 11.6 us -> 15.4 us  [shifted(): return lax.ppermute(value, axis, pairs)]
    pallas_call x4, Pallas kernels: 6.67 us -> 2.86 us  [per_device(): force, = react_own(at)(*rows)]
    all_to_all x4, waiting for transfers between devices: 8.14 us -> 10.3 us  [per_device(): lax.all_to_all(react.reshape(peers, per_peer, SEG), 'mesh', split_axis=0,...]
    pallas_call x4, Pallas kernels: 16.8 us -> 14.8 us  [per_device(): acc, = internal_of(pushes, conn)]
    ppermute x16, starting transfers between devices: 17.9 us -> 16.1 us  [shifted(): return lax.ppermute(value, axis, pairs)]
  transfers between devices with their start and end apart: 24 -> 24, of which waited for: 11 -> 15; matrix products, arithmetic and copies ran while one was open for 0% -> 0% of each run, Pallas kernels for 27% -> 24%
where the time goes in v2:
time: 160 us; the launch traced here: 158 us
  Pallas kernels  71 us (44%)
  starting transfers between devices  44.6 us (28%)
  waiting for transfers between devices  39.1 us (24%)
  local copies, waits for them, and re-layouts  2.16 us (1%)
    ppermute x16, starting transfers between devices, shifted(): return lax.ppermute(value, axis, pairs)  16.1 us
    ppermute x16, waiting for transfers between devices, shifted(): return lax.ppermute(value, axis, pairs)  15.4 us
    all_to_all x4, starting transfers between devices, per_device(): lax.all_to_all(outgoing, 'mesh', split_axis=0, concat_axis=0, tiled=True)  15.2 us
    pallas_call x4, Pallas kernels, per_device(): acc, = internal_of(pushes, conn)  14.8 us
    pallas_call x4, Pallas kernels, per_device(): slave, react = contact(step)(bucket_list, node, incoming)  14.3 us
    all_to_all x4, starting transfers between devices, per_device(): lax.all_to_all(react.reshape(peers, per_peer, SEG), 'mesh', split_axis=0,...  13.4 us
    all_to_all x4, waiting for transfers between devices, per_device(): lax.all_to_all(outgoing, 'mesh', split_axis=0, concat_axis=0, tiled=True)  13.3 us
    pallas_call x4, Pallas kernels, per_device(): forces(own, from_mesh, from_sub, conn, corner, stress_now)  12.9 us
  transfers between devices with their start and end apart: 24, of which 15 were waited for; matrix products, arithmetic and copies ran while one was open for 0% of the time, Pallas kernels for 24%

profile of v2, /device:TPU:0, one launch (start us, length us, event | category | flops | bytes accessed | tf_op | source)
XLA Modules:
  0.0 157.9 jit_solution(3631692548123191345)
XLA Ops:
  0.6 1.1 shard_map.113
  1.7 3.0 %collective-permute-start = (f32[8,512]{1,0:T(8,128)S(1)}, f32[8,512]{1,0:T(8,128)S(1)}, u32[]{:S(2)}, u32[]{:S(2)}) collective-permute-start(f32[8,512]{1,0:T(8,128)S(1)} %get-tuple-element.51), channel_id=1, source_target_pairs={{0,4},{4,8},{8,12},{12,16},{16,20},{20,24},{24,28},{28,0},{1,5},{5... | collective-permute-start | bytes 49160 | tf_op jit(solution)/shard_map/ppermute | solution.py:34
  4.8 0.8 copy-done.1
  5.6 1.9 %shard_map.114.refs_4_ = f32[512,128]{1,0:T(8,128)S(1)} custom-call(f32[8,2048]{1,0:T(8,128)S(1)} %get-tuple-element.50.own_ref.refs_0_, s32[4,4096]{1,0:T(4,128)S(1)} %copy-done.1), custom_call_target="tpu_custom_call" | custom-call | flops 2147483648 | bytes 1048576 | tf_op jit(solution)/shard_map/pallas_call | solution.py:748
  7.5 1.2 shard_map.116.node_ref
  8.7 0.8 shard_map.118.tiles_ref
  9.5 1.5 shard_map.115
  11.1 4.9 %all-to-all-start = ((f32[8,3,4,128]{3,2,1,0:T(4,128)}), f32[8,3,4,128]{3,2,1,0:T(4,128)S(1)}, u32[]{:S(2)}, u32[]{:S(2)}) async-start(f32[8,3,4,128]{3,2,1,0:T(4,128)} %get-tuple-element.54), calls=%async_computation | async-start | bytes 98304 | tf_op jit(solution)/shard_map/all_to_all | solution.py:753
  16.0 3.2 %shard_map.119 = (f32[1024,128]{1,0:T(8,128)S(1)}, f32[3,32,128]{2,1,0:T(8,128)S(1)}) custom-call(f32[8,2048]{1,0:T(8,128)S(1)} %get-tuple-element.50.own_ref.refs_0_, f32[8,512]{1,0:T(8,128)S(1)} %collective-permute-done.refs_1_.mesh_ref, f32[8,512]{1,0:T(8,128)S(1)} %collective-permute-done.1.refs_2_.sub_ref, s32[4,4096]{1,0:T(4,128)S(1)} %copy-done.2, ...), custom_call_target="tpu_custom_call" | custom-call | flops 2147483648 | bytes 1048576 | tf_op jit(solution)/shard_map/pallas_call | solution.py:756
  19.2 3.6 %all-to-all-done.slots_ref = f32[8,3,4,128]{3,2,1,0:T(4,128)S(1)} async-done(((f32[8,3,4,128]{3,2,1,0:T(4,128)}), f32[8,3,4,128]{3,2,1,0:T(4,128)S(1)}, u32[]{:S(2)}, u32[]{:S(2)}) %all-to-all-start) | async-done | bytes 49184 | tf_op jit(solution)/shard_map/all_to_all | solution.py:753
  22.8 3.6 %shard_map.117 = (f32[8,2048]{1,0:T(8,128)S(1)}, f32[16,128]{1,0:T(8,128)}) custom-call(s32[4,4,16]{2,1,0:T(4,128)S(1)} %copy-done.7, bf16[4,2048,128]{2,1,0:T(8,128)(2,1)S(1)} %shard_map.116.node_ref, f32[8,3,4,128]{3,2,1,0:T(4,128)S(1)} %all-to-all-done.slots_ref), custom_call_target="tpu_custom_call" | custom-call | flops 2147483648 | bytes 1048576 | tf_op jit(solution)/shard_map/pallas_call | solution.py:757
  26.4 3.3 %all-to-all-start.1 = ((f32[8,2,128]{2,1,0:T(2,128)}), f32[8,2,128]{2,1,0:T(2,128)S(1)}, u32[]{:S(2)}, u32[]{:S(2)}) async-start(f32[8,2,128]{2,1,0:T(2,128)} %bitcast.2), calls=%async_computation.1 | async-start | bytes 16384 | tf_op jit(solution)/shard_map/all_to_all | solution.py:758
  29.7 3.7 %shard_map.120.acc_ref = f32[96,256]{1,0:T(8,128)S(1)} custom-call(f32[1024,128]{1,0:T(8,128)S(1)} %get-tuple-element.57.rows_ref, s32[4,4096]{1,0:T(4,128)S(1)} %copy-done.2), custom_call_target="tpu_custom_call" | custom-call | flops 2147483648 | bytes 1048576 | tf_op jit(solution)/shard_map/pallas_call | solution.py:762
  33.4 2.7 %all-to-all-done.1 = f32[8,2,128]{2,1,0:T(2,128)S(1)} async-done(((f32[8,2,128]{2,1,0:T(2,128)}), f32[8,2,128]{2,1,0:T(2,128)S(1)}, u32[]{:S(2)}, u32[]{:S(2)}) %all-to-all-start.1) | async-done | bytes 8224 | tf_op jit(solution)/shard_map/all_to_all | solution.py:758
  36.2 0.8 shard_map.122
  37.0 2.0 %collective-permute-start.2 = (f32[8,512]{1,0:T(8,128)S(1)}, f32[8,512]{1,0:T(8,128)S(1)}, u32[]{:S(2)}, u32[]{:S(2)}) collective-permute-start(f32[8,512]{1,0:T(8,128)S(1)} %get-tuple-element.59), channel_id=1, source_target_pairs={{0,28},{4,0},{8,4},{12,8},{16,12},{20,16},{24,20},{28,24},{1,29},{... | collective-permute-start | bytes 49160 | tf_op jit(solution)/shard_map/ppermute | solution.py:34
  39.0 0.7 shard_map.121.refs_1_
  39.7 1.1 collective-permute-done.2.refs_3_
  41.5 1.9 %shard_map.124.refs_4_ = f32[512,128]{1,0:T(8,128)S(1)} custom-call(f32[8,2048]{1,0:T(8,128)S(1)} %get-tuple-element.61.own_ref.refs_0_, s32[4,4096]{1,0:T(4,128)S(1)} %copy-done.2), custom_call_target="tpu_custom_call" | custom-call | flops 2147483648 | bytes 1048576 | tf_op jit(solution)/shard_map/pallas_call | solution.py:748
  43.3 1.5 collective-permute-start.4
  44.8 1.2 shard_map.126.node_ref
  46.0 3.8 %collective-permute-done.4.refs_1_.mesh_ref = f32[8,512]{1,0:T(8,128)S(1)} collective-permute-done((f32[8,512]{1,0:T(8,128)S(1)}, f32[8,512]{1,0:T(8,128)S(1)}, u32[]{:S(2)}, u32[]{:S(2)}) %collective-permute-start.4) | collective-permute-done | bytes 16416 | tf_op jit(solution)/shard_map/ppermute | solution.py:34
  49.8 1.5 shard_map.125
  51.3 3.5 %all-to-all-start.2 = ((f32[8,3,4,128]{3,2,1,0:T(4,128)}), f32[8,3,4,128]{3,2,1,0:T(4,128)S(1)}, u32[]{:S(2)}, u32[]{:S(2)}) async-start(f32[8,3,4,128]{3,2,1,0:T(4,128)} %get-tuple-element.65), calls=%async_computation.2 | async-start | bytes 98304 | tf_op jit(solution)/shard_map/all_to_all | solution.py:753
  54.9 3.2 %shard_map.128 = (f32[1024,128]{1,0:T(8,128)S(1)}, f32[3,32,128]{2,1,0:T(8,128)S(1)}) custom-call(f32[8,2048]{1,0:T(8,128)S(1)} %get-tuple-element.61.own_ref.refs_0_, f32[8,512]{1,0:T(8,128)S(1)} %collective-permute-done.4.refs_1_.mesh_ref, f32[8,512]{1,0:T(8,128)S(1)} %collective-permute-done.5.refs_2_.sub_ref, s32[4,4096]{1,0:T(4,128)S(1)} %copy-done.2, ...), custom_call_target="tpu_custom_call" | custom-call | flops 2147483648 | bytes 1048576 | tf_op jit(solution)/shard_map/pallas_call | solution.py:756
  58.7 2.7 %all-to-all-done.2.slots_ref = f32[8,3,4,128]{3,2,1,0:T(4,128)S(1)} async-done(((f32[8,3,4,128]{3,2,1,0:T(4,128)}), f32[8,3,4,128]{3,2,1,0:T(4,128)S(1)}, u32[]{:S(2)}, u32[]{:S(2)}) %all-to-all-start.2) | async-done | bytes 49184 | tf_op jit(solution)/shard_map/all_to_all | solution.py:753
  61.4 3.6 %shard_map.127 = (f32[8,2048]{1,0:T(8,128)S(1)}, f32[16,128]{1,0:T(8,128)}) custom-call(s32[4,4,16]{2,1,0:T(4,128)S(1)} %copy-done.7, bf16[4,2048,128]{2,1,0:T(8,128)(2,1)S(1)} %shard_map.126.node_ref, f32[8,3,4,128]{3,2,1,0:T(4,128)S(1)} %all-to-all-done.2.slots_ref), custom_call_target="tpu_custom_call" | custom-call | flops 2147483648 | bytes 1048576 | tf_op jit(solution)/shard_map/pallas_call | solution.py:757
  65.0 3.3 %all-to-all-start.3 = ((f32[8,2,128]{2,1,0:T(2,128)}), f32[8,2,128]{2,1,0:T(2,128)S(1)}, u32[]{:S(2)}, u32[]{:S(2)}) async-start(f32[8,2,128]{2,1,0:T(2,128)} %bitcast.5), calls=%async_computation.3 | async-start | bytes 16384 | tf_op jit(solution)/shard_map/all_to_all | solution.py:758
  68.4 3.7 %shard_map.129.acc_ref = f32[96,256]{1,0:T(8,128)S(1)} custom-call(f32[1024,128]{1,0:T(8,128)S(1)} %get-tuple-element.69.rows_ref, s32[4,4096]{1,0:T(4,128)S(1)} %copy-done.2), custom_call_target="tpu_custom_call" | custom-call | flops 2147483648 | bytes 1048576 | tf_op jit(solution)/shard_map/pallas_call | solution.py:762
  72.1 2.7 %all-to-all-done.3 = f32[8,2,128]{2,1,0:T(2,128)S(1)} async-done(((f32[8,2,128]{2,1,0:T(2,128)}), f32[8,2,128]{2,1,0:T(2,128)S(1)}, u32[]{:S(2)}, u32[]{:S(2)}) %all-to-all-start.3) | async-done | bytes 8224 | tf_op jit(solution)/shard_map/all_to_all | solution.py:758
  74.9 0.8 shard_map.131
  75.7 2.0 %collective-permute-start.6 = (f32[8,512]{1,0:T(8,128)S(1)}, f32[8,512]{1,0:T(8,128)S(1)}, u32[]{:S(2)}, u32[]{:S(2)}) collective-permute-start(f32[8,512]{1,0:T(8,128)S(1)} %get-tuple-element.71), channel_id=1, source_target_pairs={{0,28},{4,0},{8,4},{12,8},{16,12},{20,16},{24,20},{28,24},{1,29},{... | collective-permute-start | bytes 49160 | tf_op jit(solution)/shard_map/ppermute | solution.py:34
  78.4 1.1 collective-permute-done.6.refs_3_
  80.1 1.9 %shard_map.133.refs_4_ = f32[512,128]{1,0:T(8,128)S(1)} custom-call(f32[8,2048]{1,0:T(8,128)S(1)} %get-tuple-element.73.own_ref.refs_0_, s32[4,4096]{1,0:T(4,128)S(1)} %copy-done.2), custom_call_target="tpu_custom_call" | custom-call | flops 2147483648 | bytes 1048576 | tf_op jit(solution)/shard_map/pallas_call | solution.py:748
  82.0 1.5 collective-permute-start.8
  83.5 1.2 shard_map.135.node_ref
  84.6 3.8 %collective-permute-done.8.refs_1_.mesh_ref = f32[8,512]{1,0:T(8,128)S(1)} collective-permute-done((f32[8,512]{1,0:T(8,128)S(1)}, f32[8,512]{1,0:T(8,128)S(1)}, u32[]{:S(2)}, u32[]{:S(2)}) %collective-permute-start.8) | collective-permute-done | bytes 16416 | tf_op jit(solution)/shard_map/ppermute | solution.py:34
  88.5 1.5 shard_map.134
  90.0 3.4 %all-to-all-start.4 = ((f32[8,3,4,128]{3,2,1,0:T(4,128)}), f32[8,3,4,128]{3,2,1,0:T(4,128)S(1)}, u32[]{:S(2)}, u32[]{:S(2)}) async-start(f32[8,3,4,128]{3,2,1,0:T(4,128)} %get-tuple-element.77), calls=%async_computation.4 | async-start | bytes 98304 | tf_op jit(solution)/shard_map/all_to_all | solution.py:753
  93.4 3.2 %shard_map.137 = (f32[1024,128]{1,0:T(8,128)S(1)}, f32[3,32,128]{2,1,0:T(8,128)S(1)}) custom-call(f32[8,2048]{1,0:T(8,128)S(1)} %get-tuple-element.73.own_ref.refs_0_, f32[8,512]{1,0:T(8,128)S(1)} %collective-permute-done.8.refs_1_.mesh_ref, f32[8,512]{1,0:T(8,128)S(1)} %collective-permute-done.9.refs_2_.sub_ref, s32[4,4096]{1,0:T(4,128)S(1)} %copy-done.2, ...), custom_call_target="tpu_custom_call" | custom-call | flops 2147483648 | bytes 1048576 | tf_op jit(solution)/shard_map/pallas_call | solution.py:756
  96.6 3.5 %all-to-all-done.4.slots_ref = f32[8,3,4,128]{3,2,1,0:T(4,128)S(1)} async-done(((f32[8,3,4,128]{3,2,1,0:T(4,128)}), f32[8,3,4,128]{3,2,1,0:T(4,128)S(1)}, u32[]{:S(2)}, u32[]{:S(2)}) %all-to-all-start.4) | async-done | bytes 49184 | tf_op jit(solution)/shard_map/all_to_all | solution.py:753
  100.1 3.6 %shard_map.136 = (f32[8,2048]{1,0:T(8,128)S(1)}, f32[16,128]{1,0:T(8,128)}) custom-call(s32[4,4,16]{2,1,0:T(4,128)S(1)} %copy-done.7, bf16[4,2048,128]{2,1,0:T(8,128)(2,1)S(1)} %shard_map.135.node_ref, f32[8,3,4,128]{3,2,1,0:T(4,128)S(1)} %all-to-all-done.4.slots_ref), custom_call_target="tpu_custom_call" | custom-call | flops 2147483648 | bytes 1048576 | tf_op jit(solution)/shard_map/pallas_call | solution.py:757
  103.7 3.3 %all-to-all-start.5 = ((f32[8,2,128]{2,1,0:T(2,128)}), f32[8,2,128]{2,1,0:T(2,128)S(1)}, u32[]{:S(2)}, u32[]{:S(2)}) async-start(f32[8,2,128]{2,1,0:T(2,128)} %bitcast.7), calls=%async_computation.5 | async-start | bytes 16384 | tf_op jit(solution)/shard_map/all_to_all | solution.py:758
  107.0 3.7 %shard_map.138.acc_ref = f32[96,256]{1,0:T(8,128)S(1)} custom-call(f32[1024,128]{1,0:T(8,128)S(1)} %get-tuple-element.81.rows_ref, s32[4,4096]{1,0:T(4,128)S(1)} %copy-done.2), custom_call_target="tpu_custom_call" | custom-call | flops 2147483648 | bytes 1048576 | tf_op jit(solution)/shard_map/pallas_call | solution.py:762
  110.7 2.7 %all-to-all-done.5 = f32[8,2,128]{2,1,0:T(2,128)S(1)} async-done(((f32[8,2,128]{2,1,0:T(2,128)}), f32[8,2,128]{2,1,0:T(2,128)S(1)}, u32[]{:S(2)}, u32[]{:S(2)}) %all-to-all-start.5) | async-done | bytes 8224 | tf_op jit(solution)/shard_map/all_to_all | solution.py:758
  113.5 0.8 shard_map.140
  114.3 2.0 %collective-permute-start.10 = (f32[8,512]{1,0:T(8,128)S(1)}, f32[8,512]{1,0:T(8,128)S(1)}, u32[]{:S(2)}, u32[]{:S(2)}) collective-permute-start(f32[8,512]{1,0:T(8,128)S(1)} %get-tuple-element.83), channel_id=1, source_target_pairs={{0,28},{4,0},{8,4},{12,8},{16,12},{20,16},{24,20},{28,24},{1,29},{... | collective-permute-start | bytes 49160 | tf_op jit(solution)/shard_map/ppermute | solution.py:34
  117.0 1.1 collective-permute-done.10.refs_3_
  118.7 1.9 %shard_map.142.refs_4_ = f32[512,128]{1,0:T(8,128)S(1)} custom-call(f32[8,2048]{1,0:T(8,128)S(1)} %get-tuple-element.85.own_ref.refs_0_, s32[4,4096]{1,0:T(4,128)S(1)} %copy-done.2), custom_call_target="tpu_custom_call" | custom-call | flops 2147483648 | bytes 1048576 | tf_op jit(solution)/shard_map/pallas_call | solution.py:748
  120.6 1.5 collective-permute-start.12
  122.1 1.2 shard_map.144.node_ref
  123.3 3.8 %collective-permute-done.12.refs_1_.mesh_ref = f32[8,512]{1,0:T(8,128)S(1)} collective-permute-done((f32[8,512]{1,0:T(8,128)S(1)}, f32[8,512]{1,0:T(8,128)S(1)}, u32[]{:S(2)}, u32[]{:S(2)}) %collective-permute-start.12) | collective-permute-done | bytes 16416 | tf_op jit(solution)/shard_map/ppermute | solution.py:34
  127.1 1.5 shard_map.143
  128.6 3.4 %all-to-all-start.6 = ((f32[8,3,4,128]{3,2,1,0:T(4,128)}), f32[8,3,4,128]{3,2,1,0:T(4,128)S(1)}, u32[]{:S(2)}, u32[]{:S(2)}) async-start(f32[8,3,4,128]{3,2,1,0:T(4,128)} %get-tuple-element.89), calls=%async_computation.6 | async-start | bytes 98304 | tf_op jit(solution)/shard_map/all_to_all | solution.py:753
  132.0 3.2 %shard_map.146 = (f32[1024,128]{1,0:T(8,128)S(1)}, f32[3,32,128]{2,1,0:T(8,128)S(1)}) custom-call(f32[8,2048]{1,0:T(8,128)S(1)} %get-tuple-element.85.own_ref.refs_0_, f32[8,512]{1,0:T(8,128)S(1)} %collective-permute-done.12.refs_1_.mesh_ref, f32[8,512]{1,0:T(8,128)S(1)} %collective-permute-done.13.refs_2_.sub_ref, s32[4,4096]{1,0:T(4,128)S(1)} %copy-done.2, ...), custom_call_target="tpu_custom_call" | custom-call | flops 2147483648 | bytes 1048576 | tf_op jit(solution)/shard_map/pallas_call | solution.py:756
  135.2 3.5 %all-to-all-done.6.slots_ref = f32[8,3,4,128]{3,2,1,0:T(4,128)S(1)} async-done(((f32[8,3,4,128]{3,2,1,0:T(4,128)}), f32[8,3,4,128]{3,2,1,0:T(4,128)S(1)}, u32[]{:S(2)}, u32[]{:S(2)}) %all-to-all-start.6) | async-done | bytes 49184 | tf_op jit(solution)/shard_map/all_to_all | solution.py:753
  138.7 3.6 %shard_map.145 = (f32[8,2048]{1,0:T(8,128)S(1)}, f32[16,128]{1,0:T(8,128)}) custom-call(s32[4,4,16]{2,1,0:T(4,128)S(1)} %copy-done.7, bf16[4,2048,128]{2,1,0:T(8,128)(2,1)S(1)} %shard_map.144.node_ref, f32[8,3,4,128]{3,2,1,0:T(4,128)S(1)} %all-to-all-done.6.slots_ref), custom_call_target="tpu_custom_call" | custom-call | flops 2147483648 | bytes 1048576 | tf_op jit(solution)/shard_map/pallas_call | solution.py:757
  142.3 3.3 %all-to-all-start.7 = ((f32[8,2,128]{2,1,0:T(2,128)}), f32[8,2,128]{2,1,0:T(2,128)S(1)}, u32[]{:S(2)}, u32[]{:S(2)}) async-start(f32[8,2,128]{2,1,0:T(2,128)} %bitcast.9), calls=%async_computation.7 | async-start | bytes 16384 | tf_op jit(solution)/shard_map/all_to_all | solution.py:758
  145.7 3.7 %shard_map.147.acc_ref = f32[96,256]{1,0:T(8,128)S(1)} custom-call(f32[1024,128]{1,0:T(8,128)S(1)} %get-tuple-element.93.rows_ref, s32[4,4096]{1,0:T(4,128)S(1)} %copy-done.2), custom_call_target="tpu_custom_call" | custom-call | flops 2147483648 | bytes 1048576 | tf_op jit(solution)/shard_map/pallas_call | solution.py:762
  150.0 2.1 %all-to-all-done.7 = f32[8,2,128]{2,1,0:T(2,128)S(1)} async-done(((f32[8,2,128]{2,1,0:T(2,128)}), f32[8,2,128]{2,1,0:T(2,128)S(1)}, u32[]{:S(2)}, u32[]{:S(2)}) %all-to-all-start.7) | async-done | bytes 8224 | tf_op jit(solution)/shard_map/all_to_all | solution.py:758
  152.1 0.8 shard_map.149
  153.0 2.6 %collective-permute-start.14 = (f32[8,512]{1,0:T(8,128)S(1)}, f32[8,512]{1,0:T(8,128)S(1)}, u32[]{:S(2)}, u32[]{:S(2)}) collective-permute-start(f32[8,512]{1,0:T(8,128)S(1)} %get-tuple-element.95), channel_id=1, source_target_pairs={{0,28},{4,0},{8,4},{12,8},{16,12},{20,16},{24,20},{28,24},{1,29},{... | collective-permute-start | bytes 49160 | tf_op jit(solution)/shard_map/ppermute | solution.py:34
  156.3 0.7 collective-permute-done.14.refs_3_
  157.0 0.9 shard_map.150
  (46 shorter events, 5.3 us)
Async XLA Ops:
  1.7 7.8 %collective-permute-start = (f32[8,512]{1,0:T(8,128)S(1)}, f32[8,512]{1,0:T(8,128)S(1)}, u32[]{:S(2)}, u32[]{:S(2)}) collective-permute-start(f32[8,512]{1,0:T(8,128)S(1)} %get-tuple-element.51), channel_id=1, source_target_pairs={{0,4},{4,8},{8,12},{12,16},{16,20},{20,24},{24,28},{28,0},{1,5},{5... | collective-permute-start | bytes 49160 | tf_op jit(solution)/shard_map/ppermute | solution.py:34
  4.8 4.8 %collective-permute-start.1 = (f32[8,512]{1,0:T(8,128)S(1)}, f32[8,512]{1,0:T(8,128)S(1)}, u32[]{:S(2)}, u32[]{:S(2)}) collective-permute-start(f32[8,512]{1,0:T(8,128)S(1)} %get-tuple-element.52), channel_id=1, source_target_pairs={{0,1},{1,2},{2,3},{3,0},{4,5},{5,6},{6,7},{7,4},{8,9},{9,10},{10,1... | collective-permute-start | bytes 49160 | tf_op jit(solution)/shard_map/ppermute | solution.py:34
  4.8 0.8 copy-start.1
  5.6 1.9 %copy-start.6 = (s32[4,4,2048]{2,1,0:T(4,128)S(1)}, s32[4,4,2048]{2,1,0:T(4,128)}, u32[]{:S(2)}) copy-start(s32[4,4,2048]{2,1,0:T(4,128)} %mask_ref.7) | copy-start | bytes 393220
  7.5 1.2 copy-start.10
  7.5 1.2 copy-start.2
  7.5 1.2 copy-start.5
  11.1 11.7 %all-to-all-start = ((f32[8,3,4,128]{3,2,1,0:T(4,128)}), f32[8,3,4,128]{3,2,1,0:T(4,128)S(1)}, u32[]{:S(2)}, u32[]{:S(2)}) async-start(f32[8,3,4,128]{3,2,1,0:T(4,128)} %get-tuple-element.54), calls=%async_computation | async-start | bytes 98304 | tf_op jit(solution)/shard_map/all_to_all | solution.py:753
  16.0 6.8 %copy-start.7 = (s32[4,4,16]{2,1,0:T(4,128)S(1)}, s32[4,4,16]{2,1,0:T(4,128)}, u32[]{:S(2)}) copy-start(s32[4,4,16]{2,1,0:T(4,128)} %list_any.7) | copy-start | bytes 3076
  26.4 9.8 %all-to-all-start.1 = ((f32[8,2,128]{2,1,0:T(2,128)}), f32[8,2,128]{2,1,0:T(2,128)S(1)}, u32[]{:S(2)}, u32[]{:S(2)}) async-start(f32[8,2,128]{2,1,0:T(2,128)} %bitcast.2), calls=%async_computation.1 | async-start | bytes 16384 | tf_op jit(solution)/shard_map/all_to_all | solution.py:758
  37.0 3.8 %copy-start = (f32[2048]{0:T(1024)S(1)}, f32[2048]{0:T(1024)}, u32[]{:S(2)}) copy-start(f32[2048]{0:T(1024)} %param.12) | copy-start | bytes 24580
  37.0 3.8 %copy-start.3 = (s32[512]{0:T(512)S(1)}, s32[512]{0:T(512)}, u32[]{:S(2)}) copy-start(s32[512]{0:T(512)} %param.15) | copy-start | bytes 6148
  37.0 3.8 %copy-start.4 = (s32[512]{0:T(512)S(1)}, s32[512]{0:T(512)}, u32[]{:S(2)}) copy-start(s32[512]{0:T(512)} %param.16) | copy-start | bytes 6148
  37.0 3.8 %collective-permute-start.2 = (f32[8,512]{1,0:T(8,128)S(1)}, f32[8,512]{1,0:T(8,128)S(1)}, u32[]{:S(2)}, u32[]{:S(2)}) collective-permute-start(f32[8,512]{1,0:T(8,128)S(1)} %get-tuple-element.59), channel_id=1, source_target_pairs={{0,28},{4,0},{8,4},{12,8},{16,12},{20,16},{24,20},{28,24},{1,29},{... | collective-permute-start | bytes 49160 | tf_op jit(solution)/shard_map/ppermute | solution.py:34
  39.0 1.8 %collective-permute-start.3 = (f32[8,512]{1,0:T(8,128)S(1)}, f32[8,512]{1,0:T(8,128)S(1)}, u32[]{:S(2)}, u32[]{:S(2)}) collective-permute-start(f32[8,512]{1,0:T(8,128)S(1)} %get-tuple-element.60), channel_id=1, source_target_pairs={{0,3},{1,0},{2,1},{3,2},{4,7},{5,4},{6,5},{7,6},{8,11},{9,8},{10,9... | collective-permute-start | bytes 49160 | tf_op jit(solution)/shard_map/ppermute | solution.py:34
  43.3 6.5 %collective-permute-start.4 = (f32[8,512]{1,0:T(8,128)S(1)}, f32[8,512]{1,0:T(8,128)S(1)}, u32[]{:S(2)}, u32[]{:S(2)}) collective-permute-start(f32[8,512]{1,0:T(8,128)S(1)} %get-tuple-element.62), channel_id=1, source_target_pairs={{0,4},{4,8},{8,12},{12,16},{16,20},{20,24},{24,28},{28,0},{1,5},{5... | collective-permute-start | bytes 49160 | tf_op jit(solution)/shard_map/ppermute | solution.py:34
  44.8 5.0 %collective-permute-start.5 = (f32[8,512]{1,0:T(8,128)S(1)}, f32[8,512]{1,0:T(8,128)S(1)}, u32[]{:S(2)}, u32[]{:S(2)}) collective-permute-start(f32[8,512]{1,0:T(8,128)S(1)} %get-tuple-element.63), channel_id=1, source_target_pairs={{0,1},{1,2},{2,3},{3,0},{4,5},{5,6},{6,7},{7,4},{8,9},{9,10},{10,1... | collective-permute-start | bytes 49160 | tf_op jit(solution)/shard_map/ppermute | solution.py:34
  51.3 10.1 %all-to-all-start.2 = ((f32[8,3,4,128]{3,2,1,0:T(4,128)}), f32[8,3,4,128]{3,2,1,0:T(4,128)S(1)}, u32[]{:S(2)}, u32[]{:S(2)}) async-start(f32[8,3,4,128]{3,2,1,0:T(4,128)} %get-tuple-element.65), calls=%async_computation.2 | async-start | bytes 98304 | tf_op jit(solution)/shard_map/all_to_all | solution.py:753
  58.1 0.6 copy-start.8
  65.0 9.8 %all-to-all-start.3 = ((f32[8,2,128]{2,1,0:T(2,128)}), f32[8,2,128]{2,1,0:T(2,128)S(1)}, u32[]{:S(2)}, u32[]{:S(2)}) async-start(f32[8,2,128]{2,1,0:T(2,128)} %bitcast.5), calls=%async_computation.3 | async-start | bytes 16384 | tf_op jit(solution)/shard_map/all_to_all | solution.py:758
  75.7 3.8 %collective-permute-start.6 = (f32[8,512]{1,0:T(8,128)S(1)}, f32[8,512]{1,0:T(8,128)S(1)}, u32[]{:S(2)}, u32[]{:S(2)}) collective-permute-start(f32[8,512]{1,0:T(8,128)S(1)} %get-tuple-element.71), channel_id=1, source_target_pairs={{0,28},{4,0},{8,4},{12,8},{16,12},{20,16},{24,20},{28,24},{1,29},{... | collective-permute-start | bytes 49160 | tf_op jit(solution)/shard_map/ppermute | solution.py:34
  77.7 1.8 %collective-permute-start.7 = (f32[8,512]{1,0:T(8,128)S(1)}, f32[8,512]{1,0:T(8,128)S(1)}, u32[]{:S(2)}, u32[]{:S(2)}) collective-permute-start(f32[8,512]{1,0:T(8,128)S(1)} %get-tuple-element.72), channel_id=1, source_target_pairs={{0,3},{1,0},{2,1},{3,2},{4,7},{5,4},{6,5},{7,6},{8,11},{9,8},{10,9... | collective-permute-start | bytes 49160 | tf_op jit(solution)/shard_map/ppermute | solution.py:34
  82.0 6.5 %collective-permute-start.8 = (f32[8,512]{1,0:T(8,128)S(1)}, f32[8,512]{1,0:T(8,128)S(1)}, u32[]{:S(2)}, u32[]{:S(2)}) collective-permute-start(f32[8,512]{1,0:T(8,128)S(1)} %get-tuple-element.74), channel_id=1, source_target_pairs={{0,4},{4,8},{8,12},{12,16},{16,20},{20,24},{24,28},{28,0},{1,5},{5... | collective-permute-start | bytes 49160 | tf_op jit(solution)/shard_map/ppermute | solution.py:34
  83.5 5.0 %collective-permute-start.9 = (f32[8,512]{1,0:T(8,128)S(1)}, f32[8,512]{1,0:T(8,128)S(1)}, u32[]{:S(2)}, u32[]{:S(2)}) collective-permute-start(f32[8,512]{1,0:T(8,128)S(1)} %get-tuple-element.75), channel_id=1, source_target_pairs={{0,1},{1,2},{2,3},{3,0},{4,5},{5,6},{6,7},{7,4},{8,9},{9,10},{10,1... | collective-permute-start | bytes 49160 | tf_op jit(solution)/shard_map/ppermute | solution.py:34
  84.6 8.7 %copy-start.9 = (f32[3,32,128]{2,1,0:T(8,128)S(1)}, f32[3,32,128]{2,1,0:T(8,128)}, u32[]{:S(2)}) copy-start(f32[3,32,128]{2,1,0:T(8,128)} %copy-done.8) | copy-start | bytes 147460
  90.0 10.1 %all-to-all-start.4 = ((f32[8,3,4,128]{3,2,1,0:T(4,128)}), f32[8,3,4,128]{3,2,1,0:T(4,128)S(1)}, u32[]{:S(2)}, u32[]{:S(2)}) async-start(f32[8,3,4,128]{3,2,1,0:T(4,128)} %get-tuple-element.77), calls=%async_computation.4 | async-start | bytes 98304 | tf_op jit(solution)/shard_map/all_to_all | solution.py:753
  103.7 9.8 %all-to-all-start.5 = ((f32[8,2,128]{2,1,0:T(2,128)}), f32[8,2,128]{2,1,0:T(2,128)S(1)}, u32[]{:S(2)}, u32[]{:S(2)}) async-start(f32[8,2,128]{2,1,0:T(2,128)} %bitcast.7), calls=%async_computation.5 | async-start | bytes 16384 | tf_op jit(solution)/shard_map/all_to_all | solution.py:758
  114.3 3.8 %collective-permute-start.10 = (f32[8,512]{1,0:T(8,128)S(1)}, f32[8,512]{1,0:T(8,128)S(1)}, u32[]{:S(2)}, u32[]{:S(2)}) collective-permute-start(f32[8,512]{1,0:T(8,128)S(1)} %get-tuple-element.83), channel_id=1, source_target_pairs={{0,28},{4,0},{8,4},{12,8},{16,12},{20,16},{24,20},{28,24},{1,29},{... | collective-permute-start | bytes 49160 | tf_op jit(solution)/shard_map/ppermute | solution.py:34
  116.3 1.8 %collective-permute-start.11 = (f32[8,512]{1,0:T(8,128)S(1)}, f32[8,512]{1,0:T(8,128)S(1)}, u32[]{:S(2)}, u32[]{:S(2)}) collective-permute-start(f32[8,512]{1,0:T(8,128)S(1)} %get-tuple-element.84), channel_id=1, source_target_pairs={{0,3},{1,0},{2,1},{3,2},{4,7},{5,4},{6,5},{7,6},{8,11},{9,8},{10,9... | collective-permute-start | bytes 49160 | tf_op jit(solution)/shard_map/ppermute | solution.py:34
  120.6 6.5 %collective-permute-start.12 = (f32[8,512]{1,0:T(8,128)S(1)}, f32[8,512]{1,0:T(8,128)S(1)}, u32[]{:S(2)}, u32[]{:S(2)}) collective-permute-start(f32[8,512]{1,0:T(8,128)S(1)} %get-tuple-element.86), channel_id=1, source_target_pairs={{0,4},{4,8},{8,12},{12,16},{16,20},{20,24},{24,28},{28,0},{1,5},{5... | collective-permute-start | bytes 49160 | tf_op jit(solution)/shard_map/ppermute | solution.py:34
  122.1 5.0 %collective-permute-start.13 = (f32[8,512]{1,0:T(8,128)S(1)}, f32[8,512]{1,0:T(8,128)S(1)}, u32[]{:S(2)}, u32[]{:S(2)}) collective-permute-start(f32[8,512]{1,0:T(8,128)S(1)} %get-tuple-element.87), channel_id=1, source_target_pairs={{0,1},{1,2},{2,3},{3,0},{4,5},{5,6},{6,7},{7,4},{8,9},{9,10},{10,1... | collective-permute-start | bytes 49160 | tf_op jit(solution)/shard_map/ppermute | solution.py:34
  128.6 10.1 %all-to-all-start.6 = ((f32[8,3,4,128]{3,2,1,0:T(4,128)}), f32[8,3,4,128]{3,2,1,0:T(4,128)S(1)}, u32[]{:S(2)}, u32[]{:S(2)}) async-start(f32[8,3,4,128]{3,2,1,0:T(4,128)} %get-tuple-element.89), calls=%async_computation.6 | async-start | bytes 98304 | tf_op jit(solution)/shard_map/all_to_all | solution.py:753
  142.3 9.8 %all-to-all-start.7 = ((f32[8,2,128]{2,1,0:T(2,128)}), f32[8,2,128]{2,1,0:T(2,128)S(1)}, u32[]{:S(2)}, u32[]{:S(2)}) async-start(f32[8,2,128]{2,1,0:T(2,128)} %bitcast.9), calls=%async_computation.7 | async-start | bytes 16384 | tf_op jit(solution)/shard_map/all_to_all | solution.py:758
  153.0 4.1 %collective-permute-start.14 = (f32[8,512]{1,0:T(8,128)S(1)}, f32[8,512]{1,0:T(8,128)S(1)}, u32[]{:S(2)}, u32[]{:S(2)}) collective-permute-start(f32[8,512]{1,0:T(8,128)S(1)} %get-tuple-element.95), channel_id=1, source_target_pairs={{0,28},{4,0},{8,4},{12,8},{16,12},{20,16},{24,20},{28,24},{1,29},{... | collective-permute-start | bytes 49160 | tf_op jit(solution)/shard_map/ppermute | solution.py:34
  155.6 1.4 collective-permute-start.15

commit v3 on v2

--- a/solution.py
+++ b/solution.py
@@ -473,8 +473,8 @@
     first, last = count * LOW // SEG - ghosts // SEG, count * LOW // SEG
     total = react_tiles(step, first, last, SEG, 16, blocks_ref, back_ref, tiles_ref)
     full = unstack(total) + unstack(acc_ref[(count - ghosts // LOW) * ROWS :, :])
-    mesh_ref[...] = full[:, : mesh_ref.shape[1]]
-    sub_ref[...] = full[:, mesh_ref.shape[1] :]
+    mesh_ref[...] = full[:4, : mesh_ref.shape[1]]
+    sub_ref[...] = full[:4, mesh_ref.shape[1] :]
 
 
 def react_own_kernel(step, blocks_ref, back_ref, tiles_ref, acc_ref, own_ref):
@@ -714,7 +714,7 @@
     internal_of = call(internal_kernel, [(width // LOW * ROWS, LOW)], [VM] * 2, flops=1 << 31)
     react_ghost = lambda step: call(
         functools.partial(react_ghost_kernel, step),
-        [(ROWS, ghost_mesh), (ROWS, ghost_sub)],
+        [(4, ghost_mesh), (4, ghost_sub)],
         [VM] * 4,
         flops=1 << 29,
     )

time: 160 us -> 159 us (level)
  no operation moved by 1% of the time
where the time goes in v3:
time: 159 us; the launch traced here: 158 us
  Pallas kernels  71 us (45%)
  starting transfers between devices  44.6 us (28%)
  waiting for transfers between devices  38.7 us (24%)
  local copies, waits for them, and re-layouts  2.16 us (1%)
    ppermute x16, starting transfers between devices, shifted(): return lax.ppermute(value, axis, pairs)  16.1 us
    all_to_all x4, starting transfers between devices, per_device(): lax.all_to_all(outgoing, 'mesh', split_axis=0, concat_axis=0, tiled=True)  15.2 us
    ppermute x16, waiting for transfers between devices, shifted(): return lax.ppermute(value, axis, pairs)  15.1 us
    pallas_call x4, Pallas kernels, per_device(): acc, = internal_of(pushes, conn)  14.8 us
    pallas_call x4, Pallas kernels, per_device(): slave, react = contact(step)(bucket_list, node, incoming)  14.3 us
    all_to_all x4, starting transfers between devices, per_device(): lax.all_to_all(react.reshape(peers, per_peer, SEG), 'mesh', split_axis=0,...  13.4 us
    all_to_all x4, waiting for transfers between devices, per_device(): lax.all_to_all(outgoing, 'mesh', split_axis=0, concat_axis=0, tiled=True)  13.3 us
    pallas_call x4, Pallas kernels, per_device(): forces(own, from_mesh, from_sub, conn, corner, stress_now)  12.9 us
  transfers between devices with their start and end apart: 24, of which 15 were waited for; matrix products, arithmetic and copies ran while one was open for 0% of the time, Pallas kernels for 24%

profile of v3, /device:TPU:0, one launch (start us, length us, event | category | flops | bytes accessed | tf_op | source)
XLA Modules:
  0.0 157.6 jit_solution(16229147950652738070)
XLA Ops:
  0.6 1.1 shard_map.113
  1.7 3.0 %collective-permute-start = (f32[8,512]{1,0:T(8,128)S(1)}, f32[8,512]{1,0:T(8,128)S(1)}, u32[]{:S(2)}, u32[]{:S(2)}) collective-permute-start(f32[8,512]{1,0:T(8,128)S(1)} %get-tuple-element.51), channel_id=1, source_target_pairs={{0,4},{4,8},{8,12},{12,16},{16,20},{20,24},{24,28},{28,0},{1,5},{5... | collective-permute-start | bytes 49160 | tf_op jit(solution)/shard_map/ppermute | solution.py:34
  4.8 0.8 copy-done.1
  5.6 1.9 %shard_map.114.refs_4_ = f32[512,128]{1,0:T(8,128)S(1)} custom-call(f32[8,2048]{1,0:T(8,128)S(1)} %get-tuple-element.50.own_ref.refs_0_, s32[4,4096]{1,0:T(4,128)S(1)} %copy-done.1), custom_call_target="tpu_custom_call" | custom-call | flops 2147483648 | bytes 1048576 | tf_op jit(solution)/shard_map/pallas_call | solution.py:748
  7.5 1.2 shard_map.116.node_ref
  8.7 0.8 shard_map.118.tiles_ref
  9.5 1.5 shard_map.115
  11.1 4.9 %all-to-all-start = ((f32[8,3,4,128]{3,2,1,0:T(4,128)}), f32[8,3,4,128]{3,2,1,0:T(4,128)S(1)}, u32[]{:S(2)}, u32[]{:S(2)}) async-start(f32[8,3,4,128]{3,2,1,0:T(4,128)} %get-tuple-element.54), calls=%async_computation | async-start | bytes 98304 | tf_op jit(solution)/shard_map/all_to_all | solution.py:753
  16.0 3.2 %shard_map.119 = (f32[1024,128]{1,0:T(8,128)S(1)}, f32[3,32,128]{2,1,0:T(8,128)S(1)}) custom-call(f32[8,2048]{1,0:T(8,128)S(1)} %get-tuple-element.50.own_ref.refs_0_, f32[8,512]{1,0:T(8,128)S(1)} %collective-permute-done.refs_1_.mesh_ref, f32[8,512]{1,0:T(8,128)S(1)} %collective-permute-done.1.refs_2_.sub_ref, s32[4,4096]{1,0:T(4,128)S(1)} %copy-done.2, ...), custom_call_target="tpu_custom_call" | custom-call | flops 2147483648 | bytes 1048576 | tf_op jit(solution)/shard_map/pallas_call | solution.py:756
  19.2 3.6 %all-to-all-done.slots_ref = f32[8,3,4,128]{3,2,1,0:T(4,128)S(1)} async-done(((f32[8,3,4,128]{3,2,1,0:T(4,128)}), f32[8,3,4,128]{3,2,1,0:T(4,128)S(1)}, u32[]{:S(2)}, u32[]{:S(2)}) %all-to-all-start) | async-done | bytes 49184 | tf_op jit(solution)/shard_map/all_to_all | solution.py:753
  22.8 3.6 %shard_map.117 = (f32[8,2048]{1,0:T(8,128)S(1)}, f32[16,128]{1,0:T(8,128)}) custom-call(s32[4,4,16]{2,1,0:T(4,128)S(1)} %copy-done.7, bf16[4,2048,128]{2,1,0:T(8,128)(2,1)S(1)} %shard_map.116.node_ref, f32[8,3,4,128]{3,2,1,0:T(4,128)S(1)} %all-to-all-done.slots_ref), custom_call_target="tpu_custom_call" | custom-call | flops 2147483648 | bytes 1048576 | tf_op jit(solution)/shard_map/pallas_call | solution.py:757
  26.4 3.3 %all-to-all-start.1 = ((f32[8,2,128]{2,1,0:T(2,128)}), f32[8,2,128]{2,1,0:T(2,128)S(1)}, u32[]{:S(2)}, u32[]{:S(2)}) async-start(f32[8,2,128]{2,1,0:T(2,128)} %bitcast.2), calls=%async_computation.1 | async-start | bytes 16384 | tf_op jit(solution)/shard_map/all_to_all | solution.py:758
  29.7 3.7 %shard_map.120.acc_ref = f32[96,256]{1,0:T(8,128)S(1)} custom-call(f32[1024,128]{1,0:T(8,128)S(1)} %get-tuple-element.57.rows_ref, s32[4,4096]{1,0:T(4,128)S(1)} %copy-done.2), custom_call_target="tpu_custom_call" | custom-call | flops 2147483648 | bytes 1048576 | tf_op jit(solution)/shard_map/pallas_call | solution.py:762
  33.4 2.7 %all-to-all-done.1 = f32[8,2,128]{2,1,0:T(2,128)S(1)} async-done(((f32[8,2,128]{2,1,0:T(2,128)}), f32[8,2,128]{2,1,0:T(2,128)S(1)}, u32[]{:S(2)}, u32[]{:S(2)}) %all-to-all-start.1) | async-done | bytes 8224 | tf_op jit(solution)/shard_map/all_to_all | solution.py:758
  36.2 0.8 shard_map.122
  37.0 2.0 %collective-permute-start.2 = (f32[4,512]{1,0:T(4,128)S(1)}, f32[4,512]{1,0:T(4,128)S(1)}, u32[]{:S(2)}, u32[]{:S(2)}) collective-permute-start(f32[4,512]{1,0:T(4,128)S(1)} %get-tuple-element.59), channel_id=1, source_target_pairs={{0,28},{4,0},{8,4},{12,8},{16,12},{20,16},{24,20},{28,24},{1,29},{... | collective-permute-start | bytes 24584 | tf_op jit(solution)/shard_map/ppermute | solution.py:34
  39.0 0.7 shard_map.121.refs_1_
  39.7 1.0 collective-permute-done.2.refs_3_
  41.4 1.9 %shard_map.124.refs_4_ = f32[512,128]{1,0:T(8,128)S(1)} custom-call(f32[8,2048]{1,0:T(8,128)S(1)} %get-tuple-element.61.own_ref.refs_0_, s32[4,4096]{1,0:T(4,128)S(1)} %copy-done.2), custom_call_target="tpu_custom_call" | custom-call | flops 2147483648 | bytes 1048576 | tf_op jit(solution)/shard_map/pallas_call | solution.py:748
  43.2 1.5 collective-permute-start.4
  44.7 1.2 shard_map.126.node_ref
  45.9 3.8 %collective-permute-done.4.refs_1_.mesh_ref = f32[8,512]{1,0:T(8,128)S(1)} collective-permute-done((f32[8,512]{1,0:T(8,128)S(1)}, f32[8,512]{1,0:T(8,128)S(1)}, u32[]{:S(2)}, u32[]{:S(2)}) %collective-permute-start.4) | collective-permute-done | bytes 16416 | tf_op jit(solution)/shard_map/ppermute | solution.py:34
  49.7 1.5 shard_map.125
  51.3 3.5 %all-to-all-start.2 = ((f32[8,3,4,128]{3,2,1,0:T(4,128)}), f32[8,3,4,128]{3,2,1,0:T(4,128)S(1)}, u32[]{:S(2)}, u32[]{:S(2)}) async-start(f32[8,3,4,128]{3,2,1,0:T(4,128)} %get-tuple-element.65), calls=%async_computation.2 | async-start | bytes 98304 | tf_op jit(solution)/shard_map/all_to_all | solution.py:753
  54.8 3.2 %shard_map.128 = (f32[1024,128]{1,0:T(8,128)S(1)}, f32[3,32,128]{2,1,0:T(8,128)S(1)}) custom-call(f32[8,2048]{1,0:T(8,128)S(1)} %get-tuple-element.61.own_ref.refs_0_, f32[8,512]{1,0:T(8,128)S(1)} %collective-permute-done.4.refs_1_.mesh_ref, f32[8,512]{1,0:T(8,128)S(1)} %collective-permute-done.5.refs_2_.sub_ref, s32[4,4096]{1,0:T(4,128)S(1)} %copy-done.2, ...), custom_call_target="tpu_custom_call" | custom-call | flops 2147483648 | bytes 1048576 | tf_op jit(solution)/shard_map/pallas_call | solution.py:756
  58.6 2.7 %all-to-all-done.2.slots_ref = f32[8,3,4,128]{3,2,1,0:T(4,128)S(1)} async-done(((f32[8,3,4,128]{3,2,1,0:T(4,128)}), f32[8,3,4,128]{3,2,1,0:T(4,128)S(1)}, u32[]{:S(2)}, u32[]{:S(2)}) %all-to-all-start.2) | async-done | bytes 49184 | tf_op jit(solution)/shard_map/all_to_all | solution.py:753
  61.4 3.6 %shard_map.127 = (f32[8,2048]{1,0:T(8,128)S(1)}, f32[16,128]{1,0:T(8,128)}) custom-call(s32[4,4,16]{2,1,0:T(4,128)S(1)} %copy-done.7, bf16[4,2048,128]{2,1,0:T(8,128)(2,1)S(1)} %shard_map.126.node_ref, f32[8,3,4,128]{3,2,1,0:T(4,128)S(1)} %all-to-all-done.2.slots_ref), custom_call_target="tpu_custom_call" | custom-call | flops 2147483648 | bytes 1048576 | tf_op jit(solution)/shard_map/pallas_call | solution.py:757
  65.0 3.3 %all-to-all-start.3 = ((f32[8,2,128]{2,1,0:T(2,128)}), f32[8,2,128]{2,1,0:T(2,128)S(1)}, u32[]{:S(2)}, u32[]{:S(2)}) async-start(f32[8,2,128]{2,1,0:T(2,128)} %bitcast.5), calls=%async_computation.3 | async-start | bytes 16384 | tf_op jit(solution)/shard_map/all_to_all | solution.py:758
  68.3 3.7 %shard_map.129.acc_ref = f32[96,256]{1,0:T(8,128)S(1)} custom-call(f32[1024,128]{1,0:T(8,128)S(1)} %get-tuple-element.69.rows_ref, s32[4,4096]{1,0:T(4,128)S(1)} %copy-done.2), custom_call_target="tpu_custom_call" | custom-call | flops 2147483648 | bytes 1048576 | tf_op jit(solution)/shard_map/pallas_call | solution.py:762
  72.0 2.7 %all-to-all-done.3 = f32[8,2,128]{2,1,0:T(2,128)S(1)} async-done(((f32[8,2,128]{2,1,0:T(2,128)}), f32[8,2,128]{2,1,0:T(2,128)S(1)}, u32[]{:S(2)}, u32[]{:S(2)}) %all-to-all-start.3) | async-done | bytes 8224 | tf_op jit(solution)/shard_map/all_to_all | solution.py:758
  74.8 0.8 shard_map.131
  75.6 2.0 %collective-permute-start.6 = (f32[4,512]{1,0:T(4,128)S(1)}, f32[4,512]{1,0:T(4,128)S(1)}, u32[]{:S(2)}, u32[]{:S(2)}) collective-permute-start(f32[4,512]{1,0:T(4,128)S(1)} %get-tuple-element.71), channel_id=1, source_target_pairs={{0,28},{4,0},{8,4},{12,8},{16,12},{20,16},{24,20},{28,24},{1,29},{... | collective-permute-start | bytes 24584 | tf_op jit(solution)/shard_map/ppermute | solution.py:34
  77.6 0.7 shard_map.130.refs_1_
  78.3 1.0 collective-permute-done.6.refs_3_
  79.9 1.9 %shard_map.133.refs_4_ = f32[512,128]{1,0:T(8,128)S(1)} custom-call(f32[8,2048]{1,0:T(8,128)S(1)} %get-tuple-element.73.own_ref.refs_0_, s32[4,4096]{1,0:T(4,128)S(1)} %copy-done.2), custom_call_target="tpu_custom_call" | custom-call | flops 2147483648 | bytes 1048576 | tf_op jit(solution)/shard_map/pallas_call | solution.py:748
  81.8 1.5 collective-permute-start.8
  83.3 1.2 shard_map.135.node_ref
  84.5 3.8 %collective-permute-done.8.refs_1_.mesh_ref = f32[8,512]{1,0:T(8,128)S(1)} collective-permute-done((f32[8,512]{1,0:T(8,128)S(1)}, f32[8,512]{1,0:T(8,128)S(1)}, u32[]{:S(2)}, u32[]{:S(2)}) %collective-permute-start.8) | collective-permute-done | bytes 16416 | tf_op jit(solution)/shard_map/ppermute | solution.py:34
  88.3 1.5 shard_map.134
  89.8 3.4 %all-to-all-start.4 = ((f32[8,3,4,128]{3,2,1,0:T(4,128)}), f32[8,3,4,128]{3,2,1,0:T(4,128)S(1)}, u32[]{:S(2)}, u32[]{:S(2)}) async-start(f32[8,3,4,128]{3,2,1,0:T(4,128)} %get-tuple-element.77), calls=%async_computation.4 | async-start | bytes 98304 | tf_op jit(solution)/shard_map/all_to_all | solution.py:753
  93.2 3.2 %shard_map.137 = (f32[1024,128]{1,0:T(8,128)S(1)}, f32[3,32,128]{2,1,0:T(8,128)S(1)}) custom-call(f32[8,2048]{1,0:T(8,128)S(1)} %get-tuple-element.73.own_ref.refs_0_, f32[8,512]{1,0:T(8,128)S(1)} %collective-permute-done.8.refs_1_.mesh_ref, f32[8,512]{1,0:T(8,128)S(1)} %collective-permute-done.9.refs_2_.sub_ref, s32[4,4096]{1,0:T(4,128)S(1)} %copy-done.2, ...), custom_call_target="tpu_custom_call" | custom-call | flops 2147483648 | bytes 1048576 | tf_op jit(solution)/shard_map/pallas_call | solution.py:756
  96.4 3.5 %all-to-all-done.4.slots_ref = f32[8,3,4,128]{3,2,1,0:T(4,128)S(1)} async-done(((f32[8,3,4,128]{3,2,1,0:T(4,128)}), f32[8,3,4,128]{3,2,1,0:T(4,128)S(1)}, u32[]{:S(2)}, u32[]{:S(2)}) %all-to-all-start.4) | async-done | bytes 49184 | tf_op jit(solution)/shard_map/all_to_all | solution.py:753
  99.9 3.6 %shard_map.136 = (f32[8,2048]{1,0:T(8,128)S(1)}, f32[16,128]{1,0:T(8,128)}) custom-call(s32[4,4,16]{2,1,0:T(4,128)S(1)} %copy-done.7, bf16[4,2048,128]{2,1,0:T(8,128)(2,1)S(1)} %shard_map.135.node_ref, f32[8,3,4,128]{3,2,1,0:T(4,128)S(1)} %all-to-all-done.4.slots_ref), custom_call_target="tpu_custom_call" | custom-call | flops 2147483648 | bytes 1048576 | tf_op jit(solution)/shard_map/pallas_call | solution.py:757
  103.5 3.3 %all-to-all-start.5 = ((f32[8,2,128]{2,1,0:T(2,128)}), f32[8,2,128]{2,1,0:T(2,128)S(1)}, u32[]{:S(2)}, u32[]{:S(2)}) async-start(f32[8,2,128]{2,1,0:T(2,128)} %bitcast.7), calls=%async_computation.5 | async-start | bytes 16384 | tf_op jit(solution)/shard_map/all_to_all | solution.py:758
  106.8 3.7 %shard_map.138.acc_ref = f32[96,256]{1,0:T(8,128)S(1)} custom-call(f32[1024,128]{1,0:T(8,128)S(1)} %get-tuple-element.81.rows_ref, s32[4,4096]{1,0:T(4,128)S(1)} %copy-done.2), custom_call_target="tpu_custom_call" | custom-call | flops 2147483648 | bytes 1048576 | tf_op jit(solution)/shard_map/pallas_call | solution.py:762
  110.6 2.7 %all-to-all-done.5 = f32[8,2,128]{2,1,0:T(2,128)S(1)} async-done(((f32[8,2,128]{2,1,0:T(2,128)}), f32[8,2,128]{2,1,0:T(2,128)S(1)}, u32[]{:S(2)}, u32[]{:S(2)}) %all-to-all-start.5) | async-done | bytes 8224 | tf_op jit(solution)/shard_map/all_to_all | solution.py:758
  113.3 0.8 shard_map.140
  114.1 2.0 %collective-permute-start.10 = (f32[4,512]{1,0:T(4,128)S(1)}, f32[4,512]{1,0:T(4,128)S(1)}, u32[]{:S(2)}, u32[]{:S(2)}) collective-permute-start(f32[4,512]{1,0:T(4,128)S(1)} %get-tuple-element.83), channel_id=1, source_target_pairs={{0,28},{4,0},{8,4},{12,8},{16,12},{20,16},{24,20},{28,24},{1,29},{... | collective-permute-start | bytes 24584 | tf_op jit(solution)/shard_map/ppermute | solution.py:34
  116.8 1.0 collective-permute-done.10.refs_3_
  118.5 1.9 %shard_map.142.refs_4_ = f32[512,128]{1,0:T(8,128)S(1)} custom-call(f32[8,2048]{1,0:T(8,128)S(1)} %get-tuple-element.85.own_ref.refs_0_, s32[4,4096]{1,0:T(4,128)S(1)} %copy-done.2), custom_call_target="tpu_custom_call" | custom-call | flops 2147483648 | bytes 1048576 | tf_op jit(solution)/shard_map/pallas_call | solution.py:748
  120.3 1.5 collective-permute-start.12
  121.8 1.2 shard_map.144.node_ref
  123.0 3.8 %collective-permute-done.12.refs_1_.mesh_ref = f32[8,512]{1,0:T(8,128)S(1)} collective-permute-done((f32[8,512]{1,0:T(8,128)S(1)}, f32[8,512]{1,0:T(8,128)S(1)}, u32[]{:S(2)}, u32[]{:S(2)}) %collective-permute-start.12) | collective-permute-done | bytes 16416 | tf_op jit(solution)/shard_map/ppermute | solution.py:34
  126.8 1.5 shard_map.143
  128.3 3.4 %all-to-all-start.6 = ((f32[8,3,4,128]{3,2,1,0:T(4,128)}), f32[8,3,4,128]{3,2,1,0:T(4,128)S(1)}, u32[]{:S(2)}, u32[]{:S(2)}) async-start(f32[8,3,4,128]{3,2,1,0:T(4,128)} %get-tuple-element.89), calls=%async_computation.6 | async-start | bytes 98304 | tf_op jit(solution)/shard_map/all_to_all | solution.py:753
  131.7 3.2 %shard_map.146 = (f32[1024,128]{1,0:T(8,128)S(1)}, f32[3,32,128]{2,1,0:T(8,128)S(1)}) custom-call(f32[8,2048]{1,0:T(8,128)S(1)} %get-tuple-element.85.own_ref.refs_0_, f32[8,512]{1,0:T(8,128)S(1)} %collective-permute-done.12.refs_1_.mesh_ref, f32[8,512]{1,0:T(8,128)S(1)} %collective-permute-done.13.refs_2_.sub_ref, s32[4,4096]{1,0:T(4,128)S(1)} %copy-done.2, ...), custom_call_target="tpu_custom_call" | custom-call | flops 2147483648 | bytes 1048576 | tf_op jit(solution)/shard_map/pallas_call | solution.py:756
  134.9 3.5 %all-to-all-done.6.slots_ref = f32[8,3,4,128]{3,2,1,0:T(4,128)S(1)} async-done(((f32[8,3,4,128]{3,2,1,0:T(4,128)}), f32[8,3,4,128]{3,2,1,0:T(4,128)S(1)}, u32[]{:S(2)}, u32[]{:S(2)}) %all-to-all-start.6) | async-done | bytes 49184 | tf_op jit(solution)/shard_map/all_to_all | solution.py:753
  138.4 3.6 %shard_map.145 = (f32[8,2048]{1,0:T(8,128)S(1)}, f32[16,128]{1,0:T(8,128)}) custom-call(s32[4,4,16]{2,1,0:T(4,128)S(1)} %copy-done.7, bf16[4,2048,128]{2,1,0:T(8,128)(2,1)S(1)} %shard_map.144.node_ref, f32[8,3,4,128]{3,2,1,0:T(4,128)S(1)} %all-to-all-done.6.slots_ref), custom_call_target="tpu_custom_call" | custom-call | flops 2147483648 | bytes 1048576 | tf_op jit(solution)/shard_map/pallas_call | solution.py:757
  142.0 3.3 %all-to-all-start.7 = ((f32[8,2,128]{2,1,0:T(2,128)}), f32[8,2,128]{2,1,0:T(2,128)S(1)}, u32[]{:S(2)}, u32[]{:S(2)}) async-start(f32[8,2,128]{2,1,0:T(2,128)} %bitcast.9), calls=%async_computation.7 | async-start | bytes 16384 | tf_op jit(solution)/shard_map/all_to_all | solution.py:758
  145.4 3.7 %shard_map.147.acc_ref = f32[96,256]{1,0:T(8,128)S(1)} custom-call(f32[1024,128]{1,0:T(8,128)S(1)} %get-tuple-element.93.rows_ref, s32[4,4096]{1,0:T(4,128)S(1)} %copy-done.2), custom_call_target="tpu_custom_call" | custom-call | flops 2147483648 | bytes 1048576 | tf_op jit(solution)/shard_map/pallas_call | solution.py:762
  149.8 2.1 %all-to-all-done.7 = f32[8,2,128]{2,1,0:T(2,128)S(1)} async-done(((f32[8,2,128]{2,1,0:T(2,128)}), f32[8,2,128]{2,1,0:T(2,128)S(1)}, u32[]{:S(2)}, u32[]{:S(2)}) %all-to-all-start.7) | async-done | bytes 8224 | tf_op jit(solution)/shard_map/all_to_all | solution.py:758
  151.8 0.8 shard_map.149
  152.7 2.6 %collective-permute-start.14 = (f32[4,512]{1,0:T(4,128)S(1)}, f32[4,512]{1,0:T(4,128)S(1)}, u32[]{:S(2)}, u32[]{:S(2)}) collective-permute-start(f32[4,512]{1,0:T(4,128)S(1)} %get-tuple-element.95), channel_id=1, source_target_pairs={{0,28},{4,0},{8,4},{12,8},{16,12},{20,16},{24,20},{28,24},{1,29},{... | collective-permute-start | bytes 24584 | tf_op jit(solution)/shard_map/ppermute | solution.py:34
  156.7 0.9 shard_map.150
  (46 shorter events, 5.2 us)
Async XLA Ops:
  1.7 7.8 %collective-permute-start = (f32[8,512]{1,0:T(8,128)S(1)}, f32[8,512]{1,0:T(8,128)S(1)}, u32[]{:S(2)}, u32[]{:S(2)}) collective-permute-start(f32[8,512]{1,0:T(8,128)S(1)} %get-tuple-element.51), channel_id=1, source_target_pairs={{0,4},{4,8},{8,12},{12,16},{16,20},{20,24},{24,28},{28,0},{1,5},{5... | collective-permute-start | bytes 49160 | tf_op jit(solution)/shard_map/ppermute | solution.py:34
  4.8 4.8 %collective-permute-start.1 = (f32[8,512]{1,0:T(8,128)S(1)}, f32[8,512]{1,0:T(8,128)S(1)}, u32[]{:S(2)}, u32[]{:S(2)}) collective-permute-start(f32[8,512]{1,0:T(8,128)S(1)} %get-tuple-element.52), channel_id=1, source_target_pairs={{0,1},{1,2},{2,3},{3,0},{4,5},{5,6},{6,7},{7,4},{8,9},{9,10},{10,1... | collective-permute-start | bytes 49160 | tf_op jit(solution)/shard_map/ppermute | solution.py:34
  4.8 0.8 copy-start.1
  5.6 1.9 %copy-start.6 = (s32[4,4,2048]{2,1,0:T(4,128)S(1)}, s32[4,4,2048]{2,1,0:T(4,128)}, u32[]{:S(2)}) copy-start(s32[4,4,2048]{2,1,0:T(4,128)} %mask_ref.7) | copy-start | bytes 393220
  7.5 1.2 copy-start.10
  7.5 1.2 copy-start.2
  7.5 1.2 copy-start.5
  11.1 11.7 %all-to-all-start = ((f32[8,3,4,128]{3,2,1,0:T(4,128)}), f32[8,3,4,128]{3,2,1,0:T(4,128)S(1)}, u32[]{:S(2)}, u32[]{:S(2)}) async-start(f32[8,3,4,128]{3,2,1,0:T(4,128)} %get-tuple-element.54), calls=%async_computation | async-start | bytes 98304 | tf_op jit(solution)/shard_map/all_to_all | solution.py:753
  16.0 6.8 %copy-start.7 = (s32[4,4,16]{2,1,0:T(4,128)S(1)}, s32[4,4,16]{2,1,0:T(4,128)}, u32[]{:S(2)}) copy-start(s32[4,4,16]{2,1,0:T(4,128)} %list_any.7) | copy-start | bytes 3076
  26.4 9.8 %all-to-all-start.1 = ((f32[8,2,128]{2,1,0:T(2,128)}), f32[8,2,128]{2,1,0:T(2,128)S(1)}, u32[]{:S(2)}, u32[]{:S(2)}) async-start(f32[8,2,128]{2,1,0:T(2,128)} %bitcast.2), calls=%async_computation.1 | async-start | bytes 16384 | tf_op jit(solution)/shard_map/all_to_all | solution.py:758
  37.0 3.7 %copy-start = (f32[2048]{0:T(1024)S(1)}, f32[2048]{0:T(1024)}, u32[]{:S(2)}) copy-start(f32[2048]{0:T(1024)} %param.12) | copy-start | bytes 24580
  37.0 3.7 %copy-start.3 = (s32[512]{0:T(512)S(1)}, s32[512]{0:T(512)}, u32[]{:S(2)}) copy-start(s32[512]{0:T(512)} %param.15) | copy-start | bytes 6148
  37.0 3.7 %copy-start.4 = (s32[512]{0:T(512)S(1)}, s32[512]{0:T(512)}, u32[]{:S(2)}) copy-start(s32[512]{0:T(512)} %param.16) | copy-start | bytes 6148
  37.0 3.7 %collective-permute-start.2 = (f32[4,512]{1,0:T(4,128)S(1)}, f32[4,512]{1,0:T(4,128)S(1)}, u32[]{:S(2)}, u32[]{:S(2)}) collective-permute-start(f32[4,512]{1,0:T(4,128)S(1)} %get-tuple-element.59), channel_id=1, source_target_pairs={{0,28},{4,0},{8,4},{12,8},{16,12},{20,16},{24,20},{28,24},{1,29},{... | collective-permute-start | bytes 24584 | tf_op jit(solution)/shard_map/ppermute | solution.py:34
  39.0 1.7 %collective-permute-start.3 = (f32[4,512]{1,0:T(4,128)S(1)}, f32[4,512]{1,0:T(4,128)S(1)}, u32[]{:S(2)}, u32[]{:S(2)}) collective-permute-start(f32[4,512]{1,0:T(4,128)S(1)} %get-tuple-element.60), channel_id=1, source_target_pairs={{0,3},{1,0},{2,1},{3,2},{4,7},{5,4},{6,5},{7,6},{8,11},{9,8},{10,9... | collective-permute-start | bytes 24584 | tf_op jit(solution)/shard_map/ppermute | solution.py:34
  43.2 6.5 %collective-permute-start.4 = (f32[8,512]{1,0:T(8,128)S(1)}, f32[8,512]{1,0:T(8,128)S(1)}, u32[]{:S(2)}, u32[]{:S(2)}) collective-permute-start(f32[8,512]{1,0:T(8,128)S(1)} %get-tuple-element.62), channel_id=1, source_target_pairs={{0,4},{4,8},{8,12},{12,16},{16,20},{20,24},{24,28},{28,0},{1,5},{5... | collective-permute-start | bytes 49160 | tf_op jit(solution)/shard_map/ppermute | solution.py:34
  44.7 5.0 %collective-permute-start.5 = (f32[8,512]{1,0:T(8,128)S(1)}, f32[8,512]{1,0:T(8,128)S(1)}, u32[]{:S(2)}, u32[]{:S(2)}) collective-permute-start(f32[8,512]{1,0:T(8,128)S(1)} %get-tuple-element.63), channel_id=1, source_target_pairs={{0,1},{1,2},{2,3},{3,0},{4,5},{5,6},{6,7},{7,4},{8,9},{9,10},{10,1... | collective-permute-start | bytes 49160 | tf_op jit(solution)/shard_map/ppermute | solution.py:34
  51.3 10.1 %all-to-all-start.2 = ((f32[8,3,4,128]{3,2,1,0:T(4,128)}), f32[8,3,4,128]{3,2,1,0:T(4,128)S(1)}, u32[]{:S(2)}, u32[]{:S(2)}) async-start(f32[8,3,4,128]{3,2,1,0:T(4,128)} %get-tuple-element.65), calls=%async_computation.2 | async-start | bytes 98304 | tf_op jit(solution)/shard_map/all_to_all | solution.py:753
  58.0 0.6 copy-start.8
  65.0 9.8 %all-to-all-start.3 = ((f32[8,2,128]{2,1,0:T(2,128)}), f32[8,2,128]{2,1,0:T(2,128)S(1)}, u32[]{:S(2)}, u32[]{:S(2)}) async-start(f32[8,2,128]{2,1,0:T(2,128)} %bitcast.5), calls=%async_computation.3 | async-start | bytes 16384 | tf_op jit(solution)/shard_map/all_to_all | solution.py:758
  75.6 3.7 %collective-permute-start.6 = (f32[4,512]{1,0:T(4,128)S(1)}, f32[4,512]{1,0:T(4,128)S(1)}, u32[]{:S(2)}, u32[]{:S(2)}) collective-permute-start(f32[4,512]{1,0:T(4,128)S(1)} %get-tuple-element.71), channel_id=1, source_target_pairs={{0,28},{4,0},{8,4},{12,8},{16,12},{20,16},{24,20},{28,24},{1,29},{... | collective-permute-start | bytes 24584 | tf_op jit(solution)/shard_map/ppermute | solution.py:34
  77.6 1.7 %collective-permute-start.7 = (f32[4,512]{1,0:T(4,128)S(1)}, f32[4,512]{1,0:T(4,128)S(1)}, u32[]{:S(2)}, u32[]{:S(2)}) collective-permute-start(f32[4,512]{1,0:T(4,128)S(1)} %get-tuple-element.72), channel_id=1, source_target_pairs={{0,3},{1,0},{2,1},{3,2},{4,7},{5,4},{6,5},{7,6},{8,11},{9,8},{10,9... | collective-permute-start | bytes 24584 | tf_op jit(solution)/shard_map/ppermute | solution.py:34
  81.8 6.5 %collective-permute-start.8 = (f32[8,512]{1,0:T(8,128)S(1)}, f32[8,512]{1,0:T(8,128)S(1)}, u32[]{:S(2)}, u32[]{:S(2)}) collective-permute-start(f32[8,512]{1,0:T(8,128)S(1)} %get-tuple-element.74), channel_id=1, source_target_pairs={{0,4},{4,8},{8,12},{12,16},{16,20},{20,24},{24,28},{28,0},{1,5},{5... | collective-permute-start | bytes 49160 | tf_op jit(solution)/shard_map/ppermute | solution.py:34
  83.3 5.0 %collective-permute-start.9 = (f32[8,512]{1,0:T(8,128)S(1)}, f32[8,512]{1,0:T(8,128)S(1)}, u32[]{:S(2)}, u32[]{:S(2)}) collective-permute-start(f32[8,512]{1,0:T(8,128)S(1)} %get-tuple-element.75), channel_id=1, source_target_pairs={{0,1},{1,2},{2,3},{3,0},{4,5},{5,6},{6,7},{7,4},{8,9},{9,10},{10,1... | collective-permute-start | bytes 49160 | tf_op jit(solution)/shard_map/ppermute | solution.py:34
  84.5 8.7 %copy-start.9 = (f32[3,32,128]{2,1,0:T(8,128)S(1)}, f32[3,32,128]{2,1,0:T(8,128)}, u32[]{:S(2)}) copy-start(f32[3,32,128]{2,1,0:T(8,128)} %copy-done.8) | copy-start | bytes 147460
  89.8 10.1 %all-to-all-start.4 = ((f32[8,3,4,128]{3,2,1,0:T(4,128)}), f32[8,3,4,128]{3,2,1,0:T(4,128)S(1)}, u32[]{:S(2)}, u32[]{:S(2)}) async-start(f32[8,3,4,128]{3,2,1,0:T(4,128)} %get-tuple-element.77), calls=%async_computation.4 | async-start | bytes 98304 | tf_op jit(solution)/shard_map/all_to_all | solution.py:753
  103.5 9.8 %all-to-all-start.5 = ((f32[8,2,128]{2,1,0:T(2,128)}), f32[8,2,128]{2,1,0:T(2,128)S(1)}, u32[]{:S(2)}, u32[]{:S(2)}) async-start(f32[8,2,128]{2,1,0:T(2,128)} %bitcast.7), calls=%async_computation.5 | async-start | bytes 16384 | tf_op jit(solution)/shard_map/all_to_all | solution.py:758
  114.1 3.7 %collective-permute-start.10 = (f32[4,512]{1,0:T(4,128)S(1)}, f32[4,512]{1,0:T(4,128)S(1)}, u32[]{:S(2)}, u32[]{:S(2)}) collective-permute-start(f32[4,512]{1,0:T(4,128)S(1)} %get-tuple-element.83), channel_id=1, source_target_pairs={{0,28},{4,0},{8,4},{12,8},{16,12},{20,16},{24,20},{28,24},{1,29},{... | collective-permute-start | bytes 24584 | tf_op jit(solution)/shard_map/ppermute | solution.py:34
  116.1 1.7 %collective-permute-start.11 = (f32[4,512]{1,0:T(4,128)S(1)}, f32[4,512]{1,0:T(4,128)S(1)}, u32[]{:S(2)}, u32[]{:S(2)}) collective-permute-start(f32[4,512]{1,0:T(4,128)S(1)} %get-tuple-element.84), channel_id=1, source_target_pairs={{0,3},{1,0},{2,1},{3,2},{4,7},{5,4},{6,5},{7,6},{8,11},{9,8},{10,9... | collective-permute-start | bytes 24584 | tf_op jit(solution)/shard_map/ppermute | solution.py:34
  120.3 6.5 %collective-permute-start.12 = (f32[8,512]{1,0:T(8,128)S(1)}, f32[8,512]{1,0:T(8,128)S(1)}, u32[]{:S(2)}, u32[]{:S(2)}) collective-permute-start(f32[8,512]{1,0:T(8,128)S(1)} %get-tuple-element.86), channel_id=1, source_target_pairs={{0,4},{4,8},{8,12},{12,16},{16,20},{20,24},{24,28},{28,0},{1,5},{5... | collective-permute-start | bytes 49160 | tf_op jit(solution)/shard_map/ppermute | solution.py:34
  121.8 5.0 %collective-permute-start.13 = (f32[8,512]{1,0:T(8,128)S(1)}, f32[8,512]{1,0:T(8,128)S(1)}, u32[]{:S(2)}, u32[]{:S(2)}) collective-permute-start(f32[8,512]{1,0:T(8,128)S(1)} %get-tuple-element.87), channel_id=1, source_target_pairs={{0,1},{1,2},{2,3},{3,0},{4,5},{5,6},{6,7},{7,4},{8,9},{9,10},{10,1... | collective-permute-start | bytes 49160 | tf_op jit(solution)/shard_map/ppermute | solution.py:34
  128.3 10.1 %all-to-all-start.6 = ((f32[8,3,4,128]{3,2,1,0:T(4,128)}), f32[8,3,4,128]{3,2,1,0:T(4,128)S(1)}, u32[]{:S(2)}, u32[]{:S(2)}) async-start(f32[8,3,4,128]{3,2,1,0:T(4,128)} %get-tuple-element.89), calls=%async_computation.6 | async-start | bytes 98304 | tf_op jit(solution)/shard_map/all_to_all | solution.py:753
  142.0 9.8 %all-to-all-start.7 = ((f32[8,2,128]{2,1,0:T(2,128)}), f32[8,2,128]{2,1,0:T(2,128)S(1)}, u32[]{:S(2)}, u32[]{:S(2)}) async-start(f32[8,2,128]{2,1,0:T(2,128)} %bitcast.9), calls=%async_computation.7 | async-start | bytes 16384 | tf_op jit(solution)/shard_map/all_to_all | solution.py:758
  152.7 4.0 %collective-permute-start.14 = (f32[4,512]{1,0:T(4,128)S(1)}, f32[4,512]{1,0:T(4,128)S(1)}, u32[]{:S(2)}, u32[]{:S(2)}) collective-permute-start(f32[4,512]{1,0:T(4,128)S(1)} %get-tuple-element.95), channel_id=1, source_target_pairs={{0,28},{4,0},{8,4},{12,8},{16,12},{20,16},{24,20},{28,24},{1,29},{... | collective-permute-start | bytes 24584 | tf_op jit(solution)/shard_map/ppermute | solution.py:34
  155.3 1.4 collective-permute-start.15
